TPU v7x, 32 devices: a whole 2x2x4 slice. The times are simulated.
32 devices in a mesh: dp: 8 (over z, x), mp: 4 (over y, core).
Axes of the slice: x: 2, y: 2, z: 4, core: 2. Of those that a mesh axis runs over, the one named last changes fastest.
Arguments:
- mel_frames: float32 [16384, 80], P('dp')
- frame_mask: int32 [8, 1024], replicated, may hold values from 0 to 1, as said below
- token_ids: int32 [8, 384], replicated, may hold values from 0 to 51839
- token_mask: int32 [8, 384], replicated, may hold values from 0 to 1, as said below
- embedding: float32 [51840, 768], P('dp', 'mp'), may hold values from -6 to 6
- conv_one: float32 [3, 80, 768], P(None, None, ('dp', 'mp')), may hold values from -0.375 to 0.375
- conv_two: float32 [3, 768, 768], P(None, ('dp', 'mp')), may hold values from -0.125 to 0.125
- enc_qkv: float32 [3, 768, 768], P(None, 'dp', 'mp'), may hold values from -0.21875 to 0.21875
- enc_out: float32 [768, 768], P('mp', 'dp'), may hold values from -3.5 to 3.5
- enc_up: float32 [768, 3072], P('dp', 'mp'), may hold values from -0.21875 to 0.21875
- enc_down: float32 [3072, 768], P('mp', 'dp'), may hold values from -0.109375 to 0.109375
- cross_qkv: float32 [3, 768, 768], P(None, 'dp', 'mp'), may hold values from -0.21875 to 0.21875
- cross_out: float32 [768, 768], P('mp', 'dp'), may hold values from -3.5 to 3.5
- dec_qkv: float32 [3, 768, 768], P(None, 'dp', 'mp'), may hold values from -0.21875 to 0.21875
- dec_out: float32 [768, 768], P('mp', 'dp'), may hold values from -1.75 to 1.75
- dec_up: float32 [768, 3072], P('dp', 'mp'), may hold values from -0.21875 to 0.21875
- dec_down: float32 [3072, 768], P('mp', 'dp'), may hold values from -0.109375 to 0.109375
- norm_params: float32 [6, 2, 768], P(None, None, 'dp'), as said below
- cotangent: float32 [3072, 768], P('dp'), may hold values from -6 to 6
Outputs:
- decoded: float32 [3072, 768], P('dp')
- mel_grad: float32 [16384, 80], P('dp')
- embed_grad: float32 [51840, 768], P('dp', 'mp')
- conv_one_grad: float32 [3, 80, 768], P(None, None, ('dp', 'mp'))
- conv_two_grad: float32 [3, 768, 768], P(None, ('dp', 'mp'))
- enc_qkv_grad: float32 [3, 768, 768], P(None, 'dp', 'mp')
- enc_out_grad: float32 [768, 768], P('mp', 'dp')
- enc_up_grad: float32 [768, 3072], P('dp', 'mp')
- enc_down_grad: float32 [3072, 768], P('mp', 'dp')
- cross_qkv_grad: float32 [3, 768, 768], P(None, 'dp', 'mp')
- cross_out_grad: float32 [768, 768], P('mp', 'dp')
- dec_qkv_grad: float32 [3, 768, 768], P(None, 'dp', 'mp')
- dec_out_grad: float32 [768, 768], P('mp', 'dp')
- dec_up_grad: float32 [768, 3072], P('dp', 'mp')
- dec_down_grad: float32 [3072, 768], P('mp', 'dp')
- norm_grad: float32 [6, 2, 768], P(None, None, 'dp')
- rms_stats: float32 [9], replicated
Inputs may be any that keep to these rules, and one draw needn't show every extreme that they name: `frame_mask`: each clip's row is 1 on a prefix of at least max(68, 1) frames and 0 after it; some clip is valid in full. `token_mask`: each clip's row is 1 on a prefix of at least max(24, 1) tokens and 0 after it; some clip is valid in full. `norm_params`: gains near one and biases near zero.
All inputs are finite; a program needn't handle non-finite values.
Results may differ from a plain program's by a relative error of at most 0.0003.
Values sent between devices are 32-bit elements; how exact they have to be, the bound alone decides.
A program may use at most 256 MiB of HBM per device.

v0:
```python
import math

import jax
import jax.numpy as jnp
from jax import lax
from jax.sharding import PartitionSpec as P

HEAD = 64


HIGH = lax.Precision.HIGHEST
NEG = -1e30
EPS = 1e-05


def matmul(left, right):
    return jnp.dot(left, right, precision=HIGH, preferred_element_type=jnp.float32)


def gelu_exact(tensor):
    return jax.nn.gelu(tensor, approximate=False)


def layer_norm(tensor, norm_param):
    centre = tensor - jnp.mean(tensor, axis=-1, keepdims=True)
    spread = jnp.mean(centre * centre, axis=-1, keepdims=True)
    return centre * lax.rsqrt(spread + EPS) * norm_param[0] + norm_param[1]


def sinusoid(position, model_width):
    half_width = model_width // 2
    inverse_rates = jnp.exp(
        -math.log(10000.0) * jnp.arange(half_width).astype(jnp.float32) / (half_width - 1)
    )
    angles = position.astype(jnp.float32)[:, None] * inverse_rates[None, :]
    return jnp.concatenate([jnp.sin(angles), jnp.cos(angles)], axis=1)


def split_heads(tensor):
    return tensor.reshape(tensor.shape[0], -1, HEAD)


def attend(queries, key_rows, values, allowed):
    factor = 1.0 / math.sqrt(queries.shape[-1])
    scores = jnp.einsum("qhe,khe->hqk", queries, key_rows, precision=HIGH) * factor
    scores = jnp.where(allowed[None], scores, NEG)
    peaks = jnp.max(scores, axis=-1, keepdims=True)
    weight = jnp.exp(scores - peaks)
    totals = jnp.sum(weight, axis=-1, keepdims=True)
    output = jnp.einsum("hqk,khe->qhe", weight / totals, values, precision=HIGH)
    return (output, peaks + jnp.log(totals))


def attention_grads(queries, key_rows, values, allowed, output, log_total, grad_flat):
    factor = 1.0 / math.sqrt(queries.shape[-1])
    grad_out = grad_flat.reshape(output.shape)
    scores = jnp.einsum("qhe,khe->hqk", queries, key_rows, precision=HIGH) * factor
    attn_probs = jnp.where(allowed[None], jnp.exp(scores - log_total), 0.0)
    grad_values = jnp.einsum("hqk,qhe->khe", attn_probs, grad_out, precision=HIGH)
    grad_probs = jnp.einsum("qhe,khe->hqk", grad_out, values, precision=HIGH)
    inner_dot = jnp.sum(grad_out * output, axis=-1)
    grad_scores = attn_probs * (grad_probs - inner_dot.T[:, :, None]) * factor
    grad_queries = jnp.einsum("hqk,khe->qhe", grad_scores, key_rows, precision=HIGH)
    grad_keys = jnp.einsum("hqk,qhe->khe", grad_scores, queries, precision=HIGH)
    return (
        grad_queries.reshape(grad_queries.shape[0], -1),
        grad_keys.reshape(grad_keys.shape[0], -1),
        grad_values.reshape(grad_values.shape[0], -1),
    )


def project_three(rows_in, norm_param, weight):
    normed = layer_norm(rows_in, norm_param)
    return (matmul(normed, weight[0]), matmul(normed, weight[1]), matmul(normed, weight[2]))


def project_pair(rows_in, norm_param, weight_keys, weight_values):
    normed = layer_norm(rows_in, norm_param)
    return (matmul(normed, weight_keys), matmul(normed, weight_values))


def project_one(rows_in, norm_param, weight):
    return matmul(layer_norm(rows_in, norm_param), weight)


def feed_forward(rows_in, norm_param, up_weight, down_weight):
    return matmul(gelu_exact(matmul(layer_norm(rows_in, norm_param), up_weight)), down_weight)


def stem_piece(mel_in, weight_one, weight_two):
    mel_rows = mel_in.shape[0]
    padded = jnp.pad(mel_in, ((1, 1), (0, 0)))
    activated = gelu_exact(
        matmul(padded[0:mel_rows], weight_one[0])
        + matmul(padded[1 : mel_rows + 1], weight_one[1])
        + matmul(padded[2 : mel_rows + 2], weight_one[2])
    )
    padded_one = jnp.pad(activated, ((1, 1), (0, 0)))
    return (
        matmul(padded_one[0:mel_rows:2], weight_two[0])
        + matmul(padded_one[1 : mel_rows + 1 : 2], weight_two[1])
        + matmul(padded_one[2 : mel_rows + 2 : 2], weight_two[2])
    )


def masked_squares(tensor, row_weight):
    return jnp.sum(row_weight[:, None] * tensor * tensor)


def branch_sum(tensor):
    return lax.psum(tensor, "mp")


def input_sum(grad_rows, grad_norm):
    return lax.psum((grad_rows, grad_norm), "mp")


def body(
    mel_frames,
    frame_mask,
    token_ids,
    token_mask,
    embedding,
    conv_one,
    conv_two,
    enc_qkv,
    enc_out,
    enc_up,
    enc_down,
    cross_qkv,
    cross_out,
    dec_qkv,
    dec_out,
    dec_up,
    dec_down,
    norm_params,
    cotangent,
):
    dp_place = lax.axis_index("dp")
    frames = mel_frames.shape[0] // 2
    tokens = cotangent.shape[0]
    model_width = cotangent.shape[1]
    gathered = (
        lax.all_gather(conv_one, "dp", axis=2, tiled=True),
        lax.all_gather(conv_two, "dp", axis=1, tiled=True),
        lax.all_gather(enc_qkv, "dp", axis=1, tiled=True),
        lax.all_gather(enc_out, "dp", axis=1, tiled=True),
        lax.all_gather(enc_up, "dp", axis=0, tiled=True),
        lax.all_gather(enc_down, "dp", axis=1, tiled=True),
        lax.all_gather(cross_qkv, "dp", axis=1, tiled=True),
        lax.all_gather(cross_out, "dp", axis=1, tiled=True),
        lax.all_gather(dec_qkv, "dp", axis=1, tiled=True),
        lax.all_gather(dec_out, "dp", axis=1, tiled=True),
        lax.all_gather(dec_up, "dp", axis=0, tiled=True),
        lax.all_gather(dec_down, "dp", axis=1, tiled=True),
        lax.all_gather(norm_params, "dp", axis=2, tiled=True),
    )
    (
        full_conv_one,
        full_conv_two,
        full_enc_qkv,
        full_enc_out,
        full_enc_up,
        full_enc_down,
        full_cross_qkv,
        full_cross_out,
        full_dec_qkv,
        full_dec_out,
        full_dec_up,
        full_dec_down,
        full_norms,
    ) = gathered
    frame_row = lax.dynamic_index_in_dim(frame_mask, dp_place, 0, keepdims=False) > 0
    token_row = lax.dynamic_index_in_dim(token_mask, dp_place, 0, keepdims=False) > 0
    frame_allowed = frame_row[None, :]
    stem_sum = branch_sum(stem_piece(mel_frames, full_conv_one, full_conv_two))
    stream_zero = gelu_exact(stem_sum) + sinusoid(jnp.arange(frames, dtype=jnp.int32), model_width)
    enc_query, enc_keys, enc_values = project_three(stream_zero, full_norms[0], full_enc_qkv)
    enc_query_heads = split_heads(enc_query)
    enc_key_all = split_heads(enc_keys)
    enc_value_all = split_heads(enc_values)
    enc_mixed, enc_log_total = attend(enc_query_heads, enc_key_all, enc_value_all, frame_allowed)
    enc_mixed_flat = enc_mixed.reshape(frames, -1)
    enc_attn = branch_sum(matmul(enc_mixed_flat, full_enc_out))
    stream_one = stream_zero + enc_attn
    enc_mlp = branch_sum(feed_forward(stream_one, full_norms[1], full_enc_up, full_enc_down))
    stream_two = stream_one + enc_mlp
    cross_keys, cross_values = project_pair(
        stream_two, full_norms[2], full_cross_qkv[1], full_cross_qkv[2]
    )
    cross_key_all = split_heads(cross_keys)
    cross_value_all = split_heads(cross_values)
    flat_ids = token_ids.reshape(-1)
    vocab_rows = embedding.shape[0]
    local_ids = flat_ids - dp_place * vocab_rows
    owned_flags = (local_ids >= 0) & (local_ids < vocab_rows)
    safe_ids = jnp.clip(local_ids, 0, vocab_rows - 1)
    id_block = safe_ids
    flag_block = owned_flags
    picked = jnp.take(embedding, id_block, axis=0)
    embed_share = lax.psum_scatter(
        jnp.where(flag_block[:, None], picked, 0.0), "dp", scatter_dimension=0, tiled=True
    )
    embedded = lax.all_gather(embed_share, "mp", axis=1, tiled=True)
    text_zero = embedded + sinusoid(jnp.arange(tokens, dtype=jnp.int32), model_width)
    dec_query, dec_keys, dec_values = project_three(text_zero, full_norms[3], full_dec_qkv)
    positions = jnp.arange(tokens)
    self_allowed = (positions[None, :] <= positions[:, None]) & token_row[None, :]
    dec_query_heads = split_heads(dec_query)
    dec_key_all = split_heads(dec_keys)
    dec_value_all = split_heads(dec_values)
    dec_mixed, dec_log_total = attend(dec_query_heads, dec_key_all, dec_value_all, self_allowed)
    dec_mixed_flat = dec_mixed.reshape(tokens, -1)
    dec_attn = branch_sum(matmul(dec_mixed_flat, full_dec_out))
    text_one = text_zero + dec_attn
    cross_query = project_one(text_one, full_norms[4], full_cross_qkv[0])
    cross_query_heads = split_heads(cross_query)
    cross_mixed, cross_log_total = attend(
        cross_query_heads, cross_key_all, cross_value_all, frame_allowed
    )
    cross_mixed_flat = cross_mixed.reshape(tokens, -1)
    cross_attn = branch_sum(matmul(cross_mixed_flat, full_cross_out))
    text_two = text_one + cross_attn
    dec_mlp = branch_sum(feed_forward(text_two, full_norms[5], full_dec_up, full_dec_down))
    decoded = text_two + dec_mlp
    frame_weight = frame_row.astype(jnp.float32)
    token_weight = token_row.astype(jnp.float32)
    local_sums = jnp.stack(
        [
            masked_squares(stream_zero, frame_weight),
            masked_squares(enc_attn, frame_weight),
            masked_squares(enc_mlp, frame_weight),
            masked_squares(stream_two, frame_weight),
            masked_squares(text_zero, token_weight),
            masked_squares(dec_attn, token_weight),
            masked_squares(cross_attn, token_weight),
            masked_squares(dec_mlp, token_weight),
            masked_squares(decoded, token_weight),
        ]
    )
    square_sums = lax.psum(local_sums, "dp")
    frame_total = jnp.sum((frame_mask > 0).astype(jnp.float32))
    token_total = jnp.sum((token_mask > 0).astype(jnp.float32))
    counts = jnp.concatenate([jnp.full((4,), frame_total), jnp.full((5,), token_total)])
    rms_stats = jnp.sqrt(square_sums / (counts * model_width))
    grad_part, grad_norm_five, grad_dec_up, grad_dec_down = jax.vjp(
        feed_forward, text_two, full_norms[5], full_dec_up, full_dec_down
    )[1](cotangent)
    grad_summed, grad_norm_five = input_sum(grad_part, grad_norm_five)
    grad_text_two = cotangent + grad_summed
    grad_cross_out = matmul(cross_mixed_flat.T, grad_text_two)
    grad_cross_mixed = matmul(grad_text_two, full_cross_out.T)
    grad_cross_query, grad_cross_keys, grad_cross_values = attention_grads(
        cross_query_heads,
        cross_key_all,
        cross_value_all,
        frame_allowed,
        cross_mixed,
        cross_log_total,
        grad_cross_mixed,
    )
    grad_part, grad_norm_four, grad_cross_wq = jax.vjp(
        project_one, text_one, full_norms[4], full_cross_qkv[0]
    )[1](grad_cross_query)
    grad_summed, grad_norm_four = input_sum(grad_part, grad_norm_four)
    grad_text_one = grad_text_two + grad_summed
    grad_dec_out = matmul(dec_mixed_flat.T, grad_text_one)
    grad_dec_mixed = matmul(grad_text_one, full_dec_out.T)
    grad_dec_query, grad_dec_keys, grad_dec_values = attention_grads(
        dec_query_heads,
        dec_key_all,
        dec_value_all,
        self_allowed,
        dec_mixed,
        dec_log_total,
        grad_dec_mixed,
    )
    grad_part, grad_norm_three, grad_dec_qkv = jax.vjp(
        project_three, text_zero, full_norms[3], full_dec_qkv
    )[1]((grad_dec_query, grad_dec_keys, grad_dec_values))
    grad_summed, grad_norm_three = input_sum(grad_part, grad_norm_three)
    grad_text_zero = grad_text_one + grad_summed
    mp_place = lax.axis_index("mp")
    embed_width = embedding.shape[1]
    grad_embed_share = lax.dynamic_slice_in_dim(
        grad_text_zero, mp_place * embed_width, embed_width, 1
    )
    id_block = safe_ids
    flag_block = owned_flags
    grad_embedding = (
        jnp.zeros(embedding.shape, jnp.float32)
        .at[id_block]
        .add(
            jnp.where(
                flag_block[:, None], lax.all_gather(grad_embed_share, "dp", axis=0, tiled=True), 0.0
            )
        )
    )
    grad_part, grad_norm_two, grad_cross_wk, grad_cross_wv = jax.vjp(
        project_pair, stream_two, full_norms[2], full_cross_qkv[1], full_cross_qkv[2]
    )[1]((grad_cross_keys, grad_cross_values))
    grad_cross_qkv = jnp.stack([grad_cross_wq, grad_cross_wk, grad_cross_wv])
    grad_stream_two, grad_norm_two = input_sum(grad_part, grad_norm_two)
    grad_part, grad_norm_one, grad_enc_up, grad_enc_down = jax.vjp(
        feed_forward, stream_one, full_norms[1], full_enc_up, full_enc_down
    )[1](grad_stream_two)
    grad_summed, grad_norm_one = input_sum(grad_part, grad_norm_one)
    grad_stream_one = grad_stream_two + grad_summed
    grad_enc_out = matmul(enc_mixed_flat.T, grad_stream_one)
    grad_enc_mixed = matmul(grad_stream_one, full_enc_out.T)
    grad_enc_query, grad_enc_keys, grad_enc_values = attention_grads(
        enc_query_heads,
        enc_key_all,
        enc_value_all,
        frame_allowed,
        enc_mixed,
        enc_log_total,
        grad_enc_mixed,
    )
    grad_part, grad_norm_zero, grad_enc_qkv = jax.vjp(
        project_three, stream_zero, full_norms[0], full_enc_qkv
    )[1]((grad_enc_query, grad_enc_keys, grad_enc_values))
    grad_summed, grad_norm_zero = input_sum(grad_part, grad_norm_zero)
    grad_stream_zero = grad_stream_one + grad_summed
    grad_stem = jax.vjp(gelu_exact, stem_sum)[1](grad_stream_zero)[0]
    grad_mel_part, grad_conv_one, grad_conv_two = jax.vjp(
        stem_piece, mel_frames, full_conv_one, full_conv_two
    )[1](grad_stem)
    grad_mel = branch_sum(grad_mel_part)
    grad_norms = jnp.stack(
        [
            grad_norm_zero,
            grad_norm_one,
            grad_norm_two,
            grad_norm_three,
            grad_norm_four,
            grad_norm_five,
        ]
    )
    all_parts = tuple(
        (
            lax.psum_scatter(grad_conv_one, "dp", scatter_dimension=2, tiled=True),
            lax.psum_scatter(grad_conv_two, "dp", scatter_dimension=1, tiled=True),
            lax.psum_scatter(grad_enc_qkv, "dp", scatter_dimension=1, tiled=True),
            lax.psum_scatter(grad_enc_out, "dp", scatter_dimension=1, tiled=True),
            lax.psum_scatter(grad_enc_up, "dp", scatter_dimension=0, tiled=True),
            lax.psum_scatter(grad_enc_down, "dp", scatter_dimension=1, tiled=True),
            lax.psum_scatter(grad_cross_qkv, "dp", scatter_dimension=1, tiled=True),
            lax.psum_scatter(grad_cross_out, "dp", scatter_dimension=1, tiled=True),
            lax.psum_scatter(grad_dec_qkv, "dp", scatter_dimension=1, tiled=True),
            lax.psum_scatter(grad_dec_out, "dp", scatter_dimension=1, tiled=True),
            lax.psum_scatter(grad_dec_up, "dp", scatter_dimension=0, tiled=True),
            lax.psum_scatter(grad_dec_down, "dp", scatter_dimension=1, tiled=True),
            lax.psum_scatter(grad_norms, "dp", scatter_dimension=2, tiled=True),
        )
    )
    return (decoded, grad_mel, grad_embedding) + all_parts + (rms_stats,)


def solution(mesh):
    placed = (
        P("dp", None),
        P(),
        P(),
        P(),
        P("dp", "mp"),
        P(None, None, ("dp", "mp")),
        P(None, ("dp", "mp"), None),
        P(None, "dp", "mp"),
        P("mp", "dp"),
        P("dp", "mp"),
        P("mp", "dp"),
        P(None, "dp", "mp"),
        P("mp", "dp"),
        P(None, "dp", "mp"),
        P("mp", "dp"),
        P("dp", "mp"),
        P("mp", "dp"),
        P(None, None, "dp"),
        P("dp", None),
    )
    return jax.shard_map(
        body,
        mesh=mesh,
        in_specs=placed,
        out_specs=(
            P("dp", None),
            P("dp", None),
            P("dp", "mp"),
            P(None, None, ("dp", "mp")),
            P(None, ("dp", "mp"), None),
            P(None, "dp", "mp"),
            P("mp", "dp"),
            P("dp", "mp"),
            P("mp", "dp"),
            P(None, "dp", "mp"),
            P("mp", "dp"),
            P(None, "dp", "mp"),
            P("mp", "dp"),
            P("dp", "mp"),
            P("mp", "dp"),
            P(None, None, "dp"),
            P(),
        ),
        check_vma=False,
    )
```

profile of v0, /device:TPU:0, one launch (start us, length us, event | category | flops | bytes accessed | tf_op | source)
XLA Modules:
  0.0 2457.9 jit_solution(10924375323496480957)
XLA Ops:
  8.7 33.4 %all_gather.49 = f32[3,80,192]{1,2,0:T(8,128)S(1)} all-gather(f32[3,80,24]{1,2,0:T(8,128)} %param.24), channel_id=1, replica_groups=mesh['dp'=8,'mp'=4] {'dp'}, dimensions={2}, use_global_device_ids=true | all-gather | bytes 207360 | tf_op jit(solution)/shard_map/all_gather | solution.py:144
  168.9 34.4 %all_gather.52 = f32[192,768]{0,1:T(8,128)} all-gather(f32[192,96]{0,1:T(8,128)S(1)} %copy.130), channel_id=1, replica_groups=mesh['dp'=8,'mp'=4] {'dp'}, dimensions={1}, use_global_device_ids=true | all-gather | bytes 663552 | tf_op jit(solution)/shard_map/all_gather | solution.py:147
  203.3 33.4 %all_gather.46 = f32[6,2,768]{0,1,2:T(2,128)S(1)} all-gather(f32[6,2,96]{0,1,2:T(2,128)S(1)} %copy.120), channel_id=1, replica_groups=mesh['dp'=8,'mp'=4] {'dp'}, dimensions={2}, use_global_device_ids=true | all-gather | bytes 41472 | tf_op jit(solution)/shard_map/all_gather | solution.py:156
  236.6 33.6 %slice_reduce_fusion.1 = (f32[768]{0:T(1024)S(1)}, f32[768]{0:T(1024)}, f32[768]{0:T(1024)S(1)}, f32[768]{0:T(1024)S(1)}, f32[768]{0:T(1024)}, /*index=5*/f32[76...) fusion(f32[6,2,768]{0,1,2:T(2,128)S(1)} %all_gather.46), kind=kLoop, calls=%fused_computation.322 | loop fusion | bytes 73728 | tf_op jit(solution)/shard_map/slice | solution.py:27
  345.6 33.9 %all_gather.48 = f32[192,768]{0,1:T(8,128)} all-gather(f32[192,96]{0,1:T(8,128)S(1)} %copy.125), channel_id=1, replica_groups=mesh['dp'=8,'mp'=4] {'dp'}, dimensions={1}, use_global_device_ids=true | all-gather | bytes 663552 | tf_op jit(solution)/shard_map/all_gather | solution.py:153
  392.5 27.5 %all-reduce.51.cloned.1.call-done = f32[1024,768]{1,0:T(8,128)} async-done(((f32[1024,768]{1,0:T(8,128)}), f32[1024,768]{1,0:T(8,128)}) %all-reduce.51.cloned.1.call-update) | async-done | bytes 3145744 | tf_op jit(solution)/shard_map/psum | solution.py:111
  424.4 49.7 %all-gather.19.cloned.1.call-done = f32[768,768]{1,0:T(8,128)} async-done(((f32[96,768]{1,0:T(8,128)}), f32[768,768]{1,0:T(8,128)}) %all-gather.19.cloned.1.call-update) | async-done | bytes 2359312 | tf_op jit(solution)/shard_map/all_gather | solution.py:148
  492.0 34.7 %all-gather.21.cloned.1.call-done = f32[768,768]{0,1:T(8,128)} async-done(((f32[768,96]{0,1:T(8,128)}), f32[768,768]{0,1:T(8,128)}) %all-gather.21.cloned.1.call-update) | async-done | bytes 2359312 | tf_op jit(solution)/shard_map/all_gather | solution.py:149
  561.7 34.5 %all_gather.56 = f32[192,768]{0,1:T(8,128)S(1)} all-gather(f32[192,96]{0,1:T(8,128)S(1)} %copy.134), channel_id=1, replica_groups=mesh['dp'=8,'mp'=4] {'dp'}, dimensions={1}, use_global_device_ids=true | all-gather | bytes 663552 | tf_op jit(solution)/shard_map/all_gather | solution.py:151
  614.8 82.0 %all-reduce.67.cloned.1.call-done = (f32[384,768]{1,0:T(8,128)}, f32[1024,768]{1,0:T(8,128)}) async-done(((f32[384,768]{1,0:T(8,128)}, f32[1024,768]{1,0:T(8,128)}), (f32[384,768]{1,0:T(8,128)}, f32[1024,768]{1,0:T(8,128)})) %all-reduce.67.cloned.1.call-update) | async-done | bytes 4325392 | tf_op jit(solution)/shard_map/psum | solution.py:111
  755.6 34.5 %all-reduce.53.cloned.1.call-done = f32[384,768]{1,0:T(8,128)} async-done(((f32[384,768]{1,0:T(8,128)}), f32[384,768]{1,0:T(8,128)}) %all-reduce.53.cloned.1.call-update) | async-done | bytes 1179664 | tf_op jit(solution)/shard_map/psum | solution.py:111
  794.0 50.1 %all-gather.25.cloned.1.call-done = f32[768,768]{1,0:T(8,128)} async-done(((f32[96,768]{1,0:T(8,128)}), f32[768,768]{1,0:T(8,128)}) %all-gather.25.cloned.1.call-update) | async-done | bytes 2359312 | tf_op jit(solution)/shard_map/all_gather | solution.py:154
  858.0 36.2 %all-reduce.55.cloned.1.call-done = f32[384,768]{1,0:T(8,128)} async-done(((f32[384,768]{1,0:T(8,128)}), f32[384,768]{1,0:T(8,128)}) %all-reduce.55.cloned.1.call-update) | async-done | bytes 1179664 | tf_op jit(solution)/shard_map/psum | solution.py:115
  930.7 68.0 %all-reduce.57.cloned.1.call-done = f32[1024,768]{1,0:T(8,128)} async-done(((f32[1024,768]{1,0:T(8,128)}), f32[1024,768]{1,0:T(8,128)}) %all-reduce.57.cloned.1.call-update) | async-done | bytes 3145744 | tf_op jit(solution)/shard_map/psum | solution.py:115
  1041.5 54.6 %all-reduce.59.cloned.1.call-done = f32[1024,768]{1,0:T(8,128)} async-done(((f32[1024,768]{1,0:T(8,128)}), f32[1024,768]{1,0:T(8,128)}) %all-reduce.59.cloned.1.call-update) | async-done | bytes 3145744 | tf_op jit(solution)/shard_map/psum | solution.py:115
  1186.2 79.2 %all-reduce.65.cloned.1.call-done = (f32[1024,768]{1,0:T(8,128)}, f32[384,768]{1,0:T(8,128)}) async-done(((f32[1024,768]{1,0:T(8,128)}, f32[384,768]{1,0:T(8,128)}), (f32[1024,768]{1,0:T(8,128)}, f32[384,768]{1,0:T(8,128)})) %all-reduce.65.cloned.1.call-update) | async-done | bytes 4325392 | tf_op jit(solution)/shard_map/psum | solution.py:115
  1290.4 31.0 %pad.155 = f32[2048,192]{0,1:T(8,128)} pad(f32[1024,192]{0,1:T(8,128)} %fusion.161, f32[]{:T(128)} %constant.55.clone.1), padding=1_0_1x0_0_0 | pad | bytes 2359300 | tf_op jit(solution)/shard_map/transpose(jvp(jit(_pad)))/pad | solution.py:98
  1327.2 30.9 %pad.156 = f32[2048,192]{0,1:T(8,128)} pad(f32[1024,192]{0,1:T(8,128)} %fusion.159, f32[]{:T(128)} %constant.55.clone.1), padding=0_1_1x0_0_0 | pad | bytes 2359300 | tf_op jit(solution)/shard_map/transpose(jvp(jit(_pad)))/pad | solution.py:98
  1363.8 30.9 %pad.203 = f32[2049,192]{0,1:T(8,128)} pad(f32[1024,192]{0,1:T(8,128)} %fusion.157, f32[]{:T(128)} %constant.55.clone.1), padding=0_2_1x0_0_0 | pad | bytes 2360068
  1583.1 34.6 %reduce-scatter.44.cloned.1.call-done = f32[96,576]{1,0:T(8,128)} async-done(((f32[768,576]{1,0:T(8,128)}), f32[96,576]{1,0:T(8,128)}) %reduce-scatter.44.cloned.1.call-update) | async-done | bytes 221200
  1621.4 61.9 %reduce-scatter.42.cloned.1.call-done = f32[96,192]{1,0:T(8,128)} async-done(((f32[768,192]{1,0:T(8,128)}), f32[96,192]{1,0:T(8,128)}) %reduce-scatter.42.cloned.1.call-update) | async-done | bytes 73744
  1684.9 63.0 %reduce-scatter.52.cloned.1.call-done = f32[96,12]{1,0:T(8,128)} async-done(((f32[768,12]{1,0:T(8,128)}), f32[96,12]{1,0:T(8,128)}) %reduce-scatter.52.cloned.1.call-update) | async-done | bytes 4624
  1751.3 70.6 %all-reduce.61.cloned.1.call-done = f32[3,80,192]{1,0,2:T(4,128)} async-done(((f32[3,80,192]{1,0,2:T(4,128)}), f32[3,80,192]{1,0,2:T(4,128)}) %all-reduce.61.cloned.1.call-update) | async-done | bytes 184336
  1823.3 64.2 %reduce-scatter.50.cloned.1.call-done = f32[96,192]{1,0:T(8,128)} async-done(((f32[768,192]{1,0:T(8,128)}), f32[96,192]{1,0:T(8,128)}) %reduce-scatter.50.cloned.1.call-update) | async-done | bytes 73744
  1889.2 68.3 %reduce-scatter.40.cloned.1.call-done = f32[96,576]{1,0:T(8,128)} async-done(((f32[768,576]{1,0:T(8,128)}), f32[96,576]{1,0:T(8,128)}) %reduce-scatter.40.cloned.1.call-update) | async-done | bytes 221200
  1991.5 35.7 %reduce-scatter.48.cloned.1.call-done = f32[96,576]{1,0:T(8,128)} async-done(((f32[768,576]{1,0:T(8,128)}), f32[96,576]{1,0:T(8,128)}) %reduce-scatter.48.cloned.1.call-update) | async-done | bytes 221200
  2029.1 59.7 %all-gather.29.cloned.1.call-done = f32[3072,192]{1,0:T(8,128)} async-done(((f32[384,192]{1,0:T(8,128)}), f32[3072,192]{1,0:T(8,128)}) %all-gather.29.cloned.1.call-update) | async-done | bytes 2359312 | tf_op jit(solution)/shard_map/all_gather | solution.py:295
  2120.5 40.7 %reduce-scatter.38.cloned.1.call-done = f32[768,96]{0,1:T(8,128)} async-done(((f32[768,768]{0,1:T(8,128)}), f32[768,96]{0,1:T(8,128)}) %reduce-scatter.38.cloned.1.call-update) | async-done | bytes 294928 | tf_op jit(solution)/shard_map/reduce_scatter | solution.py:353
  2161.3 72.8 %reduce-scatter.36.cloned.1.call-done = f32[96,768]{1,0:T(8,128)} async-done(((f32[768,768]{1,0:T(8,128)}), f32[96,768]{1,0:T(8,128)}) %reduce-scatter.36.cloned.1.call-update) | async-done | bytes 294928 | tf_op jit(solution)/shard_map/reduce_scatter | solution.py:352
  2234.1 72.9 %reduce-scatter.34.cloned.1.call-done = f32[768,96]{0,1:T(8,128)} async-done(((f32[768,768]{0,1:T(8,128)}), f32[768,96]{0,1:T(8,128)}) %reduce-scatter.34.cloned.1.call-update) | async-done | bytes 294928 | tf_op jit(solution)/shard_map/reduce_scatter | solution.py:347
  2307.0 72.9 %reduce-scatter.32.cloned.1.call-done = f32[96,768]{1,0:T(8,128)} async-done(((f32[768,768]{1,0:T(8,128)}), f32[96,768]{1,0:T(8,128)}) %reduce-scatter.32.cloned.1.call-update) | async-done | bytes 294928 | tf_op jit(solution)/shard_map/reduce_scatter | solution.py:346
  2379.9 69.9 %reduce-scatter.30.cloned.1.call-done = f32[3,24,768]{2,1,0:T(8,128)} async-done(((f32[3,192,768]{2,1,0:T(8,128)}), f32[3,24,768]{2,1,0:T(8,128)}) %reduce-scatter.30.cloned.1.call-update) | async-done | bytes 221200 | tf_op jit(solution)/shard_map/reduce_scatter | solution.py:343
  (772 shorter events, 838.5 us)
Async XLA Ops:
  7.2 125.6 %all-gather.15.cloned.1.call-start = ((), (), s32[]{:S(2)}) async-start(), calls=%async_computation.16 | async-start | bytes 1990656 | tf_op jit(solution)/shard_map/all_gather | solution.py:145
  7.9 270.1 %all-gather.17.cloned.1.call-start = ((), (), s32[]{:S(2)}) async-start(), calls=%async_computation.18 | async-start | bytes 2654208 | tf_op jit(solution)/shard_map/all_gather | solution.py:146
  8.7 274.3 %all-reduce.49.cloned.1.call-start = ((), (), s32[]{:S(2)}) async-start(), calls=%async_computation.17 | async-start | bytes 6291456 | tf_op jit(solution)/shard_map/psum | solution.py:111
  145.0 197.1 %reduce-scatter.28.cloned.1.call-start = ((), (), s32[]{:S(2)}) async-start(), calls=%async_computation.13 | async-start | bytes 3538944 | tf_op jit(solution)/shard_map/reduce_scatter | solution.py:201
  167.7 215.0 %all-gather.13.cloned.1.call-start = ((), (), s32[]{:S(2)}) async-start(), calls=%async_computation.15 | async-start | bytes 2654208 | tf_op jit(solution)/shard_map/all_gather | solution.py:152
  168.3 251.6 %all-reduce.51.cloned.1.call-start = ((), (), s32[]{:S(2)}) async-start(), calls=%async_computation.19 | async-start | bytes 6291456 | tf_op jit(solution)/shard_map/psum | solution.py:111
  340.5 133.6 %all-gather.19.cloned.1.call-start = ((), (), s32[]{:S(2)}) async-start(), calls=%async_computation.20 | async-start | bytes 2654208 | tf_op jit(solution)/shard_map/all_gather | solution.py:148
  341.2 185.4 %all-gather.21.cloned.1.call-start = ((), (), s32[]{:S(2)}) async-start(), calls=%async_computation.21 | async-start | bytes 2654208 | tf_op jit(solution)/shard_map/all_gather | solution.py:149
  342.0 202.8 %all-gather.11.cloned.1.call-start = ((), (), s32[]{:S(2)}) async-start(), calls=%async_computation.14 | async-start | bytes 1474560 | tf_op jit(solution)/shard_map/all_gather | solution.py:204
  343.9 262.5 %all-gather.23.cloned.1.call-start = ((), (), s32[]{:S(2)}) async-start(), calls=%async_computation.22 | async-start | bytes 2654208 | tf_op jit(solution)/shard_map/all_gather | solution.py:150
  344.5 352.3 %all-reduce.67.cloned.1.call-start = ((), (), s32[]{:S(2)}) async-start(), calls=%async_computation.45 | async-start | bytes 8650752 | tf_op jit(solution)/shard_map/psum | solution.py:111
  560.8 190.1 %all-gather.27.cloned.1.call-start = ((), (), s32[]{:S(2)}) async-start(), calls=%async_computation.25 | async-start | bytes 2654208 | tf_op jit(solution)/shard_map/all_gather | solution.py:155
  561.4 228.8 %all-reduce.53.cloned.1.call-start = ((), (), s32[]{:S(2)}) async-start(), calls=%async_computation.23 | async-start | bytes 2359296 | tf_op jit(solution)/shard_map/psum | solution.py:111
  731.6 162.5 %all-reduce.55.cloned.1.call-start = ((), (), s32[]{:S(2)}) async-start(), calls=%async_computation.26 | async-start | bytes 2359296 | tf_op jit(solution)/shard_map/psum | solution.py:115
  857.9 140.8 %all-reduce.57.cloned.1.call-start = ((), (), s32[]{:S(2)}) async-start(), calls=%async_computation.27 | async-start | bytes 6291456 | tf_op jit(solution)/shard_map/psum | solution.py:115
  930.0 166.2 %all-reduce.59.cloned.1.call-start = ((), (), s32[]{:S(2)}) async-start(), calls=%async_computation.28 | async-start | bytes 6291456 | tf_op jit(solution)/shard_map/psum | solution.py:115
  1027.5 237.9 %all-reduce.65.cloned.1.call-start = ((), (), s32[]{:S(2)}) async-start(), calls=%async_computation.44 | async-start | bytes 8650752 | tf_op jit(solution)/shard_map/psum | solution.py:115
  1177.5 344.1 %all-reduce.63.cloned.1.call-start = ((), (), s32[]{:S(2)}) async-start(), calls=%async_computation.43 | async-start | bytes 6029312 | tf_op jit(solution)/shard_map/psum | solution.py:111
  1414.3 167.2 %reduce-scatter.46.cloned.1.call-start = ((), (), s32[]{:S(2)}) async-start(), calls=%async_computation.38 | async-start | bytes 884736
  1418.9 198.8 %reduce-scatter.44.cloned.1.call-start = ((), (), s32[]{:S(2)}) async-start(), calls=%async_computation.37 | async-start | bytes 2211840
  1440.9 242.4 %reduce-scatter.42.cloned.1.call-start = ((), (), s32[]{:S(2)}) async-start(), calls=%async_computation.36 | async-start | bytes 884736
  1449.4 298.4 %reduce-scatter.52.cloned.1.call-start = ((), (), s32[]{:S(2)}) async-start(), calls=%async_computation.41 | async-start | bytes 442368
  1474.4 347.5 %all-reduce.61.cloned.1.call-start = ((), (), s32[]{:S(2)}) async-start(), calls=%async_computation.42 | async-start | bytes 786432
  1478.0 409.6 %reduce-scatter.50.cloned.1.call-start = ((), (), s32[]{:S(2)}) async-start(), calls=%async_computation.40 | async-start | bytes 884736
  1482.4 475.0 %reduce-scatter.40.cloned.1.call-start = ((), (), s32[]{:S(2)}) async-start(), calls=%async_computation.35 | async-start | bytes 2211840
  1504.1 523.1 %reduce-scatter.48.cloned.1.call-start = ((), (), s32[]{:S(2)}) async-start(), calls=%async_computation.39 | async-start | bytes 2211840
  1521.6 567.3 %all-gather.29.cloned.1.call-start = ((), (), s32[]{:S(2)}) async-start(), calls=%async_computation.29 | async-start | bytes 3538944 | tf_op jit(solution)/shard_map/all_gather | solution.py:295
  1523.9 637.3 %reduce-scatter.38.cloned.1.call-start = ((), (), s32[]{:S(2)}) async-start(), calls=%async_computation.34 | async-start | bytes 2654208 | tf_op jit(solution)/shard_map/reduce_scatter | solution.py:353
  1531.5 702.6 %reduce-scatter.36.cloned.1.call-start = ((), (), s32[]{:S(2)}) async-start(), calls=%async_computation.33 | async-start | bytes 2654208 | tf_op jit(solution)/shard_map/reduce_scatter | solution.py:352
  1540.4 766.6 %reduce-scatter.34.cloned.1.call-start = ((), (), s32[]{:S(2)}) async-start(), calls=%async_computation.32 | async-start | bytes 2654208 | tf_op jit(solution)/shard_map/reduce_scatter | solution.py:347
  1552.6 827.3 %reduce-scatter.32.cloned.1.call-start = ((), (), s32[]{:S(2)}) async-start(), calls=%async_computation.31 | async-start | bytes 2654208 | tf_op jit(solution)/shard_map/reduce_scatter | solution.py:346
  1567.4 882.4 %reduce-scatter.30.cloned.1.call-start = ((), (), s32[]{:S(2)}) async-start(), calls=%async_computation.30 | async-start | bytes 1990656 | tf_op jit(solution)/shard_map/reduce_scatter | solution.py:343
  (222 other events, 9723.6 us)
Sparse Core Ops, SparseCore 0:
  10.2 49.2 all-gather.14
  61.7 50.6 all-gather.16
  145.1 69.0 all-reduce.48
  218.2 75.4 reduce-scatter.27
  295.7 55.1 all-gather.12
  353.1 66.8 all-reduce.50
  422.1 51.9 all-gather.18
  476.3 50.3 all-gather.20
  546.8 59.5 all-gather.22
  609.5 87.3 all-reduce.66
  698.8 51.9 all-gather.26
  753.8 36.2 all-reduce.52
  792.2 51.9 all-gather.24
  858.0 36.0 all-reduce.54
  930.1 68.5 all-reduce.56
  1027.6 68.5 all-reduce.58
  1177.6 87.7 all-reduce.64
  1414.4 66.8 all-reduce.62
  1484.4 63.3 reduce-scatter.45
  1551.3 66.4 reduce-scatter.43
  1621.0 62.1 reduce-scatter.41
  1686.5 61.2 reduce-scatter.51
  1751.1 70.7 all-reduce.60
  1825.2 62.2 reduce-scatter.49
  1890.9 66.5 reduce-scatter.39
  1960.8 66.4 reduce-scatter.47
  2030.0 58.8 all-gather.28
  2092.9 68.2 reduce-scatter.37
  2165.2 68.8 reduce-scatter.35
  2238.2 68.8 reduce-scatter.33
  2311.1 68.7 reduce-scatter.31
  2383.8 65.9 reduce-scatter.29
  (1 shorter events, 15.9 us)
where the time goes:
time: 2470 us; the launch traced here: 2460 us
  waiting for transfers between devices  1340 us (54%)
  matrix products  430 us (17%)
  local copies, waits for them, and re-layouts  335 us (14%)
  blocking collectives  200 us (8%)
  other arithmetic  125 us (5%)
    unnamed x41, waiting for transfers between devices  404 us
    dot_general x63, matrix products, matmul(): jnp.dot(left, right, precision=HIGH, preferred_element_type=jnp.float32)  296 us
    psum x4, waiting for transfers between devices, input_sum(): return lax.psum((grad_rows, grad_norm), 'mp')  238 us
    psum x5, waiting for transfers between devices, branch_sum(): return lax.psum(tensor, 'mp')  144 us
    unnamed x478, local copies, waits for them, and re-layouts  111 us
    reduce_scatter x1, waiting for transfers between devices, body(): lax.psum_scatter(grad_enc_down, 'dp', scatter_dimension=1, tiled=True)  72.9 us
    reduce_scatter x1, waiting for transfers between devices, body(): lax.psum_scatter(grad_enc_up, 'dp', scatter_dimension=0, tiled=True)  72.9 us
    reduce_scatter x1, waiting for transfers between devices, body(): lax.psum_scatter(grad_dec_up, 'dp', scatter_dimension=0, tiled=True)  72.8 us
  transfers between devices with their start and end apart: 33, of which 26 were waited for; matrix products, arithmetic and copies ran while one was open for 23% of the time, Pallas kernels for 0%

commit v1 on v0

v1 whole, which is shorter than its diff:
```python
import functools
import math

import jax
import jax.numpy as jnp
from jax import lax
from jax.experimental import pallas as pl
from jax.experimental.pallas import tpu as pltpu
from jax.sharding import PartitionSpec as P

HEAD = 64
HIGH = lax.Precision.HIGH
NEG = -1e30
EPS = 1e-05
RSQRT2 = 1.0 / math.sqrt(2.0)
RSQRT2PI = 1.0 / math.sqrt(2.0 * math.pi)


def dot(left, right, contract):
    return lax.dot_general(
        left, right, (contract, ((), ())), precision=HIGH, preferred_element_type=jnp.float32
    )


def mm(left, right):
    return dot(left, right, ((1,), (0,)))


def mm_nt(left, right):
    return dot(left, right, ((1,), (1,)))


def mm_tn(left, right):
    return dot(left, right, ((0,), (0,)))


def gelu(v):
    return 0.5 * v * (1.0 + lax.erf(v * RSQRT2))


def gelu_slope(v):
    return 0.5 * (1.0 + lax.erf(v * RSQRT2)) + v * (RSQRT2PI * jnp.exp(-0.5 * v * v))


def normalize(rows):
    centre = rows - jnp.mean(rows, axis=-1, keepdims=True)
    scale = lax.rsqrt(jnp.mean(centre * centre, axis=-1, keepdims=True) + EPS)
    return centre * scale, scale


def norm_back(grad, xhat, scale, gain):
    inner = grad * gain
    return (
        inner
        - jnp.mean(inner, axis=-1, keepdims=True)
        - xhat * jnp.mean(inner * xhat, axis=-1, keepdims=True)
    ) * scale


def exchange(value, axis, flip):
    size = lax.axis_size(axis)
    return lax.ppermute(value, axis, [(i, i ^ flip) for i in range(size)])


def model_sum(part):
    if lax.axis_size("mp") != 4:
        raise ValueError("mp size")
    half = part.shape[0] // 2
    pair = part[:half] + exchange(part[half:], "mp", 1)
    total = pair + exchange(pair, "mp", 2)
    return jnp.concatenate([total, exchange(total, "mp", 1)], axis=0)


def place_pieces(pieces):
    count = len(pieces)
    rows, width = pieces[0].shape

    def kernel(*refs):
        out = refs[count]
        place = lax.axis_index("dp")
        for flip in range(count):
            out[jnp.bitwise_xor(place, flip)] = refs[flip][...]

    size = count * rows * width * 4
    return pl.pallas_call(
        kernel,
        out_shape=jax.ShapeDtypeStruct((count, rows, width), jnp.float32),
        in_specs=[pl.BlockSpec(memory_space=pltpu.VMEM)] * count,
        out_specs=pl.BlockSpec(memory_space=pltpu.VMEM),
        cost_estimate=pl.CostEstimate(flops=0, bytes_accessed=2 * size, transcendentals=0),
        name="place_pieces",
    )(*pieces)


def gather_data(shard):
    count = lax.axis_size("dp")
    if count > 8:
        return lax.all_gather(shard, "dp", axis=0, tiled=False)
    pieces = [None] * count
    pieces[0] = shard
    for flip in range(2, count, 2):
        pieces[flip] = exchange(shard, "dp", flip)
    for flip in range(0, count, 2):
        pieces[flip + 1] = exchange(pieces[flip], "dp", 1)
    return place_pieces(pieces)


def scatter_data(blocks):
    count = lax.axis_size("dp")
    if count > 8:
        return lax.psum_scatter(blocks, "dp", scatter_dimension=0, tiled=False)
    place = lax.axis_index("dp")
    high, low = place // 2, place % 2
    grouped = blocks.reshape((count // 2, 2) + blocks.shape[1:])
    away = lax.dynamic_index_in_dim(grouped, 1 - low, 1, keepdims=False)
    kept = lax.dynamic_index_in_dim(grouped, low, 1, keepdims=False)
    pair = kept + exchange(away, "dp", 1)
    total = lax.dynamic_index_in_dim(pair, high, 0, keepdims=False)
    for flip in range(1, count // 2):
        piece = lax.dynamic_index_in_dim(pair, high ^ flip, 0, keepdims=False)
        total = total + exchange(piece, "dp", 2 * flip)
    return total


def data_sum(value):
    count = lax.axis_size("dp")
    if count > 8:
        return lax.psum(value, "dp")
    flip = 1
    while flip < count:
        value = value + exchange(value, "dp", flip)
        flip *= 2
    return value


def split_heads(rows):
    return rows.reshape(rows.shape[0], -1, HEAD)


def attend(queries, keys, values, allowed):
    factor = 1.0 / math.sqrt(HEAD)
    q, k, v = split_heads(queries), split_heads(keys), split_heads(values)
    scores = jnp.einsum("qhe,khe->hqk", q, k, precision=HIGH) * factor
    scores = jnp.where(allowed[None], scores, NEG)
    peaks = jnp.max(scores, axis=-1, keepdims=True)
    weight = jnp.exp(scores - peaks)
    totals = jnp.sum(weight, axis=-1, keepdims=True)
    output = jnp.einsum("hqk,khe->qhe", weight / totals, v, precision=HIGH)
    return output.reshape(queries.shape), peaks + jnp.log(totals)


def attend_back(queries, keys, values, allowed, output, log_total, grad):
    factor = 1.0 / math.sqrt(HEAD)
    q, k, v = split_heads(queries), split_heads(keys), split_heads(values)
    grad_out, out = split_heads(grad), split_heads(output)
    scores = jnp.einsum("qhe,khe->hqk", q, k, precision=HIGH) * factor
    probs = jnp.where(allowed[None], jnp.exp(scores - log_total), 0.0)
    grad_v = jnp.einsum("hqk,qhe->khe", probs, grad_out, precision=HIGH)
    grad_p = jnp.einsum("qhe,khe->hqk", grad_out, v, precision=HIGH)
    inner = jnp.sum(grad_out * out, axis=-1)
    grad_s = probs * (grad_p - inner.T[:, :, None]) * factor
    grad_q = jnp.einsum("hqk,khe->qhe", grad_s, k, precision=HIGH)
    grad_k = jnp.einsum("hqk,qhe->khe", grad_s, q, precision=HIGH)
    return (
        grad_q.reshape(queries.shape),
        grad_k.reshape(keys.shape),
        grad_v.reshape(values.shape),
    )


def rows_of(flat, width):
    flat = flat.reshape(-1)
    short = -flat.shape[0] % width
    return jnp.pad(flat, (0, short)).reshape(-1, width)


def pad_rows(rows):
    return jnp.pad(rows, ((0, -rows.shape[0] % 8), (0, 0)))


def attn_pack(weight, out_weight):
    return jnp.concatenate([weight[0], weight[1], weight[2], out_weight.T], axis=1)


def body(
    mel_frames,
    frame_mask,
    token_ids,
    token_mask,
    embedding,
    conv_one,
    conv_two,
    enc_qkv,
    enc_out,
    enc_up,
    enc_down,
    cross_qkv,
    cross_out,
    dec_qkv,
    dec_out,
    dec_up,
    dec_down,
    norm_params,
    cotangent,
):
    n_dp = lax.axis_size("dp")
    dp_place, mp_place = lax.axis_index("dp"), lax.axis_index("mp")
    turned = (mp_place % 2) == 1
    frames = mel_frames.shape[0] // 2
    mel = mel_frames.shape[1]
    tokens, width = cotangent.shape
    local = enc_qkv.shape[2]
    taps, chans = conv_one.shape[0], conv_one.shape[2]

    def turn(rows):
        half = rows.shape[0] // 2
        return jnp.where(turned, jnp.concatenate([rows[half:], rows[:half]], axis=0), rows)

    def positions(count):
        index = lax.broadcasted_iota(jnp.int32, (count, 1), 0)
        return jnp.where(turned, jnp.where(index >= count // 2, index - count // 2, index + count // 2), index)

    def sinusoid(count):
        half_width = width // 2
        rates = jnp.exp(-math.log(10000.0) * jnp.arange(half_width).astype(jnp.float32) / (half_width - 1))
        angles = positions(count).astype(jnp.float32) * rates[None, :]
        return jnp.concatenate([jnp.sin(angles), jnp.cos(angles)], axis=1)

    conv_rows = pad_rows(
        jnp.concatenate(
            [
                conv_two.reshape(-1, width),
                rows_of(conv_one.transpose(2, 0, 1), width),
                rows_of(norm_params, width),
            ],
            axis=0,
        )
    )
    stem_all = gather_data(conv_rows)
    enc_attn_all = gather_data(attn_pack(enc_qkv, enc_out)).reshape(width, -1)
    dec_attn_all = gather_data(attn_pack(dec_qkv, dec_out)).reshape(width, -1)
    enc_mlp_all = gather_data(jnp.concatenate([enc_up, enc_down.T], axis=0))
    cross_all = gather_data(attn_pack(cross_qkv, cross_out)).reshape(width, -1)
    dec_mlp_all = gather_data(jnp.concatenate([dec_up, dec_down.T], axis=0))

    part = width // n_dp
    two_rows = taps * chans
    one_size = taps * mel * chans
    one_rows = -(-one_size // width)
    stem_width = n_dp * chans
    w_two = (
        stem_all[:, :two_rows]
        .reshape(n_dp, taps, chans, width)
        .transpose(1, 0, 2, 3)
        .reshape(taps * stem_width, width)
    )
    w_one = (
        stem_all[:, two_rows : two_rows + one_rows]
        .reshape(n_dp, -1)[:, :one_size]
        .reshape(stem_width, taps * mel)
    )
    norms = (
        stem_all[:, two_rows + one_rows :]
        .reshape(n_dp, -1)[:, : 12 * part]
        .reshape(n_dp, 6, 2, part)
        .transpose(1, 2, 0, 3)
        .reshape(6, 2, width)
    )
    w_both = jnp.concatenate(
        [jnp.pad(w_one, ((0, 0), (0, mel))), jnp.pad(w_one, ((0, 0), (mel, 0)))], axis=0
    )
    ff = enc_up.shape[1]
    enc_up_all = enc_mlp_all[:, :part].reshape(width, ff)
    enc_down_all = enc_mlp_all[:, part:].reshape(width, ff)
    dec_up_all = dec_mlp_all[:, :part].reshape(width, ff)
    dec_down_all = dec_mlp_all[:, part:].reshape(width, ff)

    frame_row = lax.dynamic_index_in_dim(frame_mask, dp_place, 0, keepdims=False) > 0
    token_row = lax.dynamic_index_in_dim(token_mask, dp_place, 0, keepdims=False) > 0
    frame_ok, token_ok = turn(frame_row), turn(token_row)
    frame_allowed = frame_ok[None, :]
    text_at = positions(tokens)
    self_allowed = (text_at.reshape(1, -1) <= text_at) & token_ok[None, :]
    cot = turn(cotangent)

    frame_at = positions(frames)
    first, last = frame_at == 0, frame_at == frames - 1
    both = turn(mel_frames.reshape(frames, 2 * mel))
    before = jnp.where(first, 0.0, jnp.roll(both[:, mel:], 1, axis=0))
    after = jnp.where(last, 0.0, jnp.roll(both[:, :mel], -1, axis=0))
    window = jnp.concatenate([before, both, after], axis=1)
    pre_one = mm_nt(window, w_both)
    stem_one = gelu(pre_one)
    odd = stem_one[:, stem_width:]
    stem_cat = jnp.concatenate([jnp.where(first, 0.0, jnp.roll(odd, 1, axis=0)), stem_one], axis=1)
    stem_sum = model_sum(mm(stem_cat, w_two))
    stream_zero = gelu(stem_sum) + sinusoid(frames)

    hat_zero, scale_zero = normalize(stream_zero)
    ln_zero = hat_zero * norms[0, 0] + norms[0, 1]
    enc_three = mm(ln_zero, enc_attn_all[:, : 3 * local])
    enc_q, enc_k, enc_v = (enc_three[:, i * local : (i + 1) * local] for i in range(3))
    enc_mixed, enc_lse = attend(enc_q, enc_k, enc_v, frame_allowed)
    enc_attn = model_sum(mm_nt(enc_mixed, enc_attn_all[:, 3 * local :]))
    stream_one = stream_zero + enc_attn
    hat_one, scale_one = normalize(stream_one)
    ln_one = hat_one * norms[1, 0] + norms[1, 1]
    enc_pre = mm(ln_one, enc_up_all)
    enc_hidden = gelu(enc_pre)
    enc_mlp = model_sum(mm_nt(enc_hidden, enc_down_all))
    stream_two = stream_one + enc_mlp
    hat_two, scale_two = normalize(stream_two)
    memory = hat_two * norms[2, 0] + norms[2, 1]
    cross_two = mm(memory, cross_all[:, local : 3 * local])
    cross_k, cross_v = cross_two[:, :local], cross_two[:, local:]

    vocab_rows, embed_width = embedding.shape
    local_ids = token_ids.reshape(-1) - dp_place * vocab_rows
    owned = (local_ids >= 0) & (local_ids < vocab_rows)
    safe_ids = jnp.clip(local_ids, 0, vocab_rows - 1)
    picked = jnp.where(owned[:, None], jnp.take(embedding, safe_ids, axis=0), 0.0)
    share = lax.psum_scatter(picked, "dp", scatter_dimension=0, tiled=True)
    text_zero = turn(lax.all_gather(share, "mp", axis=1, tiled=True)) + sinusoid(tokens)

    hat_three, scale_three = normalize(text_zero)
    ln_three = hat_three * norms[3, 0] + norms[3, 1]
    dec_three = mm(ln_three, dec_attn_all[:, : 3 * local])
    dec_q, dec_k, dec_v = (dec_three[:, i * local : (i + 1) * local] for i in range(3))
    dec_mixed, dec_lse = attend(dec_q, dec_k, dec_v, self_allowed)
    dec_attn = model_sum(mm_nt(dec_mixed, dec_attn_all[:, 3 * local :]))
    text_one = text_zero + dec_attn
    hat_four, scale_four = normalize(text_one)
    ln_four = hat_four * norms[4, 0] + norms[4, 1]
    cross_q = mm(ln_four, cross_all[:, :local])
    cross_mixed, cross_lse = attend(cross_q, cross_k, cross_v, frame_allowed)
    cross_attn = model_sum(mm_nt(cross_mixed, cross_all[:, 3 * local :]))
    text_two = text_one + cross_attn
    hat_five, scale_five = normalize(text_two)
    ln_five = hat_five * norms[5, 0] + norms[5, 1]
    dec_pre = mm(ln_five, dec_up_all)
    dec_hidden = gelu(dec_pre)
    dec_mlp = model_sum(mm_nt(dec_hidden, dec_down_all))
    decoded = text_two + dec_mlp

    def half_of(rows):
        return rows[: rows.shape[0] // 2]

    frame_weight = half_of(frame_ok).astype(jnp.float32)[:, None]
    token_weight = half_of(token_ok).astype(jnp.float32)[:, None]

    def squares(rows, weight):
        kept = half_of(rows)
        return jnp.sum(kept * kept * weight)

    local_sums = jnp.stack(
        [squares(x, frame_weight) for x in (stream_zero, enc_attn, enc_mlp, stream_two)]
        + [squares(x, token_weight) for x in (text_zero, dec_attn, cross_attn, dec_mlp, decoded)]
    )
    local_sums = local_sums + exchange(local_sums, "mp", 1)
    square_sums = data_sum(local_sums)
    frame_total = jnp.sum((frame_mask > 0).astype(jnp.float32))
    token_total = jnp.sum((token_mask > 0).astype(jnp.float32))
    counts = jnp.concatenate([jnp.full((4,), frame_total), jnp.full((5,), token_total)])
    rms_stats = jnp.sqrt(square_sums / (counts * width))

    def norm_grads(grad, xhat):
        kept = half_of(grad)
        return jnp.stack([jnp.sum(kept * half_of(xhat), axis=0), jnp.sum(kept, axis=0)])

    def block(grad):
        return grad.reshape(n_dp, grad.shape[0] // n_dp, grad.shape[1])

    grad_dec_down = scatter_data(block(mm_tn(cot, dec_hidden)))
    grad_pre = mm(cot, dec_down_all) * gelu_slope(dec_pre)
    grad_dec_up = scatter_data(block(mm_tn(ln_five, grad_pre)))
    grad_ln = model_sum(mm_nt(grad_pre, dec_up_all))
    norm_five = norm_grads(grad_ln, hat_five)
    grad_text_two = cot + norm_back(grad_ln, hat_five, scale_five, norms[5, 0])

    grad_cross_out = mm_tn(grad_text_two, cross_mixed)
    grad_cq, grad_ck, grad_cv = attend_back(
        cross_q,
        cross_k,
        cross_v,
        frame_allowed,
        cross_mixed,
        cross_lse,
        mm(grad_text_two, cross_all[:, 3 * local :]),
    )
    grad_ckv = jnp.concatenate([grad_ck, grad_cv], axis=1)
    grad_cross = scatter_data(
        block(
            jnp.concatenate([mm_tn(ln_four, grad_cq), mm_tn(memory, grad_ckv), grad_cross_out], axis=1)
        )
    )
    grad_memory = model_sum(mm_nt(grad_ckv, cross_all[:, local : 3 * local]))
    grad_ln = model_sum(mm_nt(grad_cq, cross_all[:, :local]))
    norm_four = norm_grads(grad_ln, hat_four)
    grad_text_one = grad_text_two + norm_back(grad_ln, hat_four, scale_four, norms[4, 0])

    grad_dec_out = mm_tn(grad_text_one, dec_mixed)
    grad_three = jnp.concatenate(
        attend_back(
            dec_q,
            dec_k,
            dec_v,
            self_allowed,
            dec_mixed,
            dec_lse,
            mm(grad_text_one, dec_attn_all[:, 3 * local :]),
        ),
        axis=1,
    )
    grad_dec_attn = scatter_data(
        block(jnp.concatenate([mm_tn(ln_three, grad_three), grad_dec_out], axis=1))
    )
    grad_ln = model_sum(mm_nt(grad_three, dec_attn_all[:, : 3 * local]))
    norm_three = norm_grads(grad_ln, hat_three)
    grad_text_zero = grad_text_one + norm_back(grad_ln, hat_three, scale_three, norms[3, 0])
    grad_share = lax.dynamic_slice_in_dim(turn(grad_text_zero), mp_place * embed_width, embed_width, 1)
    grad_rows = lax.all_gather(grad_share, "dp", axis=0, tiled=True)
    grad_embedding = (
        jnp.zeros(embedding.shape, jnp.float32)
        .at[safe_ids]
        .add(jnp.where(owned[:, None], grad_rows, 0.0))
    )

    norm_two = norm_grads(grad_memory, hat_two)
    grad_stream_two = norm_back(grad_memory, hat_two, scale_two, norms[2, 0])
    grad_enc_down = scatter_data(block(mm_tn(grad_stream_two, enc_hidden)))
    grad_pre = mm(grad_stream_two, enc_down_all) * gelu_slope(enc_pre)
    grad_enc_up = scatter_data(block(mm_tn(ln_one, grad_pre)))
    grad_ln = model_sum(mm_nt(grad_pre, enc_up_all))
    norm_one = norm_grads(grad_ln, hat_one)
    grad_stream_one = grad_stream_two + norm_back(grad_ln, hat_one, scale_one, norms[1, 0])

    grad_enc_out = mm_tn(grad_stream_one, enc_mixed)
    grad_three = jnp.concatenate(
        attend_back(
            enc_q,
            enc_k,
            enc_v,
            frame_allowed,
            enc_mixed,
            enc_lse,
            mm(grad_stream_one, enc_attn_all[:, 3 * local :]),
        ),
        axis=1,
    )
    grad_enc_attn = scatter_data(
        block(jnp.concatenate([mm_tn(ln_zero, grad_three), grad_enc_out], axis=1))
    )
    grad_ln = model_sum(mm_nt(grad_three, enc_attn_all[:, : 3 * local]))
    norm_zero = norm_grads(grad_ln, hat_zero)
    grad_stream_zero = grad_stream_one + norm_back(grad_ln, hat_zero, scale_zero, norms[0, 0])

    grad_stem = grad_stream_zero * gelu_slope(stem_sum)
    grad_w_two = mm_tn(stem_cat, grad_stem)
    grad_cat = mm_nt(grad_stem, w_two)
    grad_back = jnp.roll(jnp.where(first, 0.0, grad_cat[:, :stem_width]), -1, axis=0)
    grad_one = jnp.concatenate(
        [grad_cat[:, stem_width : 2 * stem_width], grad_cat[:, 2 * stem_width :] + grad_back], axis=1
    )
    grad_pre = grad_one * gelu_slope(pre_one)
    grad_both = mm_tn(grad_pre, window)
    grad_w_one = grad_both[:stem_width, : taps * mel] + grad_both[stem_width:, mel:]
    grad_window = mm(grad_pre, w_both)
    grad_mel = grad_window[:, mel : 3 * mel] + jnp.concatenate(
        [
            jnp.roll(jnp.where(last, 0.0, grad_window[:, 3 * mel :]), 1, axis=0),
            jnp.roll(jnp.where(first, 0.0, grad_window[:, :mel]), -1, axis=0),
        ],
        axis=1,
    )
    grad_mel = turn(model_sum(grad_mel)).reshape(mel_frames.shape)

    norm_all = jnp.stack([norm_zero, norm_one, norm_two, norm_three, norm_four, norm_five])
    norm_all = norm_all + exchange(norm_all, "mp", 1)
    norm_blocks = norm_all.reshape(12, n_dp, part).transpose(1, 0, 2).reshape(n_dp, -1)
    one_blocks = grad_w_one.reshape(n_dp, one_size)

    def lay(flat):
        short = -flat.shape[1] % width
        return jnp.pad(flat, ((0, 0), (0, short))).reshape(n_dp, -1, width)

    two_blocks = (
        grad_w_two.reshape(taps, n_dp, chans, width).transpose(1, 0, 2, 3).reshape(n_dp, -1, width)
    )
    stem_blocks = jnp.concatenate([two_blocks, lay(one_blocks), lay(norm_blocks)], axis=1)
    stem_blocks = jnp.pad(stem_blocks, ((0, 0), (0, -stem_blocks.shape[1] % 8), (0, 0)))
    stem_grads = scatter_data(stem_blocks)
    grad_conv_two = stem_grads[:two_rows].reshape(taps, chans, width)
    grad_conv_one = (
        stem_grads[two_rows : two_rows + one_rows]
        .reshape(-1)[:one_size]
        .reshape(chans, taps, mel)
        .transpose(1, 2, 0)
    )
    grad_norms = stem_grads[two_rows + one_rows :].reshape(-1)[: 12 * part].reshape(6, 2, part)

    def three(grads):
        return jnp.stack([grads[:, i * local : (i + 1) * local] for i in range(3)])

    return (
        turn(decoded),
        grad_mel,
        grad_embedding,
        grad_conv_one,
        grad_conv_two,
        three(grad_enc_attn),
        grad_enc_attn[:, 3 * local :].T,
        grad_enc_up,
        grad_enc_down.T,
        three(grad_cross),
        grad_cross[:, 3 * local :].T,
        three(grad_dec_attn),
        grad_dec_attn[:, 3 * local :].T,
        grad_dec_up,
        grad_dec_down.T,
        grad_norms,
        rms_stats,
    )


def solution(mesh):
    placed = (
        P("dp", None),
        P(),
        P(),
        P(),
        P("dp", "mp"),
        P(None, None, ("dp", "mp")),
        P(None, ("dp", "mp"), None),
        P(None, "dp", "mp"),
        P("mp", "dp"),
        P("dp", "mp"),
        P("mp", "dp"),
        P(None, "dp", "mp"),
        P("mp", "dp"),
        P(None, "dp", "mp"),
        P("mp", "dp"),
        P("dp", "mp"),
        P("mp", "dp"),
        P(None, None, "dp"),
        P("dp", None),
    )
    return jax.shard_map(
        body,
        mesh=mesh,
        in_specs=placed,
        out_specs=(
            P("dp", None),
            P("dp", None),
            P("dp", "mp"),
            P(None, None, ("dp", "mp")),
            P(None, ("dp", "mp"), None),
            P(None, "dp", "mp"),
            P("mp", "dp"),
            P("dp", "mp"),
            P("mp", "dp"),
            P(None, "dp", "mp"),
            P("mp", "dp"),
            P(None, "dp", "mp"),
            P("mp", "dp"),
            P("dp", "mp"),
            P("mp", "dp"),
            P(None, None, "dp"),
            P(),
        ),
        check_vma=False,
    )
```

time: 2470 us -> 1120 us (0.45)
  waiting for transfers between devices: 1340 us -> 465 us
  matrix products: 430 us -> 173 us
  local copies, waits for them, and re-layouts: 335 us -> 133 us
  blocking collectives: 200 us -> 0 us
  starting transfers between devices: 3.75 us -> 110 us
  other arithmetic: 125 us -> 184 us
    ppermute x0 -> x118, waiting for transfers between devices: none -> 465 us  [exchange(): return lax.ppermute(value, axis, [(i, i ^ flip) for i in range(size)])]
    unnamed x41 -> x3, waiting for transfers between devices: 404 us -> 0.05 us
    psum x9 -> x0, waiting for transfers between devices: 382 us -> none  [the longest x4 238 us: input_sum(): return lax.psum((grad_rows, grad_norm), 'mp')]
    reduce_scatter x6 -> x1, waiting for transfers between devices: 329 us -> 0.01 us  [body(): share = lax.psum_scatter(picked, 'dp', scatter_dimension=0, tiled=True)]
    dot_general x81 -> x57, matrix products: 413 us -> 173 us  [the longest x39 106 us: dot(): lax.dot_general(left, right, (contract, ((), ())), precision=HIGH, prefer...]
    all_gather x10 -> x2, waiting for transfers between devices: 230 us -> 0.01 us  [the longest x1 0.01 us: body(): lax.all_gather(share, 'mp', axis=1, tiled=True)]
    all_gather x5 -> x0, blocking collectives: 170 us -> none  [the longest x1 34.5 us: body(): lax.all_gather(cross_out, 'dp', axis=1, tiled=True)]
    ppermute x0 -> x118, starting transfers between devices: none -> 110 us  [exchange(): return lax.ppermute(value, axis, [(i, i ^ flip) for i in range(size)])]
  transfers between devices with their start and end apart: 33 -> 121, of which waited for: 26 -> 43; matrix products, arithmetic and copies ran while one was open for 23% -> 34% of each run, Pallas kernels for 0% -> 2%
where the time goes in v1:
time: 1120 us; the launch traced here: 1100 us
  waiting for transfers between devices  465 us (42%)
  other arithmetic  184 us (16%)
  matrix products  173 us (15%)
  local copies, waits for them, and re-layouts  133 us (12%)
  starting transfers between devices  110 us (10%)
  Pallas kernels  22.2 us (2%)
  between operations  18.1 us (2%)
    ppermute x118, waiting for transfers between devices, exchange(): return lax.ppermute(value, axis, [(i, i ^ flip) for i in range(size)])  465 us
    ppermute x118, starting transfers between devices, exchange(): return lax.ppermute(value, axis, [(i, i ^ flip) for i in range(size)])  110 us
    dot_general x39, matrix products, dot(): lax.dot_general(left, right, (contract, ((), ())), precision=HIGH, prefer...  106 us
    unnamed x480, local copies, waits for them, and re-layouts  51.1 us
    scatter-add x1, other arithmetic, body(): grad_embedding = jnp.zeros(embedding.shape, jnp.float32).at[safe_ids].add...  24.1 us
  transfers between devices with their start and end apart: 121, of which 43 were waited for; matrix products, arithmetic and copies ran while one was open for 34% of the time, Pallas kernels for 2%

profile of v1, /device:TPU:0, one launch (start us, length us, event | category | flops | bytes accessed | tf_op | source)
XLA Modules:
  0.0 1104.6 jit_solution(3194881980029047104)
XLA Ops:
  25.2 13.9 %collective-permute-done.3.refs_4_ = f32[88,768]{1,0:T(8,128)} collective-permute-done((f32[88,768]{1,0:T(8,128)}, f32[88,768]{1,0:T(8,128)}, u32[]{:S(2)}, u32[]{:S(2)}) %collective-permute-start.3) | collective-permute-done | bytes 270368 | tf_op jit(solution)/shard_map/ppermute | solution.py:62
  41.4 7.2 collective-permute-done.4.refs_5_
  80.8 7.0 copy.124
  87.9 15.2 %gather_fusion = f32[3072,192]{1,0:T(8,128)} fusion(f32[6480,192]{1,0:T(8,128)} %copy.124, s32[3072]{0:T(1024)S(1)} %broadcast_clamp_fusion), kind=kCustom, calls=%fused_computation | custom fusion | bytes 4730880 | tf_op jit(solution)/shard_map/jit(_take)/gather | solution.py:321
  103.1 12.0 %collective-permute-done.18 = f32[512,768]{1,0:T(8,128)S(1)} collective-permute-done((f32[512,768]{1,0:T(8,128)}, f32[512,768]{1,0:T(8,128)S(1)}, u32[]{:S(2)}, u32[]{:S(2)}) %collective-permute-start.18) | collective-permute-done | bytes 1572896 | tf_op jit(solution)/shard_map/ppermute | solution.py:62
  121.2 7.0 multiply_sine_fusion
  132.4 7.0 collective-permute-done.26.refs_7_
  139.4 9.2 collective-permute-done.24.refs_5_
  148.6 7.5 collective-permute-done.22.refs_3_
  210.3 15.2 %collective-permute-done.10.refs_4_ = f32[96,768]{1,0:T(8,128)} collective-permute-done((f32[96,768]{1,0:T(8,128)S(1)}, f32[96,768]{1,0:T(8,128)}, u32[]{:S(2)}, u32[]{:S(2)}) %collective-permute-start.10) | collective-permute-done | bytes 294944 | tf_op jit(solution)/shard_map/ppermute | solution.py:62
  247.8 32.0 %collective-permute-done.33.refs_4_ = f32[192,768]{1,0:T(8,128)} collective-permute-done((f32[192,768]{1,0:T(8,128)}, f32[192,768]{1,0:T(8,128)}, u32[]{:S(2)}, u32[]{:S(2)}) %collective-permute-start.33) | collective-permute-done | bytes 589856 | tf_op jit(solution)/shard_map/ppermute | solution.py:62
  288.7 7.6 collective-permute-done.34.refs_5_
  296.3 10.2 collective-permute-done.32.refs_3_
  357.1 40.9 %collective-permute-done.15 = f32[192,768]{1,0:T(8,128)} collective-permute-done((f32[192,768]{1,0:T(8,128)}, f32[192,768]{1,0:T(8,128)}, u32[]{:S(2)}, u32[]{:S(2)}) %collective-permute-start.15) | collective-permute-done | bytes 589856 | tf_op jit(solution)/shard_map/ppermute | solution.py:62
  460.3 8.6 collective-permute-done.53.refs_4_
  476.9 12.1 %collective-permute-done.54.refs_5_ = f32[192,768]{1,0:T(8,128)} collective-permute-done((f32[192,768]{1,0:T(8,128)}, f32[192,768]{1,0:T(8,128)}, u32[]{:S(2)}, u32[]{:S(2)}) %collective-permute-start.54) | collective-permute-done | bytes 589856 | tf_op jit(solution)/shard_map/ppermute | solution.py:62
  489.1 12.1 %collective-permute-done.52.refs_3_ = f32[192,768]{1,0:T(8,128)} collective-permute-done((f32[192,768]{1,0:T(8,128)}, f32[192,768]{1,0:T(8,128)}, u32[]{:S(2)}, u32[]{:S(2)}) %collective-permute-start.52) | collective-permute-done | bytes 589856 | tf_op jit(solution)/shard_map/ppermute | solution.py:62
  532.9 10.9 collective-permute-done.61
  543.9 7.8 collective-permute-done.106
  554.8 21.5 %collective-permute-done.110 = f32[4,96,768]{2,1,0:T(8,128)S(1)} collective-permute-done((f32[4,96,768]{2,1,0:T(8,128)S(1)}, f32[4,96,768]{2,1,0:T(8,128)S(1)}, u32[]{:S(2)}, u32[]{:S(2)}) %collective-permute-start.110) | collective-permute-done | bytes 1179680 | tf_op jit(solution)/shard_map/ppermute | solution.py:62
  583.9 10.5 collective-permute-done.108
  600.7 16.4 %collective-permute-done.112 = f32[96,768]{1,0:T(8,128)S(1)} collective-permute-done((f32[96,768]{1,0:T(8,128)S(1)}, f32[96,768]{1,0:T(8,128)S(1)}, u32[]{:S(2)}, u32[]{:S(2)}) %collective-permute-start.112) | collective-permute-done | bytes 294944 | tf_op jit(solution)/shard_map/ppermute | solution.py:62
  687.2 20.4 %collective-permute-done.76 = f32[192,768]{1,0:T(8,128)} collective-permute-done((f32[192,768]{1,0:T(8,128)}, f32[192,768]{1,0:T(8,128)}, u32[]{:S(2)}, u32[]{:S(2)}) %collective-permute-start.76) | collective-permute-done | bytes 589856 | tf_op jit(solution)/shard_map/ppermute | solution.py:62
  764.3 19.3 %collective-permute-done.67 = f32[512,768]{1,0:T(8,128)} collective-permute-done((f32[512,768]{1,0:T(8,128)}, f32[512,768]{1,0:T(8,128)}, u32[]{:S(2)}, u32[]{:S(2)}) %collective-permute-start.67) | collective-permute-done | bytes 1572896 | tf_op jit(solution)/shard_map/ppermute | solution.py:62
  805.4 13.1 %collective-permute-done.104 = f32[96,768]{1,0:T(8,128)} collective-permute-done((f32[96,768]{1,0:T(8,128)}, f32[96,768]{1,0:T(8,128)}, u32[]{:S(2)}, u32[]{:S(2)}) %collective-permute-start.104) | collective-permute-done | bytes 294944 | tf_op jit(solution)/shard_map/ppermute | solution.py:62
  834.1 9.3 fusion.3
  843.4 9.7 multiply_multiply_fusion
  891.2 20.0 %collective-permute-done.94 = f32[4,96,768]{2,1,0:T(8,128)} collective-permute-done((f32[4,96,768]{2,1,0:T(8,128)}, f32[4,96,768]{2,1,0:T(8,128)}, u32[]{:S(2)}, u32[]{:S(2)}) %collective-permute-start.94) | collective-permute-done | bytes 1179680 | tf_op jit(solution)/shard_map/ppermute | solution.py:62
  916.8 27.1 %collective-permute-done.90 = f32[4,96,768]{2,1,0:T(8,128)} collective-permute-done((f32[4,96,768]{2,1,0:T(8,128)}, f32[4,96,768]{2,1,0:T(8,128)}, u32[]{:S(2)}, u32[]{:S(2)}) %collective-permute-start.90) | collective-permute-done | bytes 1179680 | tf_op jit(solution)/shard_map/ppermute | solution.py:62
  949.8 22.8 %collective-permute-done.96 = f32[96,768]{1,0:T(8,128)S(1)} collective-permute-done((f32[96,768]{1,0:T(8,128)S(1)}, f32[96,768]{1,0:T(8,128)S(1)}, u32[]{:S(2)}, u32[]{:S(2)}) %collective-permute-start.96) | collective-permute-done | bytes 294944 | tf_op jit(solution)/shard_map/ppermute | solution.py:62
  1031.1 24.1 %scatter_custom_fusion = f32[6480,192]{1,0:T(8,128)} fusion(s32[3072]{0:T(1024)} %bitcast.507, f32[]{:T(128)} %constant.267.clone.1, f32[3072,192]{1,0:T(8,128)} %all-gather.5.cloned.1.call-done, pred[3072]{0:T(1024)(128)(4,1)S(1)} %copy-done.195), kind=kCustom, calls=%fused_computation.29 | custom fusion | flops 1179648 | bytes 8126464 | tf_op jit(solution)/shard_map/scatter-add | solution.py:425
  1081.8 12.9 %collective-permute-done.84 = f32[88,768]{1,0:T(8,128)} collective-permute-done((f32[88,768]{1,0:T(8,128)}, f32[88,768]{1,0:T(8,128)}, u32[]{:S(2)}, u32[]{:S(2)}) %collective-permute-start.84) | collective-permute-done | bytes 270368 | tf_op jit(solution)/shard_map/ppermute | solution.py:62
  (1047 shorter events, 616.1 us)
Async XLA Ops:
  7.2 201.1 %reduce-scatter.2.cloned.1.call-start = ((), (), s32[]{:S(2)}) async-start(), calls=%async_computation.1 | async-start | bytes 3538944 | tf_op jit(solution)/shard_map/reduce_scatter | solution.py:322
  70.5 57.7 %collective-permute-start.25 = (f32[96,768]{1,0:T(8,128)S(1)}, f32[96,768]{1,0:T(8,128)}, u32[]{:S(2)}, u32[]{:S(2)}) collective-permute-start(f32[96,768]{1,0:T(8,128)S(1)} %pad_maximum_fusion.22.refs_0_), channel_id=1, source_target_pairs={{0,24},{4,28},{8,16},{12,20},{16,8},{20,12},{24,0},{28,4},{1,25},{... | collective-permute-start | bytes 884744 | tf_op jit(solution)/shard_map/ppermute | solution.py:62
  72.8 55.9 %collective-permute-start.23 = (f32[96,768]{1,0:T(8,128)S(1)}, f32[96,768]{1,0:T(8,128)}, u32[]{:S(2)}, u32[]{:S(2)}) collective-permute-start(f32[96,768]{1,0:T(8,128)S(1)} %pad_maximum_fusion.22.refs_0_), channel_id=1, source_target_pairs={{0,16},{4,20},{8,24},{12,28},{16,0},{20,4},{24,8},{28,12},{1,17},{... | collective-permute-start | bytes 884744 | tf_op jit(solution)/shard_map/ppermute | solution.py:62
  72.8 57.4 %collective-permute-start.21 = (f32[96,768]{1,0:T(8,128)S(1)}, f32[96,768]{1,0:T(8,128)}, u32[]{:S(2)}, u32[]{:S(2)}) collective-permute-start(f32[96,768]{1,0:T(8,128)S(1)} %pad_maximum_fusion.22.refs_0_), channel_id=1, source_target_pairs={{0,8},{4,12},{8,0},{12,4},{16,24},{20,28},{24,16},{28,20},{1,9},{5... | collective-permute-start | bytes 884744 | tf_op jit(solution)/shard_map/ppermute | solution.py:62
  74.9 57.4 %collective-permute-start.20 = (f32[96,768]{1,0:T(8,128)S(1)}, f32[96,768]{1,0:T(8,128)}, u32[]{:S(2)}, u32[]{:S(2)}) collective-permute-start(f32[96,768]{1,0:T(8,128)S(1)} %pad_maximum_fusion.22.refs_0_), channel_id=1, source_target_pairs={{0,4},{4,0},{8,12},{12,8},{16,20},{20,16},{24,28},{28,24},{1,5},{5... | collective-permute-start | bytes 884744 | tf_op jit(solution)/shard_map/ppermute | solution.py:62
  120.3 197.1 %all-gather.3.cloned.1.call-start = ((), (), s32[]{:S(2)}) async-start(), calls=%async_computation.2 | async-start | bytes 1474560 | tf_op jit(solution)/shard_map/all_gather | solution.py:323
  203.0 108.3 %collective-permute-start.28 = (f32[512,768]{1,0:T(8,128)}, f32[512,768]{1,0:T(8,128)}, u32[]{:S(2)}, u32[]{:S(2)}) collective-permute-start(f32[512,768]{1,0:T(8,128)} %slice_add_fusion.4), channel_id=1, source_target_pairs={{0,2},{1,3},{2,0},{3,1},{4,6},{5,7},{6,4},{7,5},{8,10},{9,11},{10,... | collective-permute-start | bytes 4718600 | tf_op jit(solution)/shard_map/ppermute | solution.py:62
  210.2 820.9 %all-gather.5.cloned.1.call-start = ((), (), s32[]{:S(2)}) async-start(), calls=%async_computation.3 | async-start | bytes 3538944 | tf_op jit(solution)/shard_map/all_gather | solution.py:421
  230.4 49.4 %collective-permute-start.33 = (f32[192,768]{1,0:T(8,128)}, f32[192,768]{1,0:T(8,128)}, u32[]{:S(2)}, u32[]{:S(2)}) collective-permute-start(f32[192,768]{1,0:T(8,128)} %pad_maximum_fusion.19.refs_0_), channel_id=1, source_target_pairs={{0,16},{4,20},{8,24},{12,28},{16,0},{20,4},{24,8},{28,12},{1,17},{... | collective-permute-start | bytes 1769480 | tf_op jit(solution)/shard_map/ppermute | solution.py:62
  230.4 51.0 %collective-permute-start.31 = (f32[192,768]{1,0:T(8,128)}, f32[192,768]{1,0:T(8,128)}, u32[]{:S(2)}, u32[]{:S(2)}) collective-permute-start(f32[192,768]{1,0:T(8,128)} %pad_maximum_fusion.19.refs_0_), channel_id=1, source_target_pairs={{0,8},{4,12},{8,0},{12,4},{16,24},{20,28},{24,16},{28,20},{1,9},{5... | collective-permute-start | bytes 1769480 | tf_op jit(solution)/shard_map/ppermute | solution.py:62
  242.3 46.3 %collective-permute-start.30 = (f32[192,768]{1,0:T(8,128)}, f32[192,768]{1,0:T(8,128)}, u32[]{:S(2)}, u32[]{:S(2)}) collective-permute-start(f32[192,768]{1,0:T(8,128)} %pad_maximum_fusion.19.refs_0_), channel_id=1, source_target_pairs={{0,4},{4,0},{8,12},{12,8},{16,20},{20,16},{24,28},{28,24},{1,5},{5... | collective-permute-start | bytes 1769480 | tf_op jit(solution)/shard_map/ppermute | solution.py:62
  348.5 55.3 %collective-permute-start.38 = (f32[512,768]{1,0:T(8,128)}, f32[512,768]{1,0:T(8,128)}, u32[]{:S(2)}, u32[]{:S(2)}) collective-permute-start(f32[512,768]{1,0:T(8,128)} %slice_add_fusion.3), channel_id=1, source_target_pairs={{0,2},{1,3},{2,0},{3,1},{4,6},{5,7},{6,4},{7,5},{8,10},{9,11},{10,... | collective-permute-start | bytes 4718600 | tf_op jit(solution)/shard_map/ppermute | solution.py:62
  351.1 46.9 %collective-permute-start.15 = (f32[192,768]{1,0:T(8,128)}, f32[192,768]{1,0:T(8,128)}, u32[]{:S(2)}, u32[]{:S(2)}) collective-permute-start(f32[192,768]{1,0:T(8,128)} %slice_add_fusion.13), channel_id=1, source_target_pairs={{0,2},{1,3},{2,0},{3,1},{4,6},{5,7},{6,4},{7,5},{8,10},{9,11},{10,... | collective-permute-start | bytes 1769480 | tf_op jit(solution)/shard_map/ppermute | solution.py:62
  352.6 47.5 %collective-permute-start.45 = (f32[96,768]{1,0:T(8,128)S(1)}, f32[96,768]{1,0:T(8,128)S(1)}, u32[]{:S(2)}, u32[]{:S(2)}) collective-permute-start(f32[96,768]{1,0:T(8,128)S(1)} %pad_maximum_fusion.23.refs_0_), channel_id=1, source_target_pairs={{0,24},{4,28},{8,16},{12,20},{16,8},{20,12},{24,0},{28,4},{1,25},{... | collective-permute-start | bytes 884744 | tf_op jit(solution)/shard_map/ppermute | solution.py:62
  353.8 48.0 %collective-permute-start.43 = (f32[96,768]{1,0:T(8,128)S(1)}, f32[96,768]{1,0:T(8,128)S(1)}, u32[]{:S(2)}, u32[]{:S(2)}) collective-permute-start(f32[96,768]{1,0:T(8,128)S(1)} %pad_maximum_fusion.23.refs_0_), channel_id=1, source_target_pairs={{0,16},{4,20},{8,24},{12,28},{16,0},{20,4},{24,8},{28,12},{1,17},{... | collective-permute-start | bytes 884744 | tf_op jit(solution)/shard_map/ppermute | solution.py:62
  354.7 47.6 %collective-permute-start.41 = (f32[96,768]{1,0:T(8,128)S(1)}, f32[96,768]{1,0:T(8,128)S(1)}, u32[]{:S(2)}, u32[]{:S(2)}) collective-permute-start(f32[96,768]{1,0:T(8,128)S(1)} %pad_maximum_fusion.23.refs_0_), channel_id=1, source_target_pairs={{0,8},{4,12},{8,0},{12,4},{16,24},{20,28},{24,16},{28,20},{1,9},{5... | collective-permute-start | bytes 884744 | tf_op jit(solution)/shard_map/ppermute | solution.py:62
  422.7 46.2 %collective-permute-start.53 = (f32[192,768]{1,0:T(8,128)}, f32[192,768]{1,0:T(8,128)}, u32[]{:S(2)}, u32[]{:S(2)}) collective-permute-start(f32[192,768]{1,0:T(8,128)} %pad_maximum_fusion.20.refs_0_), channel_id=1, source_target_pairs={{0,16},{4,20},{8,24},{12,28},{16,0},{20,4},{24,8},{28,12},{1,17},{... | collective-permute-start | bytes 1769480 | tf_op jit(solution)/shard_map/ppermute | solution.py:62
  525.7 50.5 %collective-permute-start.110 = (f32[4,96,768]{2,1,0:T(8,128)S(1)}, f32[4,96,768]{2,1,0:T(8,128)S(1)}, u32[]{:S(2)}, u32[]{:S(2)}) collective-permute-start(f32[4,96,768]{2,1,0:T(8,128)S(1)} %dynamic-slice_bitcast_fusion), channel_id=1, source_target_pairs={{0,4},{4,0},{8,12},{12,8},{16,20},{20,16},{24,28},{28,24},{1,5},{5... | collective-permute-start | bytes 3538952 | tf_op jit(solution)/shard_map/ppermute | solution.py:62
  532.4 45.9 %collective-permute-start.58 = (f32[192,768]{1,0:T(8,128)S(1)}, f32[192,768]{1,0:T(8,128)S(1)}, u32[]{:S(2)}, u32[]{:S(2)}) collective-permute-start(f32[192,768]{1,0:T(8,128)S(1)} %slice_add_fusion.11), channel_id=1, source_target_pairs={{0,2},{1,3},{2,0},{3,1},{4,6},{5,7},{6,4},{7,5},{8,10},{9,11},{10,... | collective-permute-start | bytes 1769480 | tf_op jit(solution)/shard_map/ppermute | solution.py:62
  543.9 74.0 %collective-permute-start.62 = (f32[192,768]{1,0:T(8,128)S(1)}, f32[192,768]{1,0:T(8,128)S(1)}, u32[]{:S(2)}, u32[]{:S(2)}) collective-permute-start(f32[192,768]{1,0:T(8,128)S(1)} %get-tuple-element.136), channel_id=1, source_target_pairs={{0,1},{1,0},{2,3},{3,2},{4,5},{5,4},{6,7},{7,6},{8,9},{9,8},{10,11... | collective-permute-start | bytes 1769480 | tf_op jit(solution)/shard_map/ppermute | solution.py:62
  594.3 65.6 %collective-permute-start.59 = (f32[192,768]{1,0:T(8,128)}, f32[192,768]{1,0:T(8,128)}, u32[]{:S(2)}, u32[]{:S(2)}) collective-permute-start(f32[192,768]{1,0:T(8,128)} %add.630), channel_id=1, source_target_pairs={{0,1},{1,0},{2,3},{3,2},{4,5},{5,4},{6,7},{7,6},{8,9},{9,8},{10,11... | collective-permute-start | bytes 1769480 | tf_op jit(solution)/shard_map/ppermute | solution.py:62
  654.6 55.0 %collective-permute-start.98 = (f32[4,96,768]{2,1,0:T(8,128)}, f32[4,96,768]{2,1,0:T(8,128)}, u32[]{:S(2)}, u32[]{:S(2)}) collective-permute-start(f32[4,96,768]{2,1,0:T(8,128)} %dynamic-slice_bitcast_fusion.3), channel_id=1, source_target_pairs={{0,4},{4,0},{8,12},{12,8},{16,20},{20,16},{24,28},{28,24},{1,5},{5... | collective-permute-start | bytes 3538952 | tf_op jit(solution)/shard_map/ppermute | solution.py:62
  658.2 52.8 %collective-permute-start.64 = (f32[512,768]{1,0:T(8,128)}, f32[512,768]{1,0:T(8,128)}, u32[]{:S(2)}, u32[]{:S(2)}) collective-permute-start(f32[512,768]{1,0:T(8,128)} %slice_add_fusion.2), channel_id=1, source_target_pairs={{0,2},{1,3},{2,0},{3,1},{4,6},{5,7},{6,4},{7,5},{8,10},{9,11},{10,... | collective-permute-start | bytes 4718600 | tf_op jit(solution)/shard_map/ppermute | solution.py:62
  687.2 69.1 %collective-permute-start.117 = (f32[9]{0:T(128)}, f32[9]{0:T(128)}, u32[]{:S(2)}, u32[]{:S(2)}) collective-permute-start(f32[9]{0:T(128)} %add.704), channel_id=1, source_target_pairs={{0,16},{4,20},{8,24},{12,28},{16,0},{20,4},{24,8},{28,12},{1,17},{... | collective-permute-start | bytes 116 | tf_op jit(solution)/shard_map/ppermute | solution.py:62
  715.7 45.8 %collective-permute-start.101 = (f32[96,768]{1,0:T(8,128)}, f32[96,768]{1,0:T(8,128)}, u32[]{:S(2)}, u32[]{:S(2)}) collective-permute-start(f32[96,768]{1,0:T(8,128)} %get-tuple-element.183), channel_id=1, source_target_pairs={{0,24},{4,28},{8,16},{12,20},{16,8},{20,12},{24,0},{28,4},{1,25},{... | collective-permute-start | bytes 884744 | tf_op jit(solution)/shard_map/ppermute | solution.py:62
  885.8 58.1 %collective-permute-start.90 = (f32[4,96,768]{2,1,0:T(8,128)}, f32[4,96,768]{2,1,0:T(8,128)}, u32[]{:S(2)}, u32[]{:S(2)}) collective-permute-start(f32[4,96,768]{2,1,0:T(8,128)} %dynamic-slice_bitcast_fusion.5), channel_id=1, source_target_pairs={{0,4},{4,0},{8,12},{12,8},{16,20},{20,16},{24,28},{28,24},{1,5},{5... | collective-permute-start | bytes 3538952 | tf_op jit(solution)/shard_map/ppermute | solution.py:62
  886.6 86.9 %collective-permute-start.70 = (f32[512,768]{1,0:T(8,128)S(1)}, f32[512,768]{1,0:T(8,128)}, u32[]{:S(2)}, u32[]{:S(2)}) collective-permute-start(f32[512,768]{1,0:T(8,128)S(1)} %slice_add_fusion), channel_id=1, source_target_pairs={{0,2},{1,3},{2,0},{3,1},{4,6},{5,7},{6,4},{7,5},{8,10},{9,11},{10,... | collective-permute-start | bytes 4718600 | tf_op jit(solution)/shard_map/ppermute | solution.py:62
  914.7 58.0 %collective-permute-start.96 = (f32[96,768]{1,0:T(8,128)S(1)}, f32[96,768]{1,0:T(8,128)S(1)}, u32[]{:S(2)}, u32[]{:S(2)}) collective-permute-start(f32[96,768]{1,0:T(8,128)S(1)} %get-tuple-element.187), channel_id=1, source_target_pairs={{0,16},{4,20},{8,24},{12,28},{16,0},{20,4},{24,8},{28,12},{1,17},{... | collective-permute-start | bytes 884744 | tf_op jit(solution)/shard_map/ppermute | solution.py:62
  946.3 74.7 %collective-permute-start.91 = (f32[96,768]{1,0:T(8,128)}, f32[96,768]{1,0:T(8,128)}, u32[]{:S(2)}, u32[]{:S(2)}) collective-permute-start(f32[96,768]{1,0:T(8,128)} %get-tuple-element.188), channel_id=1, source_target_pairs={{0,8},{4,12},{8,0},{12,4},{16,24},{20,28},{24,16},{28,20},{1,9},{5... | collective-permute-start | bytes 884744 | tf_op jit(solution)/shard_map/ppermute | solution.py:62
  946.4 74.7 %collective-permute-start.93 = (f32[96,768]{1,0:T(8,128)}, f32[96,768]{1,0:T(8,128)}, u32[]{:S(2)}, u32[]{:S(2)}) collective-permute-start(f32[96,768]{1,0:T(8,128)} %get-tuple-element.189), channel_id=1, source_target_pairs={{0,24},{4,28},{8,16},{12,20},{16,8},{20,12},{24,0},{28,4},{1,25},{... | collective-permute-start | bytes 884744 | tf_op jit(solution)/shard_map/ppermute | solution.py:62
  946.4 78.9 %collective-permute-start.92 = (f32[96,768]{1,0:T(8,128)}, f32[96,768]{1,0:T(8,128)}, u32[]{:S(2)}, u32[]{:S(2)}) collective-permute-start(f32[96,768]{1,0:T(8,128)} %get-tuple-element.190), channel_id=1, source_target_pairs={{0,16},{4,20},{8,24},{12,28},{16,0},{20,4},{24,8},{28,12},{1,17},{... | collective-permute-start | bytes 884744 | tf_op jit(solution)/shard_map/ppermute | solution.py:62
  1017.5 47.1 %collective-permute-start.82 = (f32[4,88,768]{2,1,0:T(8,128)}, f32[4,88,768]{2,1,0:T(8,128)}, u32[]{:S(2)}, u32[]{:S(2)}) collective-permute-start(f32[4,88,768]{2,1,0:T(8,128)} %dynamic-slice_bitcast_fusion.7), channel_id=1, source_target_pairs={{0,4},{4,0},{8,12},{12,8},{16,20},{20,16},{24,28},{28,24},{1,5},{5... | collective-permute-start | bytes 3244040 | tf_op jit(solution)/shard_map/ppermute | solution.py:62
  (322 other events, 5446.8 us)
Sparse Core Ops, SparseCore 0:
  120.4 78.0 reduce-scatter.1
  210.3 35.0 all-gather.2
  891.3 94.9 all-gather.4

commit v2 on v1

--- a/solution.py
+++ b/solution.py
@@ -92,17 +92,43 @@
     )(*pieces)
 
 
+def gather_slow(shard):
+    return lax.all_gather(shard, "dp", axis=0, tiled=False)
+
+
+def split_rows(full, cuts):
+    out = []
+    for r0, r1, c0, c1 in cuts:
+        x = full[:, r0:r1, c0:c1].reshape(full.shape[0] * (r1 - r0), c1 - c0)
+        hi = lax.reduce_precision(x, 8, 7)
+        out.append((hi.astype(BF), (x - hi).astype(BF)))
+    return out
+
+
+def scatter_slow(blocks):
+    return lax.psum_scatter(blocks, "dp", scatter_dimension=0, tiled=False)
+
+
+def tie(value, other):
+    return lax.optimization_barrier((value, other))[0]
+
+
 def gather_data(shard):
     count = lax.axis_size("dp")
     if count > 8:
         return lax.all_gather(shard, "dp", axis=0, tiled=False)
+    return place_pieces(gather_pieces(shard))
+
+
+def gather_pieces(shard):
+    count = lax.axis_size("dp")
     pieces = [None] * count
     pieces[0] = shard
     for flip in range(2, count, 2):
         pieces[flip] = exchange(shard, "dp", flip)
     for flip in range(0, count, 2):
         pieces[flip + 1] = exchange(pieces[flip], "dp", 1)
-    return place_pieces(pieces)
+    return pieces
 
 
 def scatter_data(blocks):
@@ -131,6 +157,262 @@
         value = value + exchange(value, "dp", flip)
         flip *= 2
     return value
+
+
+MESH = pl.DeviceIdType.MESH
+BF = jnp.bfloat16
+VMEM_LIMIT = 66_000_000
+NN = ((1,), (0,))
+NT = ((1,), (1,))
+TN = ((0,), (0,))
+
+
+def split(x):
+    hi = x.astype(BF)
+    return hi, (x - hi.astype(jnp.float32)).astype(BF)
+
+
+def bdot(a, b, contract):
+    return lax.dot_general(a, b, (contract, ((), ())), preferred_element_type=jnp.float32)
+
+
+def dot3(a, b, contract):
+    return bdot(a[0], b[0], contract) + (bdot(a[0], b[1], contract) + bdot(a[1], b[0], contract))
+
+
+def take(pair, where):
+    return pair[0][where], pair[1][where]
+
+
+def rows_at(start, count):
+    return (pl.ds(start if isinstance(start, int) else pl.multiple_of(start, 8), count), slice(None))
+
+
+def put(pair, where, value):
+    hi, lo = split(value)
+    pair[0][where] = hi
+    pair[1][where] = lo
+
+
+def erf(x):
+    x = jnp.clip(x, -3.832506856900711, 3.832506856900711)
+    s = x * x
+    num = s * 0.00022905065861350646 + 0.0034082910107109506
+    num = num * s + 0.050955695062380861
+    num = num * s + 0.18520832239976145
+    num = num * s + 1.128379143519084
+    den = s * -1.1791602954361697e-7 + 0.000023547966471313185
+    den = den * s + 0.0010179625278914885
+    den = den * s + 0.014070470171167667
+    den = den * s + 0.11098505178285362
+    den = den * s + 0.49746925110067538
+    den = den * s + 1.0
+    return x * num / den
+
+
+def k_gelu(v):
+    return 0.5 * v * (1.0 + erf(v * RSQRT2))
+
+
+def k_slope(v):
+    return 0.5 * (1.0 + erf(v * RSQRT2)) + v * (RSQRT2PI * jnp.exp(-0.5 * v * v))
+
+
+class Links:
+    def __init__(self, half, tm, bufs, sems):
+        self.half, self.tm, self.n = half, tm, half // tm
+        self.send_a, self.recv_a, self.send_b, self.recv_b, self.send_c, self.recv_c = bufs
+        self.sems = sems
+        place = lax.axis_index("mp")
+        self.near = place + 1 - 2 * (place % 2)
+        self.far = (place + 2) % 4
+
+    def greet(self):
+        barrier = pltpu.get_barrier_semaphore()
+        for peer in (self.near, self.far):
+            pl.semaphore_signal(barrier, inc=1, device_id={"mp": peer}, device_id_type=MESH)
+        pl.semaphore_wait(barrier, 2)
+
+    def copy(self, kind, i):
+        src, dst, peer = (
+            (self.send_a, self.recv_a, self.near),
+            (self.send_b, self.recv_b, self.far),
+            (self.send_c, self.recv_c, self.near),
+        )[kind]
+        part = pl.ds(i * self.tm, self.tm)
+        return pltpu.make_async_remote_copy(
+            src_ref=src.at[part],
+            dst_ref=dst.at[part],
+            send_sem=self.sems.at[2 * kind, i],
+            recv_sem=self.sems.at[2 * kind + 1, i],
+            device_id={"mp": peer},
+            device_id_type=MESH,
+        )
+
+    def begin(self, part_of):
+        for i in range(self.n):
+            at = rows_at(i * self.tm, self.tm)
+            self.send_a[at] = part_of(self.half + i * self.tm)
+            self.copy(0, i).start()
+            mine = part_of(i * self.tm)
+            self.copy(0, i).wait_recv()
+            self.send_b[at] = mine + self.recv_a[at]
+            self.copy(1, i).start()
+
+    def finish(self, done):
+        for i in range(self.n):
+            at = rows_at(i * self.tm, self.tm)
+            self.copy(1, i).wait_recv()
+            total = self.send_b[at] + self.recv_b[at]
+            self.send_c[at] = total
+            self.copy(2, i).start()
+            done(i * self.tm, total, True)
+        for i in range(self.n):
+            self.copy(2, i).wait_recv()
+            done(self.half + i * self.tm, self.recv_c[rows_at(i * self.tm, self.tm)], False)
+        for kind in range(3):
+            for i in range(self.n):
+                self.copy(kind, i).wait_send()
+
+
+def link_scratch(half, tm, width):
+    return [pltpu.VMEM((half, width), jnp.float32)] * 6 + [pltpu.SemaphoreType.DMA((6, half // tm))]
+
+
+def call(kernel, outs, ins, scratch, name, collective=None, flops=0):
+    nbytes = sum(math.prod(x.shape) * x.dtype.itemsize for x in list(ins) + list(outs))
+    return pl.pallas_call(
+        kernel,
+        out_shape=[jax.ShapeDtypeStruct(o.shape, o.dtype) for o in outs],
+        in_specs=[pl.BlockSpec(memory_space=pltpu.VMEM)] * len(ins),
+        out_specs=[pl.BlockSpec(memory_space=pltpu.VMEM)] * len(outs),
+        scratch_shapes=scratch,
+        compiler_params=pltpu.CompilerParams(
+            vmem_limit_bytes=VMEM_LIMIT,
+            collective_id=collective,
+            has_side_effects=collective is not None,
+        ),
+        cost_estimate=pl.CostEstimate(flops=flops, bytes_accessed=nbytes, transcendentals=0),
+        name=name,
+    )(*ins)
+
+
+def shape(*dims, dtype=jnp.float32):
+    return jax.ShapeDtypeStruct(dims, dtype)
+
+
+def row_stats(x):
+    mean = jnp.mean(x, axis=-1, keepdims=True)
+    centre = x - mean
+    scale = lax.rsqrt(jnp.mean(centre * centre, axis=-1, keepdims=True) + EPS)
+    return centre * scale, scale
+
+
+def chunk_of(half):
+    return 128 if half % 128 == 0 else half
+
+
+def mlp_forward(x, norm, up, down, weight, collective, name):
+    rows, width = x.shape
+    ff = up[0].shape[1]
+    half = rows // 2
+    tm = chunk_of(half)
+
+    def kernel(x_ref, norm_ref, uh, ul, dh, dl, w_ref, out, pre_out, stat, *rest):
+        links = Links(half, tm, rest[:6], rest[6])
+        links.greet()
+        gain, bias = norm_ref[0:1, :], norm_ref[1:2, :]
+
+        def part_of(start):
+            at = rows_at(start, tm)
+            hat, _ = row_stats(x_ref[at])
+            pre = dot3(split(hat * gain + bias), (uh[...], ul[...]), NN)
+            pre_out[at] = pre
+            return dot3(split(k_gelu(pre)), (dh[...], dl[...]), NT)
+
+        links.begin(part_of)
+        stat[...] = jnp.zeros_like(stat)
+
+        def done(start, total, mine):
+            at = rows_at(start, tm)
+            value = x_ref[at] + total
+            out[at] = value
+            if mine:
+                w = w_ref[at]
+                stat[0:1, :] += jnp.sum(total * total * w, axis=0, keepdims=True)
+                stat[1:2, :] += jnp.sum(value * value * w, axis=0, keepdims=True)
+
+        links.finish(done)
+
+    return call(
+        kernel,
+        [shape(rows, width), shape(rows, ff), shape(8, width)],
+        [x, norm, *up, *down, weight],
+        link_scratch(half, tm, width),
+        name,
+        collective,
+        flops=12 * rows * width * ff,
+    )
+
+
+def mlp_backward(grad, x, norm, pre, up, down, collective, name):
+    rows, width = x.shape
+    ff = up[0].shape[1]
+    half = rows // 2
+    tm = chunk_of(half)
+
+    def kernel(g_ref, x_ref, norm_ref, pre_ref, uh, ul, dh, dl, out, dup, ddown, dnorm, lh, ll, ph, plo, hh, hl, gh, gl, *rest):
+        links = Links(half, tm, rest[:6], rest[6])
+        links.greet()
+        gain, bias = norm_ref[0:1, :], norm_ref[1:2, :]
+
+        def part_of(start):
+            at = rows_at(start, tm)
+            grad_rows = split(g_ref[at])
+            gh[at], gl[at] = grad_rows
+            pre_rows = pre_ref[at]
+            cdf = 0.5 * (1.0 + erf(pre_rows * RSQRT2))
+            put((hh, hl), at, pre_rows * cdf)
+            slope = cdf + pre_rows * (RSQRT2PI * jnp.exp(-0.5 * pre_rows * pre_rows))
+            grad_pre = split(dot3(grad_rows, (dh[...], dl[...]), NN) * slope)
+            ph[at], plo[at] = grad_pre
+            return dot3(grad_pre, (uh[...], ul[...]), NT)
+
+        links.begin(part_of)
+
+        for start in range(0, rows, tm):
+            at = rows_at(start, tm)
+            hat, _ = row_stats(x_ref[at])
+            put((lh, ll), at, hat * gain + bias)
+        step = 256 if width % 256 == 0 else width
+        for c in range(0, width, step):
+            cols = (slice(None), pl.ds(c, step))
+            ddown[pl.ds(c, step), :] = dot3(take((gh, gl), cols), (hh[...], hl[...]), TN)
+            dup[pl.ds(c, step), :] = dot3(take((lh, ll), cols), (ph[...], plo[...]), TN)
+        dnorm[...] = jnp.zeros_like(dnorm)
+
+        def done(start, total, mine):
+            at = rows_at(start, tm)
+            hat, scale = row_stats(x_ref[at])
+            if mine:
+                dnorm[0:1, :] += jnp.sum(total * hat, axis=0, keepdims=True)
+                dnorm[1:2, :] += jnp.sum(total, axis=0, keepdims=True)
+            out[at] = g_ref[at] + norm_back(total, hat, scale, gain)
+
+        links.finish(done)
+
+    return call(
+        kernel,
+        [shape(rows, width), shape(width, ff), shape(width, ff), shape(8, width)],
+        [grad, x, norm, pre, *up, *down],
+        [pltpu.VMEM((rows, width), BF)] * 2
+        + [pltpu.VMEM((rows, ff), BF)] * 4
+        + [pltpu.VMEM((rows, width), BF)] * 2
+        + link_scratch(half, tm, width),
+        name,
+        collective,
+        flops=24 * rows * width * ff,
+    )
 
 
 def split_heads(rows):
@@ -237,13 +519,14 @@
         )
     )
     stem_all = gather_data(conv_rows)
-    enc_attn_all = gather_data(attn_pack(enc_qkv, enc_out)).reshape(width, -1)
+    enc_attn_all = gather_slow(attn_pack(enc_qkv, enc_out)).reshape(width, -1)
     dec_attn_all = gather_data(attn_pack(dec_qkv, dec_out)).reshape(width, -1)
-    enc_mlp_all = gather_data(jnp.concatenate([enc_up, enc_down.T], axis=0))
+    part = width // n_dp
+    ff = enc_up.shape[1]
+    mlp_cuts = [(0, part, 0, ff), (part, 2 * part, 0, ff)]
+    enc_up_all, enc_down_all = split_rows(gather_slow(jnp.concatenate([enc_up, enc_down.T], axis=0)), mlp_cuts)
     cross_all = gather_data(attn_pack(cross_qkv, cross_out)).reshape(width, -1)
-    dec_mlp_all = gather_data(jnp.concatenate([dec_up, dec_down.T], axis=0))
-
-    part = width // n_dp
+
     two_rows = taps * chans
     one_size = taps * mel * chans
     one_rows = -(-one_size // width)
@@ -269,11 +552,6 @@
     w_both = jnp.concatenate(
         [jnp.pad(w_one, ((0, 0), (0, mel))), jnp.pad(w_one, ((0, 0), (mel, 0)))], axis=0
     )
-    ff = enc_up.shape[1]
-    enc_up_all = enc_mlp_all[:, :part].reshape(width, ff)
-    enc_down_all = enc_mlp_all[:, part:].reshape(width, ff)
-    dec_up_all = dec_mlp_all[:, :part].reshape(width, ff)
-    dec_down_all = dec_mlp_all[:, part:].reshape(width, ff)
 
     frame_row = lax.dynamic_index_in_dim(frame_mask, dp_place, 0, keepdims=False) > 0
     token_row = lax.dynamic_index_in_dim(token_mask, dp_place, 0, keepdims=False) > 0
@@ -293,7 +571,10 @@
     stem_one = gelu(pre_one)
     odd = stem_one[:, stem_width:]
     stem_cat = jnp.concatenate([jnp.where(first, 0.0, jnp.roll(odd, 1, axis=0)), stem_one], axis=1)
-    stem_sum = model_sum(mm(stem_cat, w_two))
+    stem_part = mm(stem_cat, w_two)
+    stem_sum = model_sum(stem_part)
+    dec_mlp_shard = tie(jnp.concatenate([dec_up, dec_down.T], axis=0), stem_part)
+    dec_up_all, dec_down_all = split_rows(gather_slow(dec_mlp_shard), mlp_cuts)
     stream_zero = gelu(stem_sum) + sinusoid(frames)
 
     hat_zero, scale_zero = normalize(stream_zero)
@@ -303,12 +584,11 @@
     enc_mixed, enc_lse = attend(enc_q, enc_k, enc_v, frame_allowed)
     enc_attn = model_sum(mm_nt(enc_mixed, enc_attn_all[:, 3 * local :]))
     stream_one = stream_zero + enc_attn
-    hat_one, scale_one = normalize(stream_one)
-    ln_one = hat_one * norms[1, 0] + norms[1, 1]
-    enc_pre = mm(ln_one, enc_up_all)
-    enc_hidden = gelu(enc_pre)
-    enc_mlp = model_sum(mm_nt(enc_hidden, enc_down_all))
-    stream_two = stream_one + enc_mlp
+    frame_col = frame_ok.astype(jnp.float32)[:, None]
+    token_col = token_ok.astype(jnp.float32)[:, None]
+    stream_two, enc_pre, enc_stat = mlp_forward(
+        stream_one, norms[1], enc_up_all, enc_down_all, frame_col, 1, "enc_mlp_forward"
+    )
     hat_two, scale_two = normalize(stream_two)
     memory = hat_two * norms[2, 0] + norms[2, 1]
     cross_two = mm(memory, cross_all[:, local : 3 * local])
@@ -319,6 +599,7 @@
     owned = (local_ids >= 0) & (local_ids < vocab_rows)
     safe_ids = jnp.clip(local_ids, 0, vocab_rows - 1)
     picked = jnp.where(owned[:, None], jnp.take(embedding, safe_ids, axis=0), 0.0)
+    picked = tie(picked, stem_sum)
     share = lax.psum_scatter(picked, "dp", scatter_dimension=0, tiled=True)
     text_zero = turn(lax.all_gather(share, "mp", axis=1, tiled=True)) + sinusoid(tokens)
 
@@ -335,12 +616,9 @@
     cross_mixed, cross_lse = attend(cross_q, cross_k, cross_v, frame_allowed)
     cross_attn = model_sum(mm_nt(cross_mixed, cross_all[:, 3 * local :]))
     text_two = text_one + cross_attn
-    hat_five, scale_five = normalize(text_two)
-    ln_five = hat_five * norms[5, 0] + norms[5, 1]
-    dec_pre = mm(ln_five, dec_up_all)
-    dec_hidden = gelu(dec_pre)
-    dec_mlp = model_sum(mm_nt(dec_hidden, dec_down_all))
-    decoded = text_two + dec_mlp
+    decoded, dec_pre, dec_stat = mlp_forward(
+        text_two, norms[5], dec_up_all, dec_down_all, token_col, 2, "dec_mlp_forward"
+    )
 
     def half_of(rows):
         return rows[: rows.shape[0] // 2]
@@ -353,8 +631,10 @@
         return jnp.sum(kept * kept * weight)
 
     local_sums = jnp.stack(
-        [squares(x, frame_weight) for x in (stream_zero, enc_attn, enc_mlp, stream_two)]
-        + [squares(x, token_weight) for x in (text_zero, dec_attn, cross_attn, dec_mlp, decoded)]
+        [squares(x, frame_weight) for x in (stream_zero, enc_attn)]
+        + [jnp.sum(enc_stat[0]), jnp.sum(enc_stat[1])]
+        + [squares(x, token_weight) for x in (text_zero, dec_attn, cross_attn)]
+        + [jnp.sum(dec_stat[0]), jnp.sum(dec_stat[1])]
     )
     local_sums = local_sums + exchange(local_sums, "mp", 1)
     square_sums = data_sum(local_sums)
@@ -370,12 +650,12 @@
     def block(grad):
         return grad.reshape(n_dp, grad.shape[0] // n_dp, grad.shape[1])
 
-    grad_dec_down = scatter_data(block(mm_tn(cot, dec_hidden)))
-    grad_pre = mm(cot, dec_down_all) * gelu_slope(dec_pre)
-    grad_dec_up = scatter_data(block(mm_tn(ln_five, grad_pre)))
-    grad_ln = model_sum(mm_nt(grad_pre, dec_up_all))
-    norm_five = norm_grads(grad_ln, hat_five)
-    grad_text_two = cot + norm_back(grad_ln, hat_five, scale_five, norms[5, 0])
+    grad_text_two, grad_up, grad_down, norm_five = mlp_backward(
+        cot, text_two, norms[5], dec_pre, dec_up_all, dec_down_all, 3, "dec_mlp_backward"
+    )
+    grad_dec_up = scatter_slow(block(grad_up))
+    grad_dec_down = scatter_slow(block(grad_down))
+    norm_five = norm_five[:2]
 
     grad_cross_out = mm_tn(grad_text_two, cross_mixed)
     grad_cq, grad_ck, grad_cv = attend_back(
@@ -388,7 +668,7 @@
         mm(grad_text_two, cross_all[:, 3 * local :]),
     )
     grad_ckv = jnp.concatenate([grad_ck, grad_cv], axis=1)
-    grad_cross = scatter_data(
+    grad_cross = scatter_slow(
         block(
             jnp.concatenate([mm_tn(ln_four, grad_cq), mm_tn(memory, grad_ckv), grad_cross_out], axis=1)
         )
@@ -411,7 +691,7 @@
         ),
         axis=1,
     )
-    grad_dec_attn = scatter_data(
+    grad_dec_attn = scatter_slow(
         block(jnp.concatenate([mm_tn(ln_three, grad_three), grad_dec_out], axis=1))
     )
     grad_ln = model_sum(mm_nt(grad_three, dec_attn_all[:, : 3 * local]))
@@ -427,12 +707,12 @@
 
     norm_two = norm_grads(grad_memory, hat_two)
     grad_stream_two = norm_back(grad_memory, hat_two, scale_two, norms[2, 0])
-    grad_enc_down = scatter_data(block(mm_tn(grad_stream_two, enc_hidden)))
-    grad_pre = mm(grad_stream_two, enc_down_all) * gelu_slope(enc_pre)
-    grad_enc_up = scatter_data(block(mm_tn(ln_one, grad_pre)))
-    grad_ln = model_sum(mm_nt(grad_pre, enc_up_all))
-    norm_one = norm_grads(grad_ln, hat_one)
-    grad_stream_one = grad_stream_two + norm_back(grad_ln, hat_one, scale_one, norms[1, 0])
+    grad_stream_one, grad_up, grad_down, norm_one = mlp_backward(
+        grad_stream_two, stream_one, norms[1], enc_pre, enc_up_all, enc_down_all, 4, "enc_mlp_backward"
+    )
+    grad_enc_up = scatter_data(block(grad_up))
+    grad_enc_down = scatter_data(block(grad_down))
+    norm_one = norm_one[:2]
 
     grad_enc_out = mm_tn(grad_stream_one, enc_mixed)
     grad_three = jnp.concatenate(

time: 1120 us -> 1030 us (0.920)
  waiting for transfers between devices: 465 us -> 292 us
  Pallas kernels: 22.2 us -> 170 us
  matrix products: 173 us -> 138 us
  other arithmetic: 184 us -> 172 us
    ppermute x118 -> x69, waiting for transfers between devices: 465 us -> 260 us  [exchange(): return lax.ppermute(value, axis, [(i, i ^ flip) for i in range(size)])]
    pallas_call x0 -> x4, Pallas kernels: none -> 161 us  [call(): pl.pallas_call(kernel, out_shape=[jax.ShapeDtypeStruct(o.shape, o.dtype)...]
    dot_general x39 -> x27, matrix products: 106 us -> 72 us  [dot(): lax.dot_general(left, right, (contract, ((), ())), precision=HIGH, prefer...]
    reduce_scatter x1, waiting for transfers between devices: 0.01 us -> 31.5 us  [body(): share = lax.psum_scatter(picked, 'dp', scatter_dimension=0, tiled=True)]
    pallas_call x6 -> x3, Pallas kernels: 22.2 us -> 9.42 us  [place_pieces(): pl.pallas_call(kernel, out_shape=jax.ShapeDtypeStruct((count, rows, width...]
    ppermute x118 -> x69, starting transfers between devices: 110 us -> 101 us  [exchange(): return lax.ppermute(value, axis, [(i, i ^ flip) for i in range(size)])]
    unnamed x480 -> x413, local copies, waits for them, and re-layouts: 51.1 us -> 50.7 us
  transfers between devices with their start and end apart: 121 -> 79, of which waited for: 43 -> 30; matrix products, arithmetic and copies ran while one was open for 34% -> 35% of each run, Pallas kernels for 2% -> 11%
where the time goes in v2:
time: 1030 us; the launch traced here: 1020 us
  waiting for transfers between devices  292 us (28%)
  other arithmetic  172 us (17%)
  Pallas kernels  170 us (17%)
  matrix products  138 us (13%)
  local copies, waits for them, and re-layouts  129 us (13%)
  starting transfers between devices  102 us (10%)
  between operations  17.7 us (2%)
    ppermute x69, waiting for transfers between devices, exchange(): return lax.ppermute(value, axis, [(i, i ^ flip) for i in range(size)])  260 us
    pallas_call x4, Pallas kernels, call(): pl.pallas_call(kernel, out_shape=[jax.ShapeDtypeStruct(o.shape, o.dtype)...  161 us
    ppermute x69, starting transfers between devices, exchange(): return lax.ppermute(value, axis, [(i, i ^ flip) for i in range(size)])  101 us
    dot_general x27, matrix products, dot(): lax.dot_general(left, right, (contract, ((), ())), precision=HIGH, prefer...  72 us
    unnamed x413, local copies, waits for them, and re-layouts  50.7 us
    reduce_scatter x1, waiting for transfers between devices, body(): share = lax.psum_scatter(picked, 'dp', scatter_dimension=0, tiled=True)  31.5 us
    scatter-add x1, other arithmetic, body(): grad_embedding = jnp.zeros(embedding.shape, jnp.float32).at[safe_ids].add...  25 us
  transfers between devices with their start and end apart: 79, of which 30 were waited for; matrix products, arithmetic and copies ran while one was open for 35% of the time, Pallas kernels for 11%

profile of v2, /device:TPU:0, one launch (start us, length us, event | category | flops | bytes accessed | tf_op | source)
XLA Modules:
  0.0 1021.2 jit_solution(1324995953678218360)
XLA Ops:
  10.0 6.5 copy.148
  16.6 12.7 %gather_fusion = f32[3072,192]{1,0:T(8,128)S(1)} fusion(f32[6480,192]{1,0:T(8,128)} %copy.148, s32[3072]{0:T(1024)S(1)} %broadcast_clamp_fusion), kind=kCustom, calls=%fused_computation | custom fusion | bytes 4730880 | tf_op jit(solution)/shard_map/jit(_take)/gather | solution.py:601
  45.4 11.3 %collective-permute-done.1.refs_2_ = f32[88,768]{1,0:T(8,128)} collective-permute-done((f32[88,768]{1,0:T(8,128)}, f32[88,768]{1,0:T(8,128)}, u32[]{:S(2)}, u32[]{:S(2)}) %collective-permute-start.1) | collective-permute-done | bytes 270368 | tf_op jit(solution)/shard_map/ppermute | solution.py:62
  58.5 10.8 %collective-permute-done.3.refs_4_ = f32[88,768]{1,0:T(8,128)} collective-permute-done((f32[88,768]{1,0:T(8,128)}, f32[88,768]{1,0:T(8,128)}, u32[]{:S(2)}, u32[]{:S(2)}) %collective-permute-start.3) | collective-permute-done | bytes 270368 | tf_op jit(solution)/shard_map/ppermute | solution.py:62
  71.6 6.8 collective-permute-done.4.refs_5_
  99.5 31.5 %reduce-scatter.6.cloned.1.call-done = f32[384,192]{1,0:T(8,128)} async-done(((f32[3072,192]{1,0:T(8,128)}), f32[384,192]{1,0:T(8,128)}) %reduce-scatter.6.cloned.1.call-update) | async-done | bytes 294928 | tf_op jit(solution)/shard_map/reduce_scatter | solution.py:603
  153.2 18.3 %collective-permute-done.8 = f32[512,768]{1,0:T(8,128)S(1)} collective-permute-done((f32[512,768]{1,0:T(8,128)}, f32[512,768]{1,0:T(8,128)S(1)}, u32[]{:S(2)}, u32[]{:S(2)}) %collective-permute-start.8) | collective-permute-done | bytes 1572896 | tf_op jit(solution)/shard_map/ppermute | solution.py:62
  178.6 6.9 multiply_sine_fusion
  191.3 6.2 collective-permute-done.12.refs_3_
  232.5 11.9 %fusion.2 = f32[3,1024]{1,0:T(4,128)S(1)} fusion(f32[3,1024,1024]{1,2,0:T(8,128)S(1)} %get-tuple-element.266, f32[3,1024]{1,0:T(4,128)S(1)} %get-tuple-element.265, pred[1024]{0:T(1024)(128)(4,1)S(1)} %add_select_fusion.1), kind=kLoop, calls=%fused_computation.8 | loop fusion | flops 12579840 | bytes 12608512 | tf_op jit(solution)/shard_map/reduce_sum | solution.py:429
  287.2 8.0 collective-permute-done.23.refs_1_
  298.5 8.9 collective-permute-done.25.refs_3_
  307.4 6.3 collective-permute-done.27.refs_5_
  345.3 50.3 %enc_mlp_forward.1 = (f32[1024,768]{1,0:T(8,128)}, f32[1024,768]{1,0:T(8,128)}, f32[8,768]{1,0:T(8,128)}) custom-call(f32[1024,768]{1,0:T(8,128)} %maximum_add_fusion.1.x_ref, f32[2,768]{1,0:T(2,128)} %squeeze.125.norm_ref, bf16[768,768]{1,0:T(8,128)(2,1)} %get-tuple-element.183.uh, bf16[768,768]{1,0:T(8,128)(2,1)} %get-tuple-element.182.ul, ...), custom_call_target="tpu_custom_call" | custom-call | flops 7247757312 | bytes 14190592 | tf_op jit(solution)/shard_map/enc_mlp_forward/pallas_call | solution.py:284
  420.6 10.8 %collective-permute-done.31 = f32[192,768]{1,0:T(8,128)S(1)} collective-permute-done((f32[192,768]{1,0:T(8,128)S(1)}, f32[192,768]{1,0:T(8,128)S(1)}, u32[]{:S(2)}, u32[]{:S(2)}) %collective-permute-start.31) | collective-permute-done | bytes 589856 | tf_op jit(solution)/shard_map/ppermute | solution.py:62
  438.1 28.5 %dec_mlp_forward.1 = (f32[384,768]{1,0:T(8,128)}, f32[384,768]{1,0:T(8,128)}, f32[8,768]{1,0:T(8,128)}) custom-call(f32[384,768]{1,0:T(8,128)} %maximum_add_fusion.3.x_ref, f32[2,768]{1,0:T(2,128)} %squeeze.129.norm_ref, bf16[768,768]{1,0:T(8,128)(2,1)} %get-tuple-element.179.uh, bf16[768,768]{1,0:T(8,128)(2,1)} %get-tuple-element.178.ul, ...), custom_call_target="tpu_custom_call" | custom-call | flops 2717908992 | bytes 8289792 | tf_op jit(solution)/shard_map/dec_mlp_forward/pallas_call | solution.py:284
  466.6 29.7 %dec_mlp_backward.1 = (f32[384,768]{1,0:T(8,128)}, f32[768,768]{1,0:T(8,128)}, f32[768,768]{1,0:T(8,128)}, f32[8,768]{1,0:T(8,128)}) custom-call(f32[384,768]{1,0:T(8,128)} %maximum_select_fusion.2.g_ref, f32[384,768]{1,0:T(8,128)} %maximum_add_fusion.3.x_ref, f32[2,768]{1,0:T(2,128)} %squeeze.129.norm_ref, f32[384,768]{1,0:T(8,128)} %get-tuple-element.37.pre_ref, ...), custom_call_target="tpu_custom_call" | custom-call | flops 5435817984 | bytes 14186496 | tf_op jit(solution)/shard_map/dec_mlp_backward/pallas_call | solution.py:284
  525.4 9.8 collective-permute-done.43
  561.4 14.1 %collective-permute-done.46 = f32[192,768]{1,0:T(8,128)S(1)} collective-permute-done((f32[192,768]{1,0:T(8,128)S(1)}, f32[192,768]{1,0:T(8,128)S(1)}, u32[]{:S(2)}, u32[]{:S(2)}) %collective-permute-start.46) | collective-permute-done | bytes 589856 | tf_op jit(solution)/shard_map/ppermute | solution.py:62
  594.5 35.6 %collective-permute-done.34 = f32[512,768]{1,0:T(8,128)S(1)} collective-permute-done((f32[512,768]{1,0:T(8,128)S(1)}, f32[512,768]{1,0:T(8,128)S(1)}, u32[]{:S(2)}, u32[]{:S(2)}) %collective-permute-start.34) | collective-permute-done | bytes 1572896 | tf_op jit(solution)/shard_map/ppermute | solution.py:62
  642.9 52.2 %enc_mlp_backward.1 = (f32[1024,768]{1,0:T(8,128)}, f32[768,768]{1,0:T(8,128)}, f32[768,768]{1,0:T(8,128)}, f32[8,768]{1,0:T(8,128)}) custom-call(f32[1024,768]{1,0:T(8,128)} %subtract_multiply_fusion.g_ref, f32[1024,768]{1,0:T(8,128)} %maximum_add_fusion.1.x_ref, f32[2,768]{1,0:T(2,128)} %squeeze.125.norm_ref, f32[1024,768]{1,0:T(8,128)} %get-tuple-element.39.pre_ref, ...), custom_call_target="tpu_custom_call" | custom-call | flops 14495514624 | bytes 22050816 | tf_op jit(solution)/shard_map/enc_mlp_backward/pallas_call | solution.py:284
  700.6 11.1 %multiply_multiply_fusion = f32[3,1024,1024]{1,2,0:T(8,128)S(1)} fusion(f32[3,1024,1024]{1,2,0:T(8,128)} %copy-done, f32[3,1024]{1,0:T(4,128)S(1)} %bitcast.425, f32[3,1024]{1,0:T(4,128)S(1)} %log_add_fusion, pred[1024]{0:T(1024)(128)(4,1)S(1)} %copy-done.142, f32[1024,3,64]{0,2,1:T(8,128)S(1)} %bitcast.360, f32[1024,3,64]{0,2,1:T(8,128)S(1)} %bitcast.376), kind=kOutput, calls=%fused_computation.2 | convolution fusion | flops 1226833920 | bytes 26764288 | tf_op jit(solution)/shard_map/qhe,khe->hqk/dot_general | solution.py:441
  715.9 6.7 fusion.205
  722.7 7.6 fusion.3
  730.3 6.4 fusion.44
  773.2 42.1 %collective-permute-done.66 = f32[9]{0:T(128)S(1)} collective-permute-done((f32[9]{0:T(128)S(1)}, f32[9]{0:T(128)S(1)}, u32[]{:S(2)}, u32[]{:S(2)}) %collective-permute-start.66) | collective-permute-done | bytes 68 | tf_op jit(solution)/shard_map/ppermute | solution.py:62
  843.5 22.2 %collective-permute-done.57 = f32[4,96,768]{2,1,0:T(8,128)S(1)} collective-permute-done((f32[4,96,768]{2,1,0:T(8,128)S(1)}, f32[4,96,768]{2,1,0:T(8,128)S(1)}, u32[]{:S(2)}, u32[]{:S(2)}) %collective-permute-start.57) | collective-permute-done | bytes 1179680 | tf_op jit(solution)/shard_map/ppermute | solution.py:62
  908.8 26.3 %collective-permute-start.58 = (f32[96,768]{1,0:T(8,128)}, f32[96,768]{1,0:T(8,128)S(1)}, u32[]{:S(2)}, u32[]{:S(2)}) collective-permute-start(f32[96,768]{1,0:T(8,128)} %get-tuple-element.196), channel_id=1, source_target_pairs={{0,8},{4,12},{8,0},{12,4},{16,24},{20,28},{24,16},{28,20},{1,9},{5... | collective-permute-start | bytes 884744 | tf_op jit(solution)/shard_map/ppermute | solution.py:62
  949.3 9.5 collective-permute-done.60
  963.6 6.2 collective-permute-start.50
  976.1 25.0 %scatter_custom_fusion = f32[6480,192]{1,0:T(8,128)} fusion(s32[3072]{0:T(1024)} %bitcast.440, f32[]{:T(128)} %constant.190.clone.1, f32[3072,192]{1,0:T(8,128)} %all-gather.11.cloned.1.call-done, pred[3072]{0:T(1024)(128)(4,1)S(1)} %copy-done.169), kind=kCustom, calls=%fused_computation.36 | custom fusion | flops 1179648 | bytes 8126464 | tf_op jit(solution)/shard_map/scatter-add | solution.py:705
  1001.1 6.3 copy.189
  (860 shorter events, 456.8 us)
Async XLA Ops:
  7.2 123.7 %reduce-scatter.6.cloned.1.call-start = ((), (), s32[]{:S(2)}) async-start(), calls=%async_computation.5 | async-start | bytes 3538944 | tf_op jit(solution)/shard_map/reduce_scatter | solution.py:603
  32.8 187.8 %all-gather.13.cloned.1.call-start = ((), (), s32[]{:S(2)}) async-start(), calls=%async_computation.12 | async-start | bytes 2654208 | tf_op jit(solution)/shard_map/all_gather | solution.py:96
  34.6 223.1 %all-gather.9.cloned.1.call-start = ((), (), s32[]{:S(2)}) async-start(), calls=%async_computation.6 | async-start | bytes 1474560 | tf_op jit(solution)/shard_map/all_gather | solution.py:604
  132.8 194.7 %all-gather.15.cloned.1.call-start = ((), (), s32[]{:S(2)}) async-start(), calls=%async_computation.13 | async-start | bytes 5308416 | tf_op jit(solution)/shard_map/all_gather | solution.py:96
  139.2 46.3 %collective-permute-start.11 = (f32[96,768]{1,0:T(8,128)}, f32[96,768]{1,0:T(8,128)}, u32[]{:S(2)}, u32[]{:S(2)}) collective-permute-start(f32[96,768]{1,0:T(8,128)} %pad_maximum_fusion.21.refs_0_), channel_id=1, source_target_pairs={{0,8},{4,12},{8,0},{12,4},{16,24},{20,28},{24,16},{28,20},{1,9},{5... | collective-permute-start | bytes 884744 | tf_op jit(solution)/shard_map/ppermute | solution.py:62
  140.3 46.7 %collective-permute-start.13 = (f32[96,768]{1,0:T(8,128)}, f32[96,768]{1,0:T(8,128)}, u32[]{:S(2)}, u32[]{:S(2)}) collective-permute-start(f32[96,768]{1,0:T(8,128)} %pad_maximum_fusion.21.refs_0_), channel_id=1, source_target_pairs={{0,16},{4,20},{8,24},{12,28},{16,0},{20,4},{24,8},{28,12},{1,17},{... | collective-permute-start | bytes 884744 | tf_op jit(solution)/shard_map/ppermute | solution.py:62
  141.5 46.1 %collective-permute-start.15 = (f32[96,768]{1,0:T(8,128)}, f32[96,768]{1,0:T(8,128)}, u32[]{:S(2)}, u32[]{:S(2)}) collective-permute-start(f32[96,768]{1,0:T(8,128)} %pad_maximum_fusion.21.refs_0_), channel_id=1, source_target_pairs={{0,24},{4,28},{8,16},{12,20},{16,8},{20,12},{24,0},{28,4},{1,25},{... | collective-permute-start | bytes 884744 | tf_op jit(solution)/shard_map/ppermute | solution.py:62
  143.6 46.4 %collective-permute-start.10 = (f32[96,768]{1,0:T(8,128)}, f32[96,768]{1,0:T(8,128)}, u32[]{:S(2)}, u32[]{:S(2)}) collective-permute-start(f32[96,768]{1,0:T(8,128)} %pad_maximum_fusion.21.refs_0_), channel_id=1, source_target_pairs={{0,4},{4,0},{8,12},{12,8},{16,20},{20,16},{24,28},{28,24},{1,5},{5... | collective-permute-start | bytes 884744 | tf_op jit(solution)/shard_map/ppermute | solution.py:62
  147.0 270.7 %all-gather.17.cloned.1.call-start = ((), (), s32[]{:S(2)}) async-start(), calls=%async_computation.14 | async-start | bytes 5308416 | tf_op jit(solution)/shard_map/all_gather | solution.py:96
  173.1 40.0 %collective-permute-start.9 = (f32[512,768]{1,0:T(8,128)S(1)}, f32[512,768]{1,0:T(8,128)S(1)}, u32[]{:S(2)}, u32[]{:S(2)}) collective-permute-start(f32[512,768]{1,0:T(8,128)S(1)} %add.431), channel_id=1, source_target_pairs={{0,1},{1,0},{2,3},{3,2},{4,5},{5,4},{6,7},{7,6},{8,9},{9,8},{10,11... | collective-permute-start | bytes 4718600 | tf_op jit(solution)/shard_map/ppermute | solution.py:62
  190.0 90.3 %collective-permute-start.24 = (f32[96,768]{1,0:T(8,128)}, f32[96,768]{1,0:T(8,128)}, u32[]{:S(2)}, u32[]{:S(2)}) collective-permute-start(f32[96,768]{1,0:T(8,128)} %pad_maximum_fusion.23.refs_0_), channel_id=1, source_target_pairs={{0,8},{4,12},{8,0},{12,4},{16,24},{20,28},{24,16},{28,20},{1,9},{5... | collective-permute-start | bytes 884744 | tf_op jit(solution)/shard_map/ppermute | solution.py:62
  197.5 87.7 %collective-permute-start.26 = (f32[96,768]{1,0:T(8,128)}, f32[96,768]{1,0:T(8,128)}, u32[]{:S(2)}, u32[]{:S(2)}) collective-permute-start(f32[96,768]{1,0:T(8,128)} %pad_maximum_fusion.23.refs_0_), channel_id=1, source_target_pairs={{0,16},{4,20},{8,24},{12,28},{16,0},{20,4},{24,8},{28,12},{1,17},{... | collective-permute-start | bytes 884744 | tf_op jit(solution)/shard_map/ppermute | solution.py:62
  203.8 83.1 %collective-permute-start.28 = (f32[96,768]{1,0:T(8,128)}, f32[96,768]{1,0:T(8,128)}, u32[]{:S(2)}, u32[]{:S(2)}) collective-permute-start(f32[96,768]{1,0:T(8,128)} %pad_maximum_fusion.23.refs_0_), channel_id=1, source_target_pairs={{0,24},{4,28},{8,16},{12,20},{16,8},{20,12},{24,0},{28,4},{1,25},{... | collective-permute-start | bytes 884744 | tf_op jit(solution)/shard_map/ppermute | solution.py:62
  275.6 54.6 %collective-permute-start.21 = (f32[512,768]{1,0:T(8,128)}, f32[512,768]{1,0:T(8,128)}, u32[]{:S(2)}, u32[]{:S(2)}) collective-permute-start(f32[512,768]{1,0:T(8,128)} %slice_add_fusion.2), channel_id=1, source_target_pairs={{0,2},{1,3},{2,0},{3,1},{4,6},{5,7},{6,4},{7,5},{8,10},{9,11},{10,... | collective-permute-start | bytes 4718600 | tf_op jit(solution)/shard_map/ppermute | solution.py:62
  280.4 45.0 %collective-permute-start.18 = (f32[192,768]{1,0:T(8,128)}, f32[192,768]{1,0:T(8,128)}, u32[]{:S(2)}, u32[]{:S(2)}) collective-permute-start(f32[192,768]{1,0:T(8,128)} %slice_add_fusion.9), channel_id=1, source_target_pairs={{0,2},{1,3},{2,0},{3,1},{4,6},{5,7},{6,4},{7,5},{8,10},{9,11},{10,... | collective-permute-start | bytes 1769480 | tf_op jit(solution)/shard_map/ppermute | solution.py:62
  298.4 528.5 %reduce-scatter.8.cloned.1.call-start = ((), (), s32[]{:S(2)}) async-start(), calls=%async_computation.8 | async-start | bytes 2654208 | tf_op jit(solution)/shard_map/reduce_scatter | solution.py:109
  525.0 448.4 %reduce-scatter.10.cloned.1.call-start = ((), (), s32[]{:S(2)}) async-start(), calls=%async_computation.9 | async-start | bytes 2654208 | tf_op jit(solution)/shard_map/reduce_scatter | solution.py:109
  554.4 421.7 %all-gather.11.cloned.1.call-start = ((), (), s32[]{:S(2)}) async-start(), calls=%async_computation.7 | async-start | bytes 3538944 | tf_op jit(solution)/shard_map/all_gather | solution.py:701
  590.6 423.3 %reduce-scatter.12.cloned.1.call-start = ((), (), s32[]{:S(2)}) async-start(), calls=%async_computation.10 | async-start | bytes 2654208 | tf_op jit(solution)/shard_map/reduce_scatter | solution.py:109
  633.4 380.5 %reduce-scatter.14.cloned.1.call-start = ((), (), s32[]{:S(2)}) async-start(), calls=%async_computation.11 | async-start | bytes 2654208 | tf_op jit(solution)/shard_map/reduce_scatter | solution.py:109
  751.2 81.3 %collective-permute-start.61 = (f32[4,96,768]{2,1,0:T(8,128)}, f32[4,96,768]{2,1,0:T(8,128)}, u32[]{:S(2)}, u32[]{:S(2)}) collective-permute-start(f32[4,96,768]{2,1,0:T(8,128)} %dynamic-slice_bitcast_fusion), channel_id=1, source_target_pairs={{0,4},{4,0},{8,12},{12,8},{16,20},{20,16},{24,28},{28,24},{1,5},{5... | collective-permute-start | bytes 3538952 | tf_op jit(solution)/shard_map/ppermute | solution.py:62
  765.4 70.3 %collective-permute-start.53 = (f32[4,96,768]{2,1,0:T(8,128)}, f32[4,96,768]{2,1,0:T(8,128)}, u32[]{:S(2)}, u32[]{:S(2)}) collective-permute-start(f32[4,96,768]{2,1,0:T(8,128)} %dynamic-slice_bitcast_fusion.2), channel_id=1, source_target_pairs={{0,4},{4,0},{8,12},{12,8},{16,20},{20,16},{24,28},{28,24},{1,5},{5... | collective-permute-start | bytes 3538952 | tf_op jit(solution)/shard_map/ppermute | solution.py:62
  769.6 67.6 %collective-permute-start.37 = (f32[512,768]{1,0:T(8,128)}, f32[512,768]{1,0:T(8,128)}, u32[]{:S(2)}, u32[]{:S(2)}) collective-permute-start(f32[512,768]{1,0:T(8,128)} %slice_add_fusion), channel_id=1, source_target_pairs={{0,2},{1,3},{2,0},{3,1},{4,6},{5,7},{6,4},{7,5},{8,10},{9,11},{10,... | collective-permute-start | bytes 4718600 | tf_op jit(solution)/shard_map/ppermute | solution.py:62
  772.1 43.2 %collective-permute-start.66 = (f32[9]{0:T(128)S(1)}, f32[9]{0:T(128)S(1)}, u32[]{:S(2)}, u32[]{:S(2)}) collective-permute-start(f32[9]{0:T(128)S(1)} %add.508), channel_id=1, source_target_pairs={{0,4},{4,0},{8,12},{12,8},{16,20},{20,16},{24,28},{28,24},{1,5},{5... | collective-permute-start | bytes 116 | tf_op jit(solution)/shard_map/ppermute | solution.py:62
  835.1 73.7 %collective-permute-start.62 = (f32[96,768]{1,0:T(8,128)}, f32[96,768]{1,0:T(8,128)}, u32[]{:S(2)}, u32[]{:S(2)}) collective-permute-start(f32[96,768]{1,0:T(8,128)} %get-tuple-element.193), channel_id=1, source_target_pairs={{0,8},{4,12},{8,0},{12,4},{16,24},{20,28},{24,16},{28,20},{1,9},{5... | collective-permute-start | bytes 884744 | tf_op jit(solution)/shard_map/ppermute | solution.py:62
  872.1 63.0 %collective-permute-start.63 = (f32[96,768]{1,0:T(8,128)}, f32[96,768]{1,0:T(8,128)}, u32[]{:S(2)}, u32[]{:S(2)}) collective-permute-start(f32[96,768]{1,0:T(8,128)} %get-tuple-element.195), channel_id=1, source_target_pairs={{0,16},{4,20},{8,24},{12,28},{16,0},{20,4},{24,8},{28,12},{1,17},{... | collective-permute-start | bytes 884744 | tf_op jit(solution)/shard_map/ppermute | solution.py:62
  872.4 64.7 %collective-permute-start.64 = (f32[96,768]{1,0:T(8,128)}, f32[96,768]{1,0:T(8,128)}, u32[]{:S(2)}, u32[]{:S(2)}) collective-permute-start(f32[96,768]{1,0:T(8,128)} %get-tuple-element.194), channel_id=1, source_target_pairs={{0,24},{4,28},{8,16},{12,20},{16,8},{20,12},{24,0},{28,4},{1,25},{... | collective-permute-start | bytes 884744 | tf_op jit(solution)/shard_map/ppermute | solution.py:62
  906.5 54.9 %collective-permute-start.49 = (f32[4,88,768]{2,1,0:T(8,128)}, f32[4,88,768]{2,1,0:T(8,128)}, u32[]{:S(2)}, u32[]{:S(2)}) collective-permute-start(f32[4,88,768]{2,1,0:T(8,128)} %dynamic-slice_bitcast_fusion.3), channel_id=1, source_target_pairs={{0,4},{4,0},{8,12},{12,8},{16,20},{20,16},{24,28},{28,24},{1,5},{5... | collective-permute-start | bytes 3244040 | tf_op jit(solution)/shard_map/ppermute | solution.py:62
  908.8 40.5 %collective-permute-start.58 = (f32[96,768]{1,0:T(8,128)}, f32[96,768]{1,0:T(8,128)S(1)}, u32[]{:S(2)}, u32[]{:S(2)}) collective-permute-start(f32[96,768]{1,0:T(8,128)} %get-tuple-element.196), channel_id=1, source_target_pairs={{0,8},{4,12},{8,0},{12,4},{16,24},{20,28},{24,16},{28,20},{1,9},{5... | collective-permute-start | bytes 884744 | tf_op jit(solution)/shard_map/ppermute | solution.py:62
  961.3 46.1 %collective-permute-start.41 = (f32[512,160]{0,1:T(8,128)}, f32[512,160]{0,1:T(8,128)}, u32[]{:S(2)}, u32[]{:S(2)}) collective-permute-start(f32[512,160]{0,1:T(8,128)} %add.474), channel_id=1, source_target_pairs={{0,1},{1,0},{2,3},{3,2},{4,5},{5,4},{6,7},{7,6},{8,9},{9,8},{10,11... | collective-permute-start | bytes 983048 | tf_op jit(solution)/shard_map/ppermute | solution.py:62
  963.6 47.0 %collective-permute-start.50 = (f32[88,768]{1,0:T(8,128)}, f32[88,768]{1,0:T(8,128)S(1)}, u32[]{:S(2)}, u32[]{:S(2)}) collective-permute-start(f32[88,768]{1,0:T(8,128)} %get-tuple-element.210), channel_id=1, source_target_pairs={{0,8},{4,12},{8,0},{12,4},{16,24},{20,28},{24,16},{28,20},{1,9},{5... | collective-permute-start | bytes 811016 | tf_op jit(solution)/shard_map/ppermute | solution.py:62
  969.8 40.8 %collective-permute-start.51 = (f32[88,768]{1,0:T(8,128)}, f32[88,768]{1,0:T(8,128)}, u32[]{:S(2)}, u32[]{:S(2)}) collective-permute-start(f32[88,768]{1,0:T(8,128)} %get-tuple-element.212), channel_id=1, source_target_pairs={{0,16},{4,20},{8,24},{12,28},{16,0},{20,4},{24,8},{28,12},{1,17},{... | collective-permute-start | bytes 811016 | tf_op jit(solution)/shard_map/ppermute | solution.py:62
  (246 other events, 2874.4 us)
Sparse Core Ops, SparseCore 0:
  32.9 98.0 reduce-scatter.5
  133.7 74.2 all-gather.12
  210.1 19.1 all-gather.8
  231.3 90.8 all-gather.14
  324.3 79.1 all-gather.16
  525.2 68.9 reduce-scatter.7
  597.6 68.8 reduce-scatter.9
  668.7 59.2 all-gather.10
  732.0 75.9 reduce-scatter.11
  811.9 90.8 reduce-scatter.13

commit v3 on v2

--- a/solution.py
+++ b/solution.py
@@ -109,8 +109,19 @@
     return lax.psum_scatter(blocks, "dp", scatter_dimension=0, tiled=False)
 
 
-def tie(value, other):
-    return lax.optimization_barrier((value, other))[0]
+def together(*values):
+    return lax.optimization_barrier(values)
+
+
+def model_columns(share):
+    place = lax.axis_index("mp")
+    near = exchange(share, "mp", 1)
+    pieces = [share, near, exchange(share, "mp", 2), exchange(near, "mp", 2)]
+    rows, width = share.shape
+    out = jnp.zeros((rows, len(pieces) * width), share.dtype)
+    for flip, piece in enumerate(pieces):
+        out = lax.dynamic_update_slice_in_dim(out, piece, (place ^ flip) * width, 1)
+    return out
 
 
 def gather_data(shard):
@@ -561,6 +572,12 @@
     self_allowed = (text_at.reshape(1, -1) <= text_at) & token_ok[None, :]
     cot = turn(cotangent)
 
+    vocab_rows, embed_width = embedding.shape
+    local_ids = token_ids.reshape(-1) - dp_place * vocab_rows
+    owned = (local_ids >= 0) & (local_ids < vocab_rows)
+    safe_ids = jnp.clip(local_ids, 0, vocab_rows - 1)
+    picked = jnp.where(owned[:, None], jnp.take(embedding, safe_ids, axis=0), 0.0)
+
     frame_at = positions(frames)
     first, last = frame_at == 0, frame_at == frames - 1
     both = turn(mel_frames.reshape(frames, 2 * mel))
@@ -571,10 +588,9 @@
     stem_one = gelu(pre_one)
     odd = stem_one[:, stem_width:]
     stem_cat = jnp.concatenate([jnp.where(first, 0.0, jnp.roll(odd, 1, axis=0)), stem_one], axis=1)
-    stem_part = mm(stem_cat, w_two)
+    stem_part, enc_attn_all, picked = together(mm(stem_cat, w_two), enc_attn_all, picked)
     stem_sum = model_sum(stem_part)
-    dec_mlp_shard = tie(jnp.concatenate([dec_up, dec_down.T], axis=0), stem_part)
-    dec_up_all, dec_down_all = split_rows(gather_slow(dec_mlp_shard), mlp_cuts)
+    dec_up_all, dec_down_all = split_rows(gather_slow(jnp.concatenate([dec_up, dec_down.T], axis=0)), mlp_cuts)
     stream_zero = gelu(stem_sum) + sinusoid(frames)
 
     hat_zero, scale_zero = normalize(stream_zero)
@@ -594,14 +610,8 @@
     cross_two = mm(memory, cross_all[:, local : 3 * local])
     cross_k, cross_v = cross_two[:, :local], cross_two[:, local:]
 
-    vocab_rows, embed_width = embedding.shape
-    local_ids = token_ids.reshape(-1) - dp_place * vocab_rows
-    owned = (local_ids >= 0) & (local_ids < vocab_rows)
-    safe_ids = jnp.clip(local_ids, 0, vocab_rows - 1)
-    picked = jnp.where(owned[:, None], jnp.take(embedding, safe_ids, axis=0), 0.0)
-    picked = tie(picked, stem_sum)
     share = lax.psum_scatter(picked, "dp", scatter_dimension=0, tiled=True)
-    text_zero = turn(lax.all_gather(share, "mp", axis=1, tiled=True)) + sinusoid(tokens)
+    text_zero = turn(model_columns(share)) + sinusoid(tokens)
 
     hat_three, scale_three = normalize(text_zero)
     ln_three = hat_three * norms[3, 0] + norms[3, 1]

time: 1030 us -> 1010 us (0.981)
  local copies, waits for them, and re-layouts: 129 us -> 152 us
  waiting for transfers between devices: 292 us -> 270 us
  other arithmetic: 172 us -> 155 us
    reduce_scatter x1, waiting for transfers between devices: 31.5 us -> 0.02 us  [body(): share = lax.psum_scatter(picked, 'dp', scatter_dimension=0, tiled=True)]
    dynamic_update_slice x0 -> x4, local copies, waits for them, and re-layouts: none -> 14.1 us  [model_columns(): out = lax.dynamic_update_slice_in_dim(out, piece, (place ^ flip) * width, 1)]
    ppermute x69 -> x72, waiting for transfers between devices: 260 us -> 270 us  [exchange(): return lax.ppermute(value, axis, [(i, i ^ flip) for i in range(size)])]
    unnamed x413 -> x411, local copies, waits for them, and re-layouts: 50.7 us -> 57.3 us
    ppermute x69 -> x72, starting transfers between devices: 101 us -> 95.4 us  [exchange(): return lax.ppermute(value, axis, [(i, i ^ flip) for i in range(size)])]
  transfers between devices with their start and end apart: 79 -> 81, of which waited for: 30 -> 30; matrix products, arithmetic and copies ran while one was open for 35% -> 38% of each run, Pallas kernels for 11% -> 11%
where the time goes in v3:
time: 1010 us; the launch traced here: 1000 us
  waiting for transfers between devices  270 us (27%)
  Pallas kernels  171 us (17%)
  other arithmetic  155 us (15%)
  local copies, waits for them, and re-layouts  152 us (15%)
  matrix products  139 us (14%)
  starting transfers between devices  96.3 us (10%)
  between operations  17.3 us (2%)
    ppermute x72, waiting for transfers between devices, exchange(): return lax.ppermute(value, axis, [(i, i ^ flip) for i in range(size)])  270 us
    pallas_call x4, Pallas kernels, call(): pl.pallas_call(kernel, out_shape=[jax.ShapeDtypeStruct(o.shape, o.dtype)...  162 us
    ppermute x72, starting transfers between devices, exchange(): return lax.ppermute(value, axis, [(i, i ^ flip) for i in range(size)])  95.4 us
    dot_general x27, matrix products, dot(): lax.dot_general(left, right, (contract, ((), ())), precision=HIGH, prefer...  70.3 us
    unnamed x411, local copies, waits for them, and re-layouts  57.3 us
    scatter-add x1, other arithmetic, body(): grad_embedding = jnp.zeros(embedding.shape, jnp.float32).at[safe_ids].add...  25.4 us
  transfers between devices with their start and end apart: 81, of which 30 were waited for; matrix products, arithmetic and copies ran while one was open for 38% of the time, Pallas kernels for 11%

profile of v3, /device:TPU:0, one launch (start us, length us, event | category | flops | bytes accessed | tf_op | source)
XLA Modules:
  0.0 1000.6 jit_solution(10825775675864034812)
XLA Ops:
  24.8 6.6 copy.157
  32.0 12.7 %gather_fusion = f32[3072,192]{1,0:T(8,128)S(1)} fusion(f32[6480,192]{1,0:T(8,128)} %copy.157, s32[3072]{0:T(1024)S(1)} %broadcast_clamp_fusion), kind=kCustom, calls=%fused_computation | custom fusion | bytes 4730880 | tf_op jit(solution)/shard_map/jit(_take)/gather | solution.py:579
  54.2 12.6 %collective-permute-done.2.refs_3_ = f32[88,768]{1,0:T(8,128)S(1)} collective-permute-done((f32[88,768]{1,0:T(8,128)}, f32[88,768]{1,0:T(8,128)S(1)}, u32[]{:S(2)}, u32[]{:S(2)}) %collective-permute-start.2) | collective-permute-done | bytes 270368 | tf_op jit(solution)/shard_map/ppermute | solution.py:62
  66.8 11.6 %collective-permute-done.4.refs_5_ = f32[88,768]{1,0:T(8,128)S(1)} collective-permute-done((f32[88,768]{1,0:T(8,128)}, f32[88,768]{1,0:T(8,128)S(1)}, u32[]{:S(2)}, u32[]{:S(2)}) %collective-permute-start.4) | collective-permute-done | bytes 270368 | tf_op jit(solution)/shard_map/ppermute | solution.py:62
  122.9 20.1 %collective-permute-done.21 = f32[512,768]{1,0:T(8,128)S(1)} collective-permute-done((f32[512,768]{1,0:T(8,128)}, f32[512,768]{1,0:T(8,128)S(1)}, u32[]{:S(2)}, u32[]{:S(2)}) %collective-permute-start.21) | collective-permute-done | bytes 1572896 | tf_op jit(solution)/shard_map/ppermute | solution.py:62
  150.1 6.9 multiply_sine_fusion
  163.2 8.1 collective-permute-done.12.refs_3_
  172.4 9.2 collective-permute-done.14.refs_5_
  203.4 6.1 select_reduce_fusion
  217.4 9.7 fusion
  290.5 6.3 collective-permute-done.30.refs_5_
  308.0 8.3 collective-permute-done.18
  331.3 51.1 %enc_mlp_forward.1 = (f32[1024,768]{1,0:T(8,128)}, f32[1024,768]{1,0:T(8,128)}, f32[8,768]{1,0:T(8,128)}) custom-call(f32[1024,768]{1,0:T(8,128)} %maximum_add_fusion.1.x_ref, f32[2,768]{1,0:T(2,128)} %squeeze.125.norm_ref, bf16[768,768]{1,0:T(8,128)(2,1)} %get-tuple-element.185.uh, bf16[768,768]{1,0:T(8,128)(2,1)} %get-tuple-element.184.ul, ...), custom_call_target="tpu_custom_call" | custom-call | flops 7247757312 | bytes 14190592 | tf_op jit(solution)/shard_map/enc_mlp_forward/pallas_call | solution.py:295
  407.5 10.7 %collective-permute-done.34 = f32[192,768]{1,0:T(8,128)S(1)} collective-permute-done((f32[192,768]{1,0:T(8,128)S(1)}, f32[192,768]{1,0:T(8,128)S(1)}, u32[]{:S(2)}, u32[]{:S(2)}) %collective-permute-start.34) | collective-permute-done | bytes 589856 | tf_op jit(solution)/shard_map/ppermute | solution.py:62
  423.3 28.0 %dec_mlp_forward.1 = (f32[384,768]{1,0:T(8,128)}, f32[384,768]{1,0:T(8,128)}, f32[8,768]{1,0:T(8,128)}) custom-call(f32[384,768]{1,0:T(8,128)} %maximum_add_fusion.3.x_ref, f32[2,768]{1,0:T(2,128)} %squeeze.129.norm_ref, bf16[768,768]{1,0:T(8,128)(2,1)} %get-tuple-element.181.uh, bf16[768,768]{1,0:T(8,128)(2,1)} %get-tuple-element.180.ul, ...), custom_call_target="tpu_custom_call" | custom-call | flops 2717908992 | bytes 8289792 | tf_op jit(solution)/shard_map/dec_mlp_forward/pallas_call | solution.py:295
  451.4 29.8 %dec_mlp_backward.1 = (f32[384,768]{1,0:T(8,128)}, f32[768,768]{1,0:T(8,128)}, f32[768,768]{1,0:T(8,128)}, f32[8,768]{1,0:T(8,128)}) custom-call(f32[384,768]{1,0:T(8,128)} %maximum_select_fusion.2.g_ref, f32[384,768]{1,0:T(8,128)} %maximum_add_fusion.3.x_ref, f32[2,768]{1,0:T(2,128)} %squeeze.129.norm_ref, f32[384,768]{1,0:T(8,128)} %get-tuple-element.39.pre_ref, ...), custom_call_target="tpu_custom_call" | custom-call | flops 5435817984 | bytes 14186496 | tf_op jit(solution)/shard_map/dec_mlp_backward/pallas_call | solution.py:295
  510.5 9.7 collective-permute-done.46
  547.2 14.0 %collective-permute-done.49 = f32[192,768]{1,0:T(8,128)S(1)} collective-permute-done((f32[192,768]{1,0:T(8,128)S(1)}, f32[192,768]{1,0:T(8,128)S(1)}, u32[]{:S(2)}, u32[]{:S(2)}) %collective-permute-start.49) | collective-permute-done | bytes 589856 | tf_op jit(solution)/shard_map/ppermute | solution.py:62
  574.7 35.4 %collective-permute-done.37 = f32[512,768]{1,0:T(8,128)S(1)} collective-permute-done((f32[512,768]{1,0:T(8,128)S(1)}, f32[512,768]{1,0:T(8,128)S(1)}, u32[]{:S(2)}, u32[]{:S(2)}) %collective-permute-start.37) | collective-permute-done | bytes 1572896 | tf_op jit(solution)/shard_map/ppermute | solution.py:62
  623.1 52.6 %enc_mlp_backward.1 = (f32[1024,768]{1,0:T(8,128)}, f32[768,768]{1,0:T(8,128)}, f32[768,768]{1,0:T(8,128)}, f32[8,768]{1,0:T(8,128)}) custom-call(f32[1024,768]{1,0:T(8,128)} %subtract_multiply_fusion.g_ref, f32[1024,768]{1,0:T(8,128)} %maximum_add_fusion.1.x_ref, f32[2,768]{1,0:T(2,128)} %squeeze.125.norm_ref, f32[1024,768]{1,0:T(8,128)} %get-tuple-element.41.pre_ref, ...), custom_call_target="tpu_custom_call" | custom-call | flops 14495514624 | bytes 22050816 | tf_op jit(solution)/shard_map/enc_mlp_backward/pallas_call | solution.py:295
  681.4 11.0 %multiply_multiply_fusion = f32[3,1024,1024]{1,2,0:T(8,128)S(1)} fusion(f32[3,1024,1024]{1,2,0:T(8,128)} %copy-done, f32[3,1024]{1,0:T(4,128)S(1)} %bitcast.425, f32[3,1024]{1,0:T(4,128)S(1)} %log_add_fusion, pred[1024]{0:T(1024)(128)(4,1)S(1)} %copy-done.144, f32[1024,3,64]{0,2,1:T(8,128)S(1)} %bitcast.360, f32[1024,3,64]{0,2,1:T(8,128)S(1)} %bitcast.376), kind=kOutput, calls=%fused_computation.2 | convolution fusion | flops 1226833920 | bytes 26764288 | tf_op jit(solution)/shard_map/qhe,khe->hqk/dot_general | solution.py:452
  696.7 6.7 fusion.205
  703.4 7.3 fusion.3
  710.8 6.4 fusion.48
  723.5 5.8 stack.163
  753.8 43.7 %collective-permute-done.69 = f32[9]{0:T(128)S(1)} collective-permute-done((f32[9]{0:T(128)S(1)}, f32[9]{0:T(128)S(1)}, u32[]{:S(2)}, u32[]{:S(2)}) %collective-permute-start.69) | collective-permute-done | bytes 68 | tf_op jit(solution)/shard_map/ppermute | solution.py:62
  824.6 22.1 %collective-permute-done.60 = f32[4,96,768]{2,1,0:T(8,128)S(1)} collective-permute-done((f32[4,96,768]{2,1,0:T(8,128)S(1)}, f32[4,96,768]{2,1,0:T(8,128)S(1)}, u32[]{:S(2)}, u32[]{:S(2)}) %collective-permute-start.60) | collective-permute-done | bytes 1179680 | tf_op jit(solution)/shard_map/ppermute | solution.py:62
  890.2 25.8 %collective-permute-start.61 = (f32[96,768]{1,0:T(8,128)}, f32[96,768]{1,0:T(8,128)S(1)}, u32[]{:S(2)}, u32[]{:S(2)}) collective-permute-start(f32[96,768]{1,0:T(8,128)} %get-tuple-element.198), channel_id=1, source_target_pairs={{0,8},{4,12},{8,0},{12,4},{16,24},{20,28},{24,16},{28,20},{1,9},{5... | collective-permute-start | bytes 884744 | tf_op jit(solution)/shard_map/ppermute | solution.py:62
  929.3 10.4 %collective-permute-done.62 = f32[96,768]{1,0:T(8,128)S(1)} collective-permute-done((f32[96,768]{1,0:T(8,128)}, f32[96,768]{1,0:T(8,128)S(1)}, u32[]{:S(2)}, u32[]{:S(2)}) %collective-permute-start.62) | collective-permute-done | bytes 294944 | tf_op jit(solution)/shard_map/ppermute | solution.py:62
  944.5 6.0 collective-permute-start.53
  955.7 25.4 %scatter_custom_fusion = f32[6480,192]{1,0:T(8,128)} fusion(s32[3072]{0:T(1024)} %bitcast.440, f32[]{:T(128)} %constant.186.clone.1, f32[3072,192]{1,0:T(8,128)} %all-gather.8.cloned.1.call-done, pred[3072]{0:T(1024)(128)(4,1)S(1)} %copy-done.170), kind=kCustom, calls=%fused_computation.36 | custom fusion | flops 1179648 | bytes 8126464 | tf_op jit(solution)/shard_map/scatter-add | solution.py:715
  981.1 6.3 copy.185
  (863 shorter events, 456.8 us)
Async XLA Ops:
  7.2 91.9 %all-gather.10.cloned.1.call-start = ((), (), s32[]{:S(2)}) async-start(), calls=%async_computation.11 | async-start | bytes 2654208 | tf_op jit(solution)/shard_map/all_gather | solution.py:96
  10.7 40.9 %collective-permute-start.1 = (f32[88,768]{1,0:T(8,128)}, f32[88,768]{1,0:T(8,128)}, u32[]{:S(2)}, u32[]{:S(2)}) collective-permute-start(f32[88,768]{1,0:T(8,128)} %select_maximum_fusion.5.refs_0_), channel_id=1, source_target_pairs={{0,8},{4,12},{8,0},{12,4},{16,24},{20,28},{24,16},{28,20},{1,9},{5... | collective-permute-start | bytes 811016 | tf_op jit(solution)/shard_map/ppermute | solution.py:62
  20.9 196.4 %reduce-scatter.6.cloned.1.call-start = ((), (), s32[]{:S(2)}) async-start(), calls=%async_computation.5 | async-start | bytes 3538944 | tf_op jit(solution)/shard_map/reduce_scatter | solution.py:613
  99.1 206.2 %all-gather.12.cloned.1.call-start = ((), (), s32[]{:S(2)}) async-start(), calls=%async_computation.12 | async-start | bytes 5308416 | tf_op jit(solution)/shard_map/all_gather | solution.py:96
  101.1 303.6 %all-gather.14.cloned.1.call-start = ((), (), s32[]{:S(2)}) async-start(), calls=%async_computation.13 | async-start | bytes 5308416 | tf_op jit(solution)/shard_map/all_gather | solution.py:96
  109.7 47.3 %collective-permute-start.11 = (f32[96,768]{1,0:T(8,128)}, f32[96,768]{1,0:T(8,128)}, u32[]{:S(2)}, u32[]{:S(2)}) collective-permute-start(f32[96,768]{1,0:T(8,128)} %pad_maximum_fusion.22.refs_0_), channel_id=1, source_target_pairs={{0,8},{4,12},{8,0},{12,4},{16,24},{20,28},{24,16},{28,20},{1,9},{5... | collective-permute-start | bytes 884744 | tf_op jit(solution)/shard_map/ppermute | solution.py:62
  110.4 47.3 %collective-permute-start.13 = (f32[96,768]{1,0:T(8,128)}, f32[96,768]{1,0:T(8,128)}, u32[]{:S(2)}, u32[]{:S(2)}) collective-permute-start(f32[96,768]{1,0:T(8,128)} %pad_maximum_fusion.22.refs_0_), channel_id=1, source_target_pairs={{0,16},{4,20},{8,24},{12,28},{16,0},{20,4},{24,8},{28,12},{1,17},{... | collective-permute-start | bytes 884744 | tf_op jit(solution)/shard_map/ppermute | solution.py:62
  113.8 45.3 %collective-permute-start.15 = (f32[96,768]{1,0:T(8,128)}, f32[96,768]{1,0:T(8,128)}, u32[]{:S(2)}, u32[]{:S(2)}) collective-permute-start(f32[96,768]{1,0:T(8,128)} %pad_maximum_fusion.22.refs_0_), channel_id=1, source_target_pairs={{0,24},{4,28},{8,16},{12,20},{16,8},{20,12},{24,0},{28,4},{1,25},{... | collective-permute-start | bytes 884744 | tf_op jit(solution)/shard_map/ppermute | solution.py:62
  114.1 46.6 %collective-permute-start.10 = (f32[96,768]{1,0:T(8,128)}, f32[96,768]{1,0:T(8,128)}, u32[]{:S(2)}, u32[]{:S(2)}) collective-permute-start(f32[96,768]{1,0:T(8,128)} %pad_maximum_fusion.22.refs_0_), channel_id=1, source_target_pairs={{0,4},{4,0},{8,12},{12,8},{16,20},{20,16},{24,28},{28,24},{1,5},{5... | collective-permute-start | bytes 884744 | tf_op jit(solution)/shard_map/ppermute | solution.py:62
  116.7 692.6 %reduce-scatter.8.cloned.1.call-start = ((), (), s32[]{:S(2)}) async-start(), calls=%async_computation.7 | async-start | bytes 2654208 | tf_op jit(solution)/shard_map/reduce_scatter | solution.py:109
  144.6 46.2 %collective-permute-start.22 = (f32[512,768]{1,0:T(8,128)S(1)}, f32[512,768]{1,0:T(8,128)S(1)}, u32[]{:S(2)}, u32[]{:S(2)}) collective-permute-start(f32[512,768]{1,0:T(8,128)S(1)} %add.455), channel_id=1, source_target_pairs={{0,1},{1,0},{2,3},{3,2},{4,5},{5,4},{6,7},{7,6},{8,9},{9,8},{10,11... | collective-permute-start | bytes 4718600 | tf_op jit(solution)/shard_map/ppermute | solution.py:62
  160.7 113.5 %collective-permute-start.27 = (f32[96,768]{1,0:T(8,128)}, f32[96,768]{1,0:T(8,128)}, u32[]{:S(2)}, u32[]{:S(2)}) collective-permute-start(f32[96,768]{1,0:T(8,128)} %pad_maximum_fusion.23.refs_0_), channel_id=1, source_target_pairs={{0,8},{4,12},{8,0},{12,4},{16,24},{20,28},{24,16},{28,20},{1,9},{5... | collective-permute-start | bytes 884744 | tf_op jit(solution)/shard_map/ppermute | solution.py:62
  171.2 104.3 %collective-permute-start.29 = (f32[96,768]{1,0:T(8,128)}, f32[96,768]{1,0:T(8,128)}, u32[]{:S(2)}, u32[]{:S(2)}) collective-permute-start(f32[96,768]{1,0:T(8,128)} %pad_maximum_fusion.23.refs_0_), channel_id=1, source_target_pairs={{0,16},{4,20},{8,24},{12,28},{16,0},{20,4},{24,8},{28,12},{1,17},{... | collective-permute-start | bytes 884744 | tf_op jit(solution)/shard_map/ppermute | solution.py:62
  181.6 95.2 %collective-permute-start.31 = (f32[96,768]{1,0:T(8,128)}, f32[96,768]{1,0:T(8,128)}, u32[]{:S(2)}, u32[]{:S(2)}) collective-permute-start(f32[96,768]{1,0:T(8,128)} %pad_maximum_fusion.23.refs_0_), channel_id=1, source_target_pairs={{0,24},{4,28},{8,16},{12,20},{16,8},{20,12},{24,0},{28,4},{1,25},{... | collective-permute-start | bytes 884744 | tf_op jit(solution)/shard_map/ppermute | solution.py:62
  267.0 50.8 %collective-permute-start.24 = (f32[512,768]{1,0:T(8,128)}, f32[512,768]{1,0:T(8,128)}, u32[]{:S(2)}, u32[]{:S(2)}) collective-permute-start(f32[512,768]{1,0:T(8,128)} %slice_add_fusion.2), channel_id=1, source_target_pairs={{0,2},{1,3},{2,0},{3,1},{4,6},{5,7},{6,4},{7,5},{8,10},{9,11},{10,... | collective-permute-start | bytes 4718600 | tf_op jit(solution)/shard_map/ppermute | solution.py:62
  510.3 442.8 %reduce-scatter.10.cloned.1.call-start = ((), (), s32[]{:S(2)}) async-start(), calls=%async_computation.8 | async-start | bytes 2654208 | tf_op jit(solution)/shard_map/reduce_scatter | solution.py:109
  539.5 416.2 %all-gather.8.cloned.1.call-start = ((), (), s32[]{:S(2)}) async-start(), calls=%async_computation.6 | async-start | bytes 3538944 | tf_op jit(solution)/shard_map/all_gather | solution.py:711
  570.6 423.3 %reduce-scatter.12.cloned.1.call-start = ((), (), s32[]{:S(2)}) async-start(), calls=%async_computation.9 | async-start | bytes 2654208 | tf_op jit(solution)/shard_map/reduce_scatter | solution.py:109
  613.4 380.4 %reduce-scatter.14.cloned.1.call-start = ((), (), s32[]{:S(2)}) async-start(), calls=%async_computation.10 | async-start | bytes 2654208 | tf_op jit(solution)/shard_map/reduce_scatter | solution.py:109
  731.7 82.2 %collective-permute-start.64 = (f32[4,96,768]{2,1,0:T(8,128)}, f32[4,96,768]{2,1,0:T(8,128)}, u32[]{:S(2)}, u32[]{:S(2)}) collective-permute-start(f32[4,96,768]{2,1,0:T(8,128)} %dynamic-slice_bitcast_fusion), channel_id=1, source_target_pairs={{0,4},{4,0},{8,12},{12,8},{16,20},{20,16},{24,28},{28,24},{1,5},{5... | collective-permute-start | bytes 3538952 | tf_op jit(solution)/shard_map/ppermute | solution.py:62
  745.7 71.1 %collective-permute-start.56 = (f32[4,96,768]{2,1,0:T(8,128)}, f32[4,96,768]{2,1,0:T(8,128)}, u32[]{:S(2)}, u32[]{:S(2)}) collective-permute-start(f32[4,96,768]{2,1,0:T(8,128)} %dynamic-slice_bitcast_fusion.2), channel_id=1, source_target_pairs={{0,4},{4,0},{8,12},{12,8},{16,20},{20,16},{24,28},{28,24},{1,5},{5... | collective-permute-start | bytes 3538952 | tf_op jit(solution)/shard_map/ppermute | solution.py:62
  750.0 68.3 %collective-permute-start.40 = (f32[512,768]{1,0:T(8,128)}, f32[512,768]{1,0:T(8,128)}, u32[]{:S(2)}, u32[]{:S(2)}) collective-permute-start(f32[512,768]{1,0:T(8,128)} %slice_add_fusion), channel_id=1, source_target_pairs={{0,2},{1,3},{2,0},{3,1},{4,6},{5,7},{6,4},{7,5},{8,10},{9,11},{10,... | collective-permute-start | bytes 4718600 | tf_op jit(solution)/shard_map/ppermute | solution.py:62
  752.8 44.7 %collective-permute-start.69 = (f32[9]{0:T(128)S(1)}, f32[9]{0:T(128)S(1)}, u32[]{:S(2)}, u32[]{:S(2)}) collective-permute-start(f32[9]{0:T(128)S(1)} %add.521), channel_id=1, source_target_pairs={{0,4},{4,0},{8,12},{12,8},{16,20},{20,16},{24,28},{28,24},{1,5},{5... | collective-permute-start | bytes 116 | tf_op jit(solution)/shard_map/ppermute | solution.py:62
  816.5 73.7 %collective-permute-start.65 = (f32[96,768]{1,0:T(8,128)}, f32[96,768]{1,0:T(8,128)}, u32[]{:S(2)}, u32[]{:S(2)}) collective-permute-start(f32[96,768]{1,0:T(8,128)} %get-tuple-element.195), channel_id=1, source_target_pairs={{0,8},{4,12},{8,0},{12,4},{16,24},{20,28},{24,16},{28,20},{1,9},{5... | collective-permute-start | bytes 884744 | tf_op jit(solution)/shard_map/ppermute | solution.py:62
  852.2 63.8 %collective-permute-start.66 = (f32[96,768]{1,0:T(8,128)}, f32[96,768]{1,0:T(8,128)}, u32[]{:S(2)}, u32[]{:S(2)}) collective-permute-start(f32[96,768]{1,0:T(8,128)} %get-tuple-element.197), channel_id=1, source_target_pairs={{0,16},{4,20},{8,24},{12,28},{16,0},{20,4},{24,8},{28,12},{1,17},{... | collective-permute-start | bytes 884744 | tf_op jit(solution)/shard_map/ppermute | solution.py:62
  853.1 63.3 %collective-permute-start.67 = (f32[96,768]{1,0:T(8,128)}, f32[96,768]{1,0:T(8,128)}, u32[]{:S(2)}, u32[]{:S(2)}) collective-permute-start(f32[96,768]{1,0:T(8,128)} %get-tuple-element.196), channel_id=1, source_target_pairs={{0,24},{4,28},{8,16},{12,20},{16,8},{20,12},{24,0},{28,4},{1,25},{... | collective-permute-start | bytes 884744 | tf_op jit(solution)/shard_map/ppermute | solution.py:62
  886.8 55.4 %collective-permute-start.52 = (f32[4,88,768]{2,1,0:T(8,128)}, f32[4,88,768]{2,1,0:T(8,128)}, u32[]{:S(2)}, u32[]{:S(2)}) collective-permute-start(f32[4,88,768]{2,1,0:T(8,128)} %dynamic-slice_bitcast_fusion.3), channel_id=1, source_target_pairs={{0,4},{4,0},{8,12},{12,8},{16,20},{20,16},{24,28},{28,24},{1,5},{5... | collective-permute-start | bytes 3244040 | tf_op jit(solution)/shard_map/ppermute | solution.py:62
  890.2 39.1 %collective-permute-start.61 = (f32[96,768]{1,0:T(8,128)}, f32[96,768]{1,0:T(8,128)S(1)}, u32[]{:S(2)}, u32[]{:S(2)}) collective-permute-start(f32[96,768]{1,0:T(8,128)} %get-tuple-element.198), channel_id=1, source_target_pairs={{0,8},{4,12},{8,0},{12,4},{16,24},{20,28},{24,16},{28,20},{1,9},{5... | collective-permute-start | bytes 884744 | tf_op jit(solution)/shard_map/ppermute | solution.py:62
  942.2 45.3 %collective-permute-start.44 = (f32[512,160]{0,1:T(8,128)}, f32[512,160]{0,1:T(8,128)}, u32[]{:S(2)}, u32[]{:S(2)}) collective-permute-start(f32[512,160]{0,1:T(8,128)} %add.488), channel_id=1, source_target_pairs={{0,1},{1,0},{2,3},{3,2},{4,5},{5,4},{6,7},{7,6},{8,9},{9,8},{10,11... | collective-permute-start | bytes 983048 | tf_op jit(solution)/shard_map/ppermute | solution.py:62
  944.5 46.1 %collective-permute-start.53 = (f32[88,768]{1,0:T(8,128)}, f32[88,768]{1,0:T(8,128)S(1)}, u32[]{:S(2)}, u32[]{:S(2)}) collective-permute-start(f32[88,768]{1,0:T(8,128)} %get-tuple-element.212), channel_id=1, source_target_pairs={{0,8},{4,12},{8,0},{12,4},{16,24},{20,28},{24,16},{28,20},{1,9},{5... | collective-permute-start | bytes 811016 | tf_op jit(solution)/shard_map/ppermute | solution.py:62
  950.5 40.1 %collective-permute-start.54 = (f32[88,768]{1,0:T(8,128)}, f32[88,768]{1,0:T(8,128)}, u32[]{:S(2)}, u32[]{:S(2)}) collective-permute-start(f32[88,768]{1,0:T(8,128)} %get-tuple-element.214), channel_id=1, source_target_pairs={{0,16},{4,20},{8,24},{12,28},{16,0},{20,4},{24,8},{28,12},{1,17},{... | collective-permute-start | bytes 811016 | tf_op jit(solution)/shard_map/ppermute | solution.py:62
  951.1 39.5 %collective-permute-start.55 = (f32[88,768]{1,0:T(8,128)}, f32[88,768]{1,0:T(8,128)}, u32[]{:S(2)}, u32[]{:S(2)}) collective-permute-start(f32[88,768]{1,0:T(8,128)} %get-tuple-element.213), channel_id=1, source_target_pairs={{0,24},{4,28},{8,16},{12,20},{16,8},{20,12},{24,0},{28,4},{1,25},{... | collective-permute-start | bytes 811016 | tf_op jit(solution)/shard_map/ppermute | solution.py:62
  (247 other events, 2983.9 us)
Sparse Core Ops, SparseCore 0:
  21.0 69.0 all-gather.9
  99.2 113.7 reduce-scatter.5
  215.2 78.4 all-gather.11
  295.7 80.0 all-gather.13
  510.4 66.4 reduce-scatter.7
  580.2 68.9 reduce-scatter.9
  651.4 59.2 all-gather.7
  714.7 77.4 reduce-scatter.11
  796.2 86.8 reduce-scatter.13

commit v4 on v3

--- a/solution.py
+++ b/solution.py
@@ -701,7 +701,7 @@
         ),
         axis=1,
     )
-    grad_dec_attn = scatter_slow(
+    grad_dec_attn = scatter_data(
         block(jnp.concatenate([mm_tn(ln_three, grad_three), grad_dec_out], axis=1))
     )
     grad_ln = model_sum(mm_nt(grad_three, dec_attn_all[:, : 3 * local]))
@@ -721,7 +721,7 @@
         grad_stream_two, stream_one, norms[1], enc_pre, enc_up_all, enc_down_all, 4, "enc_mlp_backward"
     )
     grad_enc_up = scatter_data(block(grad_up))
-    grad_enc_down = scatter_data(block(grad_down))
+    grad_enc_down = scatter_slow(block(grad_down))
     norm_one = norm_one[:2]
 
     grad_enc_out = mm_tn(grad_stream_one, enc_mixed)

time: 1010 us -> 973 us (0.963)
  starting transfers between devices: 96.3 us -> 78.2 us
    ppermute x72, starting transfers between devices: 95.4 us -> 77.1 us  [exchange(): return lax.ppermute(value, axis, [(i, i ^ flip) for i in range(size)])]
    ppermute x72, waiting for transfers between devices: 270 us -> 259 us  [exchange(): return lax.ppermute(value, axis, [(i, i ^ flip) for i in range(size)])]
    unnamed x411 -> x397, local copies, waits for them, and re-layouts: 57.3 us -> 53.7 us
  transfers between devices with their start and end apart: 81 -> 81, of which waited for: 30 -> 29; matrix products, arithmetic and copies ran while one was open for 38% -> 40% of each run, Pallas kernels for 11% -> 12%
where the time goes in v4:
time: 973 us; the launch traced here: 963 us
  waiting for transfers between devices  260 us (27%)
  Pallas kernels  171 us (18%)
  other arithmetic  150 us (15%)
  local copies, waits for them, and re-layouts  147 us (15%)
  matrix products  140 us (14%)
  starting transfers between devices  78.2 us (8%)
  between operations  17.6 us (2%)
    ppermute x72, waiting for transfers between devices, exchange(): return lax.ppermute(value, axis, [(i, i ^ flip) for i in range(size)])  259 us
    pallas_call x4, Pallas kernels, call(): pl.pallas_call(kernel, out_shape=[jax.ShapeDtypeStruct(o.shape, o.dtype)...  162 us
    ppermute x72, starting transfers between devices, exchange(): return lax.ppermute(value, axis, [(i, i ^ flip) for i in range(size)])  77.1 us
    dot_general x27, matrix products, dot(): lax.dot_general(left, right, (contract, ((), ())), precision=HIGH, prefer...  69.9 us
    unnamed x397, local copies, waits for them, and re-layouts  53.7 us
    scatter-add x1, other arithmetic, body(): grad_embedding = jnp.zeros(embedding.shape, jnp.float32).at[safe_ids].add...  25 us
  transfers between devices with their start and end apart: 81, of which 29 were waited for; matrix products, arithmetic and copies ran while one was open for 40% of the time, Pallas kernels for 12%

profile of v4, /device:TPU:0, one launch (start us, length us, event | category | flops | bytes accessed | tf_op | source)
XLA Modules:
  0.0 963.0 jit_solution(9215994390570812672)
XLA Ops:
  24.8 6.5 copy.156
  32.0 12.7 %gather_fusion = f32[3072,192]{1,0:T(8,128)S(1)} fusion(f32[6480,192]{1,0:T(8,128)} %copy.156, s32[3072]{0:T(1024)S(1)} %broadcast_clamp_fusion), kind=kCustom, calls=%fused_computation | custom fusion | bytes 4730880 | tf_op jit(solution)/shard_map/jit(_take)/gather | solution.py:579
  54.2 12.6 %collective-permute-done.2.refs_3_ = f32[88,768]{1,0:T(8,128)S(1)} collective-permute-done((f32[88,768]{1,0:T(8,128)}, f32[88,768]{1,0:T(8,128)S(1)}, u32[]{:S(2)}, u32[]{:S(2)}) %collective-permute-start.2) | collective-permute-done | bytes 270368 | tf_op jit(solution)/shard_map/ppermute | solution.py:62
  66.8 11.6 %collective-permute-done.4.refs_5_ = f32[88,768]{1,0:T(8,128)S(1)} collective-permute-done((f32[88,768]{1,0:T(8,128)}, f32[88,768]{1,0:T(8,128)S(1)}, u32[]{:S(2)}, u32[]{:S(2)}) %collective-permute-start.4) | collective-permute-done | bytes 270368 | tf_op jit(solution)/shard_map/ppermute | solution.py:62
  122.8 20.1 %collective-permute-done.21 = f32[512,768]{1,0:T(8,128)S(1)} collective-permute-done((f32[512,768]{1,0:T(8,128)}, f32[512,768]{1,0:T(8,128)S(1)}, u32[]{:S(2)}, u32[]{:S(2)}) %collective-permute-start.21) | collective-permute-done | bytes 1572896 | tf_op jit(solution)/shard_map/ppermute | solution.py:62
  150.1 6.9 multiply_sine_fusion
  163.1 8.2 collective-permute-done.12.refs_3_
  172.3 9.3 collective-permute-done.14.refs_5_
  217.3 9.4 fusion
  290.4 6.3 collective-permute-done.30.refs_5_
  307.8 8.4 collective-permute-done.18
  331.3 51.1 %enc_mlp_forward.1 = (f32[1024,768]{1,0:T(8,128)}, f32[1024,768]{1,0:T(8,128)}, f32[8,768]{1,0:T(8,128)}) custom-call(f32[1024,768]{1,0:T(8,128)} %maximum_add_fusion.1.x_ref, f32[2,768]{1,0:T(2,128)} %squeeze.125.norm_ref, bf16[768,768]{1,0:T(8,128)(2,1)} %get-tuple-element.185.uh, bf16[768,768]{1,0:T(8,128)(2,1)} %get-tuple-element.184.ul, ...), custom_call_target="tpu_custom_call" | custom-call | flops 7247757312 | bytes 14190592 | tf_op jit(solution)/shard_map/enc_mlp_forward/pallas_call | solution.py:295
  407.6 10.7 %collective-permute-done.34 = f32[192,768]{1,0:T(8,128)S(1)} collective-permute-done((f32[192,768]{1,0:T(8,128)S(1)}, f32[192,768]{1,0:T(8,128)S(1)}, u32[]{:S(2)}, u32[]{:S(2)}) %collective-permute-start.34) | collective-permute-done | bytes 589856 | tf_op jit(solution)/shard_map/ppermute | solution.py:62
  423.5 28.1 %dec_mlp_forward.1 = (f32[384,768]{1,0:T(8,128)}, f32[384,768]{1,0:T(8,128)}, f32[8,768]{1,0:T(8,128)}) custom-call(f32[384,768]{1,0:T(8,128)} %maximum_add_fusion.3.x_ref, f32[2,768]{1,0:T(2,128)} %squeeze.129.norm_ref, bf16[768,768]{1,0:T(8,128)(2,1)} %get-tuple-element.181.uh, bf16[768,768]{1,0:T(8,128)(2,1)} %get-tuple-element.180.ul, ...), custom_call_target="tpu_custom_call" | custom-call | flops 2717908992 | bytes 8289792 | tf_op jit(solution)/shard_map/dec_mlp_forward/pallas_call | solution.py:295
  451.5 29.8 %dec_mlp_backward.1 = (f32[384,768]{1,0:T(8,128)}, f32[768,768]{1,0:T(8,128)}, f32[768,768]{1,0:T(8,128)}, f32[8,768]{1,0:T(8,128)}) custom-call(f32[384,768]{1,0:T(8,128)} %maximum_select_fusion.2.g_ref, f32[384,768]{1,0:T(8,128)} %maximum_add_fusion.3.x_ref, f32[2,768]{1,0:T(2,128)} %squeeze.129.norm_ref, f32[384,768]{1,0:T(8,128)} %get-tuple-element.39.pre_ref, ...), custom_call_target="tpu_custom_call" | custom-call | flops 5435817984 | bytes 14186496 | tf_op jit(solution)/shard_map/dec_mlp_backward/pallas_call | solution.py:295
  501.4 10.9 %collective-permute-done.46 = f32[192,768]{1,0:T(8,128)S(1)} collective-permute-done((f32[192,768]{1,0:T(8,128)S(1)}, f32[192,768]{1,0:T(8,128)S(1)}, u32[]{:S(2)}, u32[]{:S(2)}) %collective-permute-start.46) | collective-permute-done | bytes 589856 | tf_op jit(solution)/shard_map/ppermute | solution.py:62
  539.6 14.4 %collective-permute-done.49 = f32[192,768]{1,0:T(8,128)S(1)} collective-permute-done((f32[192,768]{1,0:T(8,128)S(1)}, f32[192,768]{1,0:T(8,128)S(1)}, u32[]{:S(2)}, u32[]{:S(2)}) %collective-permute-start.49) | collective-permute-done | bytes 589856 | tf_op jit(solution)/shard_map/ppermute | solution.py:62
  570.5 35.2 %collective-permute-done.37 = f32[512,768]{1,0:T(8,128)S(1)} collective-permute-done((f32[512,768]{1,0:T(8,128)S(1)}, f32[512,768]{1,0:T(8,128)S(1)}, u32[]{:S(2)}, u32[]{:S(2)}) %collective-permute-start.37) | collective-permute-done | bytes 1572896 | tf_op jit(solution)/shard_map/ppermute | solution.py:62
  626.4 52.7 %enc_mlp_backward.1 = (f32[1024,768]{1,0:T(8,128)}, f32[768,768]{1,0:T(8,128)}, f32[768,768]{1,0:T(8,128)}, f32[8,768]{1,0:T(8,128)}) custom-call(f32[1024,768]{1,0:T(8,128)} %subtract_multiply_fusion.g_ref, f32[1024,768]{1,0:T(8,128)} %maximum_add_fusion.1.x_ref, f32[2,768]{1,0:T(2,128)} %squeeze.125.norm_ref, f32[1024,768]{1,0:T(8,128)} %get-tuple-element.41.pre_ref, ...), custom_call_target="tpu_custom_call" | custom-call | flops 14495514624 | bytes 22050816 | tf_op jit(solution)/shard_map/enc_mlp_backward/pallas_call | solution.py:295
  684.4 11.1 %multiply_multiply_fusion = f32[3,1024,1024]{1,2,0:T(8,128)S(1)} fusion(f32[3,1024,1024]{1,2,0:T(8,128)} %copy-done, f32[3,1024]{1,0:T(4,128)S(1)} %bitcast.422, f32[3,1024]{1,0:T(4,128)S(1)} %log_add_fusion, pred[1024]{0:T(1024)(128)(4,1)S(1)} %copy-done.133, f32[1024,3,64]{0,2,1:T(8,128)S(1)} %bitcast.359, f32[1024,3,64]{0,2,1:T(8,128)S(1)} %bitcast.375), kind=kOutput, calls=%fused_computation.2 | convolution fusion | flops 1226833920 | bytes 26764288 | tf_op jit(solution)/shard_map/qhe,khe->hqk/dot_general | solution.py:452
  700.7 6.8 fusion.204
  707.5 7.4 fusion.3
  714.9 6.3 fusion.48
  760.1 15.4 %collective-permute-done.65 = f32[96,768]{1,0:T(8,128)S(1)} collective-permute-done((f32[96,768]{1,0:T(8,128)S(1)}, f32[96,768]{1,0:T(8,128)S(1)}, u32[]{:S(2)}, u32[]{:S(2)}) %collective-permute-start.65) | collective-permute-done | bytes 294944 | tf_op jit(solution)/shard_map/ppermute | solution.py:62
  775.6 11.1 %collective-permute-done.66 = f32[96,768]{1,0:T(8,128)S(1)} collective-permute-done((f32[96,768]{1,0:T(8,128)S(1)}, f32[96,768]{1,0:T(8,128)S(1)}, u32[]{:S(2)}, u32[]{:S(2)}) %collective-permute-start.66) | collective-permute-done | bytes 294944 | tf_op jit(solution)/shard_map/ppermute | solution.py:62
  811.7 16.1 %collective-permute-done.60 = f32[4,96,768]{2,1,0:T(8,128)} collective-permute-done((f32[4,96,768]{2,1,0:T(8,128)}, f32[4,96,768]{2,1,0:T(8,128)}, u32[]{:S(2)}, u32[]{:S(2)}) %collective-permute-start.60) | collective-permute-done | bytes 1179680 | tf_op jit(solution)/shard_map/ppermute | solution.py:62
  832.4 7.8 collective-permute-start.61
  882.6 13.3 %collective-permute-done.57 = f32[96,768]{1,0:T(8,128)S(1)} collective-permute-done((f32[96,768]{1,0:T(8,128)S(1)}, f32[96,768]{1,0:T(8,128)S(1)}, u32[]{:S(2)}, u32[]{:S(2)}) %collective-permute-start.57) | collective-permute-done | bytes 294944 | tf_op jit(solution)/shard_map/ppermute | solution.py:62
  896.0 12.2 %collective-permute-done.58 = f32[96,768]{1,0:T(8,128)S(1)} collective-permute-done((f32[96,768]{1,0:T(8,128)S(1)}, f32[96,768]{1,0:T(8,128)S(1)}, u32[]{:S(2)}, u32[]{:S(2)}) %collective-permute-start.58) | collective-permute-done | bytes 294944 | tf_op jit(solution)/shard_map/ppermute | solution.py:62
  909.4 6.3 collective-permute-start.53
  919.8 25.0 %scatter_custom_fusion = f32[6480,192]{1,0:T(8,128)} fusion(s32[3072]{0:T(1024)} %bitcast.437, f32[]{:T(128)} %constant.186.clone.1, f32[3072,192]{1,0:T(8,128)} %all-gather.8.cloned.1.call-done, pred[3072]{0:T(1024)(128)(4,1)S(1)} %copy-done.161), kind=kCustom, calls=%fused_computation.36 | custom fusion | flops 1179648 | bytes 8126464 | tf_op jit(solution)/shard_map/scatter-add | solution.py:715
  944.8 6.3 copy.184
  (849 shorter events, 455.3 us)
Async XLA Ops:
  7.2 91.8 %all-gather.10.cloned.1.call-start = ((), (), s32[]{:S(2)}) async-start(), calls=%async_computation.11 | async-start | bytes 2654208 | tf_op jit(solution)/shard_map/all_gather | solution.py:96
  10.7 40.9 %collective-permute-start.1 = (f32[88,768]{1,0:T(8,128)}, f32[88,768]{1,0:T(8,128)}, u32[]{:S(2)}, u32[]{:S(2)}) collective-permute-start(f32[88,768]{1,0:T(8,128)} %select_maximum_fusion.5.refs_0_), channel_id=1, source_target_pairs={{0,8},{4,12},{8,0},{12,4},{16,24},{20,28},{24,16},{28,20},{1,9},{5... | collective-permute-start | bytes 811016 | tf_op jit(solution)/shard_map/ppermute | solution.py:62
  13.7 38.2 %collective-permute-start.3 = (f32[88,768]{1,0:T(8,128)}, f32[88,768]{1,0:T(8,128)}, u32[]{:S(2)}, u32[]{:S(2)}) collective-permute-start(f32[88,768]{1,0:T(8,128)} %select_maximum_fusion.5.refs_0_), channel_id=1, source_target_pairs={{0,16},{4,20},{8,24},{12,28},{16,0},{20,4},{24,8},{28,12},{1,17},{... | collective-permute-start | bytes 811016 | tf_op jit(solution)/shard_map/ppermute | solution.py:62
  16.3 37.3 %collective-permute-start.5 = (f32[88,768]{1,0:T(8,128)}, f32[88,768]{1,0:T(8,128)}, u32[]{:S(2)}, u32[]{:S(2)}) collective-permute-start(f32[88,768]{1,0:T(8,128)} %select_maximum_fusion.5.refs_0_), channel_id=1, source_target_pairs={{0,24},{4,28},{8,16},{12,20},{16,8},{20,12},{24,0},{28,4},{1,25},{... | collective-permute-start | bytes 811016 | tf_op jit(solution)/shard_map/ppermute | solution.py:62
  16.3 37.9 %collective-permute-start = (f32[88,768]{1,0:T(8,128)}, f32[88,768]{1,0:T(8,128)}, u32[]{:S(2)}, u32[]{:S(2)}) collective-permute-start(f32[88,768]{1,0:T(8,128)} %select_maximum_fusion.5.refs_0_), channel_id=1, source_target_pairs={{0,4},{4,0},{8,12},{12,8},{16,20},{20,16},{24,28},{28,24},{1,5},{5... | collective-permute-start | bytes 811016 | tf_op jit(solution)/shard_map/ppermute | solution.py:62
  20.9 196.3 %reduce-scatter.6.cloned.1.call-start = ((), (), s32[]{:S(2)}) async-start(), calls=%async_computation.5 | async-start | bytes 3538944 | tf_op jit(solution)/shard_map/reduce_scatter | solution.py:613
  99.0 206.1 %all-gather.12.cloned.1.call-start = ((), (), s32[]{:S(2)}) async-start(), calls=%async_computation.12 | async-start | bytes 5308416 | tf_op jit(solution)/shard_map/all_gather | solution.py:96
  101.0 303.8 %all-gather.14.cloned.1.call-start = ((), (), s32[]{:S(2)}) async-start(), calls=%async_computation.13 | async-start | bytes 5308416 | tf_op jit(solution)/shard_map/all_gather | solution.py:96
  109.7 47.4 %collective-permute-start.11 = (f32[96,768]{1,0:T(8,128)}, f32[96,768]{1,0:T(8,128)}, u32[]{:S(2)}, u32[]{:S(2)}) collective-permute-start(f32[96,768]{1,0:T(8,128)} %pad_maximum_fusion.22.refs_0_), channel_id=1, source_target_pairs={{0,8},{4,12},{8,0},{12,4},{16,24},{20,28},{24,16},{28,20},{1,9},{5... | collective-permute-start | bytes 884744 | tf_op jit(solution)/shard_map/ppermute | solution.py:62
  110.4 47.3 %collective-permute-start.13 = (f32[96,768]{1,0:T(8,128)}, f32[96,768]{1,0:T(8,128)}, u32[]{:S(2)}, u32[]{:S(2)}) collective-permute-start(f32[96,768]{1,0:T(8,128)} %pad_maximum_fusion.22.refs_0_), channel_id=1, source_target_pairs={{0,16},{4,20},{8,24},{12,28},{16,0},{20,4},{24,8},{28,12},{1,17},{... | collective-permute-start | bytes 884744 | tf_op jit(solution)/shard_map/ppermute | solution.py:62
  113.8 45.3 %collective-permute-start.15 = (f32[96,768]{1,0:T(8,128)}, f32[96,768]{1,0:T(8,128)}, u32[]{:S(2)}, u32[]{:S(2)}) collective-permute-start(f32[96,768]{1,0:T(8,128)} %pad_maximum_fusion.22.refs_0_), channel_id=1, source_target_pairs={{0,24},{4,28},{8,16},{12,20},{16,8},{20,12},{24,0},{28,4},{1,25},{... | collective-permute-start | bytes 884744 | tf_op jit(solution)/shard_map/ppermute | solution.py:62
  114.1 46.7 %collective-permute-start.10 = (f32[96,768]{1,0:T(8,128)}, f32[96,768]{1,0:T(8,128)}, u32[]{:S(2)}, u32[]{:S(2)}) collective-permute-start(f32[96,768]{1,0:T(8,128)} %pad_maximum_fusion.22.refs_0_), channel_id=1, source_target_pairs={{0,4},{4,0},{8,12},{12,8},{16,20},{20,16},{24,28},{28,24},{1,5},{5... | collective-permute-start | bytes 884744 | tf_op jit(solution)/shard_map/ppermute | solution.py:62
  116.7 671.6 %reduce-scatter.10.cloned.1.call-start = ((), (), s32[]{:S(2)}) async-start(), calls=%async_computation.8 | async-start | bytes 2654208 | tf_op jit(solution)/shard_map/reduce_scatter | solution.py:109
  144.6 46.2 %collective-permute-start.22 = (f32[512,768]{1,0:T(8,128)S(1)}, f32[512,768]{1,0:T(8,128)S(1)}, u32[]{:S(2)}, u32[]{:S(2)}) collective-permute-start(f32[512,768]{1,0:T(8,128)S(1)} %add.455), channel_id=1, source_target_pairs={{0,1},{1,0},{2,3},{3,2},{4,5},{5,4},{6,7},{7,6},{8,9},{9,8},{10,11... | collective-permute-start | bytes 4718600 | tf_op jit(solution)/shard_map/ppermute | solution.py:62
  160.8 113.3 %collective-permute-start.27 = (f32[96,768]{1,0:T(8,128)}, f32[96,768]{1,0:T(8,128)}, u32[]{:S(2)}, u32[]{:S(2)}) collective-permute-start(f32[96,768]{1,0:T(8,128)} %pad_maximum_fusion.23.refs_0_), channel_id=1, source_target_pairs={{0,8},{4,12},{8,0},{12,4},{16,24},{20,28},{24,16},{28,20},{1,9},{5... | collective-permute-start | bytes 884744 | tf_op jit(solution)/shard_map/ppermute | solution.py:62
  171.3 103.5 %collective-permute-start.29 = (f32[96,768]{1,0:T(8,128)}, f32[96,768]{1,0:T(8,128)}, u32[]{:S(2)}, u32[]{:S(2)}) collective-permute-start(f32[96,768]{1,0:T(8,128)} %pad_maximum_fusion.23.refs_0_), channel_id=1, source_target_pairs={{0,16},{4,20},{8,24},{12,28},{16,0},{20,4},{24,8},{28,12},{1,17},{... | collective-permute-start | bytes 884744 | tf_op jit(solution)/shard_map/ppermute | solution.py:62
  181.6 94.5 %collective-permute-start.31 = (f32[96,768]{1,0:T(8,128)}, f32[96,768]{1,0:T(8,128)}, u32[]{:S(2)}, u32[]{:S(2)}) collective-permute-start(f32[96,768]{1,0:T(8,128)} %pad_maximum_fusion.23.refs_0_), channel_id=1, source_target_pairs={{0,24},{4,28},{8,16},{12,20},{16,8},{20,12},{24,0},{28,4},{1,25},{... | collective-permute-start | bytes 884744 | tf_op jit(solution)/shard_map/ppermute | solution.py:62
  266.9 50.8 %collective-permute-start.24 = (f32[512,768]{1,0:T(8,128)}, f32[512,768]{1,0:T(8,128)}, u32[]{:S(2)}, u32[]{:S(2)}) collective-permute-start(f32[512,768]{1,0:T(8,128)} %slice_add_fusion.2), channel_id=1, source_target_pairs={{0,2},{1,3},{2,0},{3,1},{4,6},{5,7},{6,4},{7,5},{8,10},{9,11},{10,... | collective-permute-start | bytes 4718600 | tf_op jit(solution)/shard_map/ppermute | solution.py:62
  521.5 398.3 %all-gather.8.cloned.1.call-start = ((), (), s32[]{:S(2)}) async-start(), calls=%async_computation.6 | async-start | bytes 3538944 | tf_op jit(solution)/shard_map/all_gather | solution.py:711
  558.8 397.3 %reduce-scatter.12.cloned.1.call-start = ((), (), s32[]{:S(2)}) async-start(), calls=%async_computation.9 | async-start | bytes 2654208 | tf_op jit(solution)/shard_map/reduce_scatter | solution.py:109
  559.6 396.6 %reduce-scatter.14.cloned.1.call-start = ((), (), s32[]{:S(2)}) async-start(), calls=%async_computation.10 | async-start | bytes 2654208 | tf_op jit(solution)/shard_map/reduce_scatter | solution.py:109
  607.8 348.4 %reduce-scatter.8.cloned.1.call-start = ((), (), s32[]{:S(2)}) async-start(), calls=%async_computation.7 | async-start | bytes 2654208 | tf_op jit(solution)/shard_map/reduce_scatter | solution.py:109
  618.6 130.7 %collective-permute-start.64 = (f32[4,96,768]{2,1,0:T(8,128)}, f32[4,96,768]{2,1,0:T(8,128)}, u32[]{:S(2)}, u32[]{:S(2)}) collective-permute-start(f32[4,96,768]{2,1,0:T(8,128)} %dynamic-slice_bitcast_fusion), channel_id=1, source_target_pairs={{0,4},{4,0},{8,12},{12,8},{16,20},{20,16},{24,28},{28,24},{1,5},{5... | collective-permute-start | bytes 3538952 | tf_op jit(solution)/shard_map/ppermute | solution.py:62
  759.4 43.1 %collective-permute-start.40 = (f32[512,768]{1,0:T(8,128)}, f32[512,768]{1,0:T(8,128)}, u32[]{:S(2)}, u32[]{:S(2)}) collective-permute-start(f32[512,768]{1,0:T(8,128)} %slice_add_fusion), channel_id=1, source_target_pairs={{0,2},{1,3},{2,0},{3,1},{4,6},{5,7},{6,4},{7,5},{8,10},{9,11},{10,... | collective-permute-start | bytes 4718600 | tf_op jit(solution)/shard_map/ppermute | solution.py:62
  810.8 62.0 %collective-permute-start.56 = (f32[4,96,768]{2,1,0:T(8,128)}, f32[4,96,768]{2,1,0:T(8,128)}, u32[]{:S(2)}, u32[]{:S(2)}) collective-permute-start(f32[4,96,768]{2,1,0:T(8,128)} %dynamic-slice_bitcast_fusion.2), channel_id=1, source_target_pairs={{0,4},{4,0},{8,12},{12,8},{16,20},{20,16},{24,28},{28,24},{1,5},{5... | collective-permute-start | bytes 3538952 | tf_op jit(solution)/shard_map/ppermute | solution.py:62
  832.4 42.1 %collective-permute-start.61 = (f32[96,768]{1,0:T(8,128)}, f32[96,768]{1,0:T(8,128)}, u32[]{:S(2)}, u32[]{:S(2)}) collective-permute-start(f32[96,768]{1,0:T(8,128)} %get-tuple-element.198), channel_id=1, source_target_pairs={{0,8},{4,12},{8,0},{12,4},{16,24},{20,28},{24,16},{28,20},{1,9},{5... | collective-permute-start | bytes 884744 | tf_op jit(solution)/shard_map/ppermute | solution.py:62
  840.2 38.8 %collective-permute-start.63 = (f32[96,768]{1,0:T(8,128)}, f32[96,768]{1,0:T(8,128)}, u32[]{:S(2)}, u32[]{:S(2)}) collective-permute-start(f32[96,768]{1,0:T(8,128)} %get-tuple-element.199), channel_id=1, source_target_pairs={{0,24},{4,28},{8,16},{12,20},{16,8},{20,12},{24,0},{28,4},{1,25},{... | collective-permute-start | bytes 884744 | tf_op jit(solution)/shard_map/ppermute | solution.py:62
  871.3 37.1 %collective-permute-start.52 = (f32[4,88,768]{2,1,0:T(8,128)S(1)}, f32[4,88,768]{2,1,0:T(8,128)S(1)}, u32[]{:S(2)}, u32[]{:S(2)}) collective-permute-start(f32[4,88,768]{2,1,0:T(8,128)S(1)} %dynamic-slice_bitcast_fusion.3), channel_id=1, source_target_pairs={{0,4},{4,0},{8,12},{12,8},{16,20},{20,16},{24,28},{28,24},{1,5},{5... | collective-permute-start | bytes 3244040 | tf_op jit(solution)/shard_map/ppermute | solution.py:62
  908.2 42.9 %collective-permute-start.44 = (f32[512,160]{0,1:T(8,128)S(1)}, f32[512,160]{0,1:T(8,128)S(1)}, u32[]{:S(2)}, u32[]{:S(2)}) collective-permute-start(f32[512,160]{0,1:T(8,128)S(1)} %add.488), channel_id=1, source_target_pairs={{0,1},{1,0},{2,3},{3,2},{4,5},{5,4},{6,7},{7,6},{8,9},{9,8},{10,11... | collective-permute-start | bytes 983048 | tf_op jit(solution)/shard_map/ppermute | solution.py:62
  909.4 43.5 %collective-permute-start.53 = (f32[88,768]{1,0:T(8,128)}, f32[88,768]{1,0:T(8,128)S(1)}, u32[]{:S(2)}, u32[]{:S(2)}) collective-permute-start(f32[88,768]{1,0:T(8,128)} %get-tuple-element.212), channel_id=1, source_target_pairs={{0,8},{4,12},{8,0},{12,4},{16,24},{20,28},{24,16},{28,20},{1,9},{5... | collective-permute-start | bytes 811016 | tf_op jit(solution)/shard_map/ppermute | solution.py:62
  915.8 37.2 %collective-permute-start.54 = (f32[88,768]{1,0:T(8,128)}, f32[88,768]{1,0:T(8,128)}, u32[]{:S(2)}, u32[]{:S(2)}) collective-permute-start(f32[88,768]{1,0:T(8,128)} %get-tuple-element.214), channel_id=1, source_target_pairs={{0,16},{4,20},{8,24},{12,28},{16,0},{20,4},{24,8},{28,12},{1,17},{... | collective-permute-start | bytes 811016 | tf_op jit(solution)/shard_map/ppermute | solution.py:62
  915.9 37.1 %collective-permute-start.55 = (f32[88,768]{1,0:T(8,128)}, f32[88,768]{1,0:T(8,128)}, u32[]{:S(2)}, u32[]{:S(2)}) collective-permute-start(f32[88,768]{1,0:T(8,128)} %get-tuple-element.213), channel_id=1, source_target_pairs={{0,24},{4,28},{8,16},{12,20},{16,8},{20,12},{24,0},{28,4},{1,25},{... | collective-permute-start | bytes 811016 | tf_op jit(solution)/shard_map/ppermute | solution.py:62
  (240 other events, 3652.9 us)
Sparse Core Ops, SparseCore 0:
  21.0 69.0 all-gather.9
  99.2 114.0 reduce-scatter.5
  215.4 77.9 all-gather.11
  295.5 79.9 all-gather.13
  521.6 67.1 reduce-scatter.9
  590.8 76.3 all-gather.7
  671.3 68.2 reduce-scatter.11
  743.7 93.9 reduce-scatter.13
  841.7 106.5 reduce-scatter.7
